TPU v7x, 512 devices: a whole 4x8x8 slice. The times are simulated.
512 devices in a mesh: rows: 64 (over x, z_lo, y), feat: 8 (over z_hi, core).
Axes of the slice: x: 4, y: 8, z: 8 (z_hi: 4, z_lo: 2; z = z_hi * 2 + z_lo), core: 2. Of those that a mesh axis runs over, the one named last changes fastest.
Arguments:
- descriptors: bfloat16 [16384, 128], P('rows'), may hold values from -6 to 6
- freqs: bfloat16 [128, 32768], P(None, 'feat'), may hold values from -0.5 to 0.5
- phases: float32 [32768], P('feat'), may hold values from -3.140625 to 3.140625
- row_weight: float32 [16384], P('rows'), may hold values from 0.3 to 15, as said below
- resid: float32 [16384, 128], P('rows'), may hold values from -6 to 6
- coef: float32 [32768, 128], P(('feat', 'rows')), may hold values from -4 to 4
- direction: float32 [32768, 128], P(('feat', 'rows')), may hold values from -6 to 6
- ridge: float32 [128], replicated, may hold values from 1 to 10
- gamma: float32 [128], replicated, may hold values from 300000 to 3000000
Outputs:
- coef_new: float32 [32768, 128], P(('feat', 'rows'))
- resid_new: float32 [16384, 128], P('rows')
- direction_new: float32 [32768, 128], P(('feat', 'rows'))
- gamma_new: float32 [128], replicated
Inputs may be any that keep to these rules, and one draw needn't show every extreme that they name: `row_weight`: positive weights of the profile rows.
All inputs are finite; a program needn't handle non-finite values.
Results may differ from a plain program's by a relative error of at most 0.0006.
The roundings to bfloat16 on the way count: a program that leaves them out, or rounds other values in their place, can miss the bound.
Values may be sent and summed in bfloat16 or wider, within the bound.
No kernel may reach another device: no remote copies, remote signals or barrier semaphores. Data moves between devices by JAX's collectives and lax.ppermute only.
A program may use at most 64 MiB of HBM per device.

v0:
```python
import math

import jax
import jax.numpy as jnp
from jax import lax
from jax.sharding import PartitionSpec as P

FEAT = 32768


def make_features(block_x, freq_cols, phase_cols):
    scale = math.sqrt(2.0 / FEAT)
    angle = jnp.dot(block_x, freq_cols, preferred_element_type=jnp.float32) + phase_cols[None, :]
    return (scale * jnp.cos(angle)).astype(jnp.bfloat16)


def body(descriptors, freqs, phases, row_weight, resid, coef, direction, ridge, gamma):
    rows_dev = descriptors.shape[0]
    targets = resid.shape[1]
    block = min(256, rows_dev)
    empty = jnp.zeros((rows_dev, targets), jnp.float32)
    total = empty
    freq_cols = freqs
    phase_cols = phases
    feats = make_features(descriptors, freq_cols, phase_cols)
    update = jnp.dot(
        feats,
        lax.all_gather(direction.astype(jnp.bfloat16), "rows", axis=0, tiled=True),
        preferred_element_type=jnp.float32,
    )
    total = total.at[0:block].add(update)
    partial_image = total
    image = row_weight[:, None] * lax.psum(partial_image, "feat")
    step_local = jnp.sum(direction * direction, axis=0)
    image_sq = lax.psum(jnp.sum(image * image, axis=0), "rows")
    step_sq = lax.psum(step_local, ("rows", "feat"))
    curvature = image_sq + ridge * step_sq
    alpha = gamma / curvature
    coef_new = coef + alpha[None, :] * direction
    resid_new = resid - alpha[None, :] * image
    weighted_b = (row_weight[:, None] * resid_new).astype(jnp.bfloat16)
    own_count = coef.shape[0]
    freq_cols = freqs
    phase_cols = phases
    feats = make_features(descriptors, freq_cols, phase_cols)
    total = lax.dot_general(
        feats, weighted_b, (((0,), (0,)), ((), ())), preferred_element_type=jnp.float32
    )
    summed = lax.psum(total, "rows")
    mine = lax.dynamic_slice_in_dim(summed, lax.axis_index("rows") * own_count, own_count, 0)
    gradient = mine - ridge[None, :] * coef_new
    gamma_new = lax.psum(jnp.sum(gradient * gradient, axis=0), ("rows", "feat"))
    direction_new = gradient + (gamma_new / gamma)[None, :] * direction
    return (coef_new, resid_new, direction_new, gamma_new)


def solution(mesh):
    return jax.shard_map(
        body,
        mesh=mesh,
        in_specs=(
            P("rows", None),
            P(None, "feat"),
            P("feat"),
            P("rows"),
            P("rows", None),
            P(("feat", "rows"), None),
            P(("feat", "rows"), None),
            P(),
            P(),
        ),
        out_specs=(P(("feat", "rows"), None), P("rows", None), P(("feat", "rows"), None), P()),
        check_vma=False,
    )
```

profile of v0, /device:TPU:1, one launch (start us, length us, event | category | flops | bytes accessed | tf_op | source)
XLA Modules:
  0.0 1283.5 jit_solution(3385097664590164081)
XLA Ops:
  7.2 0.0 copy-start
  7.2 0.0 all-gather.2.cloned.1.call-start
  7.2 1.5 multiply_reduce_fusion.2
  8.7 0.0 all-gather.2.cloned.1.call-update
  8.7 0.0 all-reduce.3.cloned.1.call-start
  8.8 0.0 copy-done
  8.8 15.6 %fusion.2 = bf16[256,4096]{1,0:T(8,128)(2,1)S(1)} fusion(bf16[256,128]{1,0:T(8,128)(2,1)} %param.13, bf16[128,4096]{1,0:T(8,128)(2,1)S(1)} %copy-done, f32[4096]{0:T(1024)} %param.15), kind=kOutput, calls=%fused_computation.3 | convolution fusion | flops 271581184 | bytes 3227648 | tf_op jit(solution)/shard_map/dot_general | solution.py:13
  24.4 0.0 copy-start.6
  24.4 0.0 copy-start.7
  24.5 0.0 copy-start.8
  24.5 0.0 copy-start.3
  24.5 246.5 %all-gather.2.cloned.1.call-done = bf16[4096,128]{1,0:T(8,128)(2,1)} async-done(((bf16[64,128]{1,0:T(8,128)(2,1)}), bf16[4096,128]{1,0:T(8,128)(2,1)}) %all-gather.2.cloned.1.call-update) | async-done | bytes 1048592 | tf_op jit(solution)/shard_map/all_gather | solution.py:28
  271.0 2.6 fusion.5
  273.6 0.0 all-reduce.3.cloned.1.call-update
  273.6 0.0 all-reduce.5.cloned.1.call-start
  273.7 141.7 %psum.37 = f32[128]{0:T(128)S(1)} all-reduce(f32[128]{0:T(128)S(1)} %get-tuple-element.26), channel_id=1, replica_groups=mesh['rows'=64,'feat'=8] {'rows','feat'}, use_global_device_ids=true, to_apply=%region_4.0 | all-reduce | flops 128 | bytes 1024 | tf_op jit(solution)/shard_map/psum | solution.py:36
  415.3 0.0 all-reduce.3.cloned.1.call-done
  415.3 0.0 copy-done.6
  415.3 1.0 multiply_reduce_fusion
  416.4 125.4 %psum.36 = f32[128]{0:T(128)S(1)} all-reduce(f32[128]{0:T(128)S(1)} %multiply_reduce_fusion), channel_id=1, replica_groups=mesh['rows'=64,'feat'=8] {'rows'}, use_global_device_ids=true, to_apply=%region_2.0 | all-reduce | flops 128 | bytes 1024 | tf_op jit(solution)/shard_map/psum | solution.py:35
  541.7 0.0 copy-done.7
  541.7 0.0 copy-done.8
  541.7 0.0 copy-done.3
  541.8 1.0 multiply_subtract_fusion
  542.8 0.0 copy-start.1
  542.8 2.1 fusion.3
  544.9 0.0 copy-done.1
  544.9 0.0 copy-start.2
  544.9 0.0 copy-start.5
  544.9 0.0 all-reduce.5.cloned.1.call-update
  544.9 587.5 %all-reduce.5.cloned.1.call-done = f32[4096,128]{1,0:T(8,128)} async-done(((f32[4096,128]{1,0:T(8,128)}), f32[4096,128]{1,0:T(8,128)}) %all-reduce.5.cloned.1.call-update) | async-done | bytes 2097168 | tf_op jit(solution)/shard_map/psum | solution.py:49
  1132.4 0.0 copy-done.2
  1132.4 0.0 copy-done.5
  1132.4 0.8 multiply_reduce_fusion.1
  1133.2 0.0 copy-start.4
  1133.2 142.4 %psum.39 = f32[128]{0:T(128)S(1)} all-reduce(f32[128]{0:T(128)S(1)} %get-tuple-element.24), channel_id=1, replica_groups=mesh['rows'=64,'feat'=8] {'rows','feat'}, use_global_device_ids=true, to_apply=%region_7.0 | all-reduce | flops 128 | bytes 1024 | tf_op jit(solution)/shard_map/psum | solution.py:52
  1275.6 0.0 copy-start.9
  1275.6 1.4 multiply_add_fusion
  1277.0 0.0 copy-done.4
  1277.0 0.0 copy-done.9
  (2 shorter events, 0.0 us)
Async XLA Ops:
  7.2 1.6 copy-start
  7.2 263.8 %all-gather.2.cloned.1.call-start = ((), (), s32[]{:S(2)}) async-start(), calls=%async_computation | async-start | bytes 1064960 | tf_op jit(solution)/shard_map/all_gather | solution.py:28
  8.7 406.6 %all-reduce.3.cloned.1.call-start = ((), (), s32[]{:S(2)}) async-start(), calls=%async_computation.1 | async-start | bytes 262144 | tf_op jit(solution)/shard_map/psum | solution.py:33
  24.4 390.9 %copy-start.6 = (f32[256]{0:T(256)S(1)}, f32[256]{0:T(256)}, u32[]{:S(2)}) copy-start(f32[256]{0:T(256)} %param.16) | copy-start | bytes 3076
  24.4 517.3 %copy-start.7 = (f32[128]{0:T(128)S(1)}, f32[128]{0:T(128)}, u32[]{:S(2)}) copy-start(f32[128]{0:T(128)} %param.20) | copy-start | bytes 1540
  24.5 517.3 %copy-start.8 = (f32[128]{0:T(128)S(1)}, f32[128]{0:T(128)}, u32[]{:S(2)}) copy-start(f32[128]{0:T(128)} %param.21) | copy-start | bytes 1540
  24.5 517.3 %copy-start.3 = (f32[256,128]{1,0:T(8,128)S(1)}, f32[256,128]{1,0:T(8,128)}, u32[]{:S(2)}) copy-start(f32[256,128]{1,0:T(8,128)} %param.17) | copy-start | bytes 393220
  273.6 858.8 %all-reduce.5.cloned.1.call-start = ((), (), s32[]{:S(2)}) async-start(), calls=%async_computation.2 | async-start | bytes 4194304 | tf_op jit(solution)/shard_map/psum | solution.py:49
  542.8 2.1 copy-start.1
  544.9 587.5 %copy-start.2 = (f32[64,128]{1,0:T(8,128)S(1)}, f32[64,128]{1,0:T(8,128)}, u32[]{:S(2)}) copy-start(f32[64,128]{1,0:T(8,128)} %param.19) | copy-start | bytes 98308
  544.9 587.5 %copy-start.5 = (f32[64,128]{1,0:T(8,128)S(1)}, f32[64,128]{1,0:T(8,128)}, u32[]{:S(2)}) copy-start(f32[64,128]{1,0:T(8,128)} %param.18) | copy-start | bytes 98308
  1133.2 143.8 %copy-start.4 = (f32[64,128]{1,0:T(8,128)}, f32[64,128]{1,0:T(8,128)S(1)}, u32[]{:S(2)}) copy-start(f32[64,128]{1,0:T(8,128)S(1)} %get-tuple-element.25) | copy-start | bytes 98308
  1275.6 1.4 copy-start.9
Sparse Core Ops, SparseCore 0:
  10.7 260.2 all-gather.1
  274.4 118.6 all-reduce.2
  545.0 587.3 all-reduce.4
where the time goes:
time: 1280 us
  waiting for transfers between devices  834 us (65%)
  blocking collectives  409 us (32%)
  matrix products  20.4 us (2%)
  between operations  13.8 us (1%)
    psum x1, waiting for transfers between devices, body(): summed = lax.psum(total, 'rows')  587 us
    all_gather x1, waiting for transfers between devices, body(): lax.all_gather(direction.astype(jnp.bfloat16), 'rows', axis=0, tiled=True)  246 us
    psum x1, blocking collectives, body(): gamma_new = lax.psum(jnp.sum(gradient * gradient, axis=0), ('rows', 'feat'))  142 us
    psum x1, blocking collectives, body(): step_sq = lax.psum(step_local, ('rows', 'feat'))  142 us
    psum x1, blocking collectives, body(): image_sq = lax.psum(jnp.sum(image * image, axis=0), 'rows')  125 us
  transfers between devices with their start and end apart: 3, of which 2 were waited for; matrix products, arithmetic and copies ran while one was open for 1% of the time, Pallas kernels for 0%

commit v1 on v0

v1 whole, which is shorter than its diff:
```python
import jax
import jax.numpy as jnp
import numpy as np
from jax import lax
from jax.sharding import Mesh, PartitionSpec as P

AXES = ("x", "zl", "y", "zh", "core")
SIZES = (4, 2, 8, 4, 2)
ROWS = ("x", "zl", "y")
FEAT = ("zh", "core")
PLANE = ("x", "y")
COLUMN = ("zl", "zh", "core")

SCALE = 2.0**-7
TURN = 1.0 / (2.0 * np.pi)
TURN_HI = 6.28125
TURN_LO = 2.0 * np.pi - 6.28125
COS = (
    1.0,
    -0.49999988079071045,
    0.041666485369205475,
    -0.0013887786772102118,
    2.476951885910239e-05,
    -2.707541852942086e-07,
    1.7231808202566867e-09,
)


def scaled_cos(angle):
    turns = jnp.round(angle * jnp.float32(TURN))
    rest = (angle - turns * jnp.float32(TURN_HI)) - turns * jnp.float32(TURN_LO)
    square = rest * rest
    value = jnp.float32(COS[-1] * SCALE)
    for c in COS[-2::-1]:
        value = value * square + jnp.float32(c * SCALE)
    return value


def spread(value, axes):
    n = lax.axis_size(axes)
    copies = jnp.broadcast_to(value[None], (n,) + value.shape)
    return lax.all_to_all(copies, axes, 0, 0, tiled=True)


def total_of(row, axes):
    return jnp.sum(spread(row, axes), axis=0)


def body(descriptors, freqs, phases, row_weight, resid, coef, direction, ridge, gamma):
    rows_dev, desc = descriptors.shape
    targets = resid.shape[1]
    own = direction.shape[0]
    zl = lax.axis_index("zl")
    swap = [(0, 1), (1, 0)]
    n_plane, n_column = lax.axis_size(PLANE), lax.axis_size(COLUMN)

    def both(mine, peer):
        return jnp.where(zl == 0, jnp.concatenate([mine, peer]), jnp.concatenate([peer, mine]))

    rows_x = both(descriptors, lax.ppermute(descriptors, "zl", swap))
    packed = jnp.concatenate([resid, row_weight.reshape(-1, targets)])
    peer = lax.ppermute(packed, "zl", swap)
    rows_resid = both(resid, peer[:rows_dev])
    rows_weight = both(row_weight, peer[rows_dev:].reshape(-1))

    n_x = lax.axis_size("x")
    freq_cols = freqs.reshape(desc, n_x, 2, -1)
    freq_cols = lax.dynamic_index_in_dim(freq_cols, zl, 2, keepdims=False).reshape(desc, -1)
    phase_cols = lax.dynamic_index_in_dim(phases.reshape(n_x, 2, -1), zl, 1, keepdims=False).reshape(-1)

    gathered = spread(direction.astype(jnp.bfloat16), PLANE).reshape(-1, targets)
    angle = jnp.dot(rows_x, freq_cols, preferred_element_type=jnp.float32) + phase_cols[None, :]
    feats = scaled_cos(angle).astype(jnp.bfloat16)
    partial = jnp.dot(feats, gathered, preferred_element_type=jnp.float32)

    penalty = ridge * jnp.sum(direction * direction, axis=0)
    extra = jnp.broadcast_to(penalty[None, None], (n_column, 8, targets))
    sent = jnp.concatenate([partial.reshape(n_column, -1, targets), extra], axis=1)
    came = jnp.sum(lax.all_to_all(sent, COLUMN, 0, 0, tiled=True), axis=0)
    share = came.shape[0] - 8
    image = rows_weight[:, None] * spread(came[:share], COLUMN).reshape(-1, targets)
    curvature = total_of(jnp.sum(image * image, axis=0)[None] + came[share : share + 1], PLANE)
    alpha = gamma / curvature[0]
    coef_new = coef + alpha[None, :] * direction
    rows_new = rows_resid - alpha[None, :] * image
    weighted_b = (rows_weight[:, None] * rows_new).astype(jnp.bfloat16)
    resid_new = lax.dynamic_slice_in_dim(rows_new, zl * rows_dev, rows_dev, 0)

    terms = lax.dot_general(
        feats, weighted_b, (((0,), (0,)), ((), ())), preferred_element_type=jnp.float32
    )
    terms = lax.all_to_all(terms.reshape(n_plane, own, targets), PLANE, 0, 0, tiled=True)
    gradient = jnp.sum(terms, axis=0) - ridge[None, :] * coef_new
    gamma_new = total_of(total_of(jnp.sum(gradient * gradient, axis=0)[None], COLUMN), PLANE)[0]
    direction_new = gradient + (gamma_new / gamma)[None, :] * direction
    return (coef_new, resid_new, direction_new, gamma_new)


def solution(mesh):
    cut = Mesh(mesh.devices.reshape(SIZES), AXES)
    split = P(FEAT + ROWS, None)
    return jax.shard_map(
        body,
        mesh=cut,
        in_specs=(P(ROWS, None), P(None, FEAT), P(FEAT), P(ROWS), P(ROWS, None), split, split, P(), P()),
        out_specs=(split, P(ROWS, None), split, P()),
        check_vma=False,
    )
```

time: 1280 us -> 152 us (0.12)
  waiting for transfers between devices: 834 us -> 58 us
  blocking collectives: 409 us -> 26.5 us
  starting transfers between devices: 0.12 us -> 44.2 us
  matrix products: 20.4 us -> 6.81 us
  between operations: 13.8 us -> 0.95 us
    psum x2 -> x0, waiting for transfers between devices: 587 us -> none  [the longest x1 587 us: body(): summed = lax.psum(total, 'rows')]
    psum x3 -> x0, blocking collectives: 409 us -> none  [the longest x1 142 us: body(): gamma_new = lax.psum(jnp.sum(gradient * gradient, axis=0), ('rows', 'feat'))]
    all_gather x1 -> x0, waiting for transfers between devices: 246 us -> none  [body(): lax.all_gather(direction.astype(jnp.bfloat16), 'rows', axis=0, tiled=True)]
    all_to_all x0 -> x6, waiting for transfers between devices: none -> 53.3 us  [the longest x5 28.5 us: spread(): return lax.all_to_all(copies, axes, 0, 0, tiled=True)]
    all_to_all x0 -> x6, starting transfers between devices: none -> 36.5 us  [the longest x5 32.6 us: spread(): return lax.all_to_all(copies, axes, 0, 0, tiled=True)]
    all_to_all x0 -> x1, blocking collectives: none -> 26.5 us  [body(): came = jnp.sum(lax.all_to_all(sent, COLUMN, 0, 0, tiled=True), axis=0)]
    dot_general x2, matrix products: 18.3 us -> 5.12 us  [the longest x1 4.41 us: body(): jnp.dot(rows_x, freq_cols, preferred_element_type=jnp.float32)]
  transfers between devices with their start and end apart: 3 -> 8, of which waited for: 2 -> 7; matrix products, arithmetic and copies ran while one was open for 1% -> 10% of each run, Pallas kernels for 0% -> 0%
where the time goes in v1:
time: 152 us; the launch traced here: 151 us
  waiting for transfers between devices  58 us (38%)
  starting transfers between devices  44.2 us (29%)
  blocking collectives  26.5 us (17%)
  local copies, waits for them, and re-layouts  9.03 us (6%)
  matrix products  6.81 us (4%)
  other arithmetic  5.65 us (4%)
    all_to_all x5, starting transfers between devices, spread(): return lax.all_to_all(copies, axes, 0, 0, tiled=True)  32.6 us
    all_to_all x5, waiting for transfers between devices, spread(): return lax.all_to_all(copies, axes, 0, 0, tiled=True)  28.5 us
    all_to_all x1, blocking collectives, body(): came = jnp.sum(lax.all_to_all(sent, COLUMN, 0, 0, tiled=True), axis=0)  26.5 us
    all_to_all x1, waiting for transfers between devices, body(): lax.all_to_all(terms.reshape(n_plane, own, targets), PLANE, 0, 0, tiled=T...  24.8 us
    ppermute x1, starting transfers between devices, body(): rows_x = both(descriptors, lax.ppermute(descriptors, 'zl', swap))  4.96 us
    ppermute x1, waiting for transfers between devices, body(): peer = lax.ppermute(packed, 'zl', swap)  4.63 us
    dot_general x1, matrix products, body(): jnp.dot(rows_x, freq_cols, preferred_element_type=jnp.float32)  4.41 us
    all_to_all x1, starting transfers between devices, body(): lax.all_to_all(terms.reshape(n_plane, own, targets), PLANE, 0, 0, tiled=T...  3.93 us
  transfers between devices with their start and end apart: 8, of which 7 were waited for; matrix products, arithmetic and copies ran while one was open for 10% of the time, Pallas kernels for 0%

profile of v1, /device:TPU:1, one launch (start us, length us, event | category | flops | bytes accessed | tf_op | source)
XLA Modules:
  0.0 151.2 jit_solution(18302255961939896833)
XLA Ops:
  0.6 0.0 copy-start.7
  0.6 0.0 copy-start.5
  0.7 5.0 %collective-permute-start.1 = (bf16[256,128]{1,0:T(8,128)(2,1)}, bf16[256,128]{1,0:T(8,128)(2,1)S(1)}, u32[]{:S(2)}, u32[]{:S(2)}) collective-permute-start(bf16[256,128]{1,0:T(8,128)(2,1)} %param.9), channel_id=1, source_target_pairs={{0,64},{64,0},{1,65},{65,1},{2,66},{66,2},{3,67},{67,3},{4,68},{68... | collective-permute-start | bytes 196616 | tf_op jit(solution)/shard_map/ppermute | solution.py:60
  5.6 0.9 fusion.14
  6.5 0.9 broadcast_in_dim.16
  7.4 9.7 %all-to-all-start = ((bf16[32,64,128]{2,1,0:T(8,128)(2,1)}), bf16[32,64,128]{2,1,0:T(8,128)(2,1)S(1)}, u32[]{:S(2)}, u32[]{:S(2)}) async-start(bf16[32,64,128]{2,1,0:T(8,128)(2,1)} %broadcast_in_dim.16), calls=%async_computation | async-start | bytes 1048576 | tf_op jit(solution)/shard_map/all_to_all | solution.py:42
  17.1 0.7 reshape.117
  17.8 1.6 %copy.19 = bf16[128,4096]{0,1:T(8,128)(2,1)S(1)} copy(bf16[128,4096]{1,0:T(8,128)(2,1)} %param.10) | data formatting | bytes 2097152 | tf_op args[1]
  19.5 0.0 copy-done.5
  19.5 0.0 collective-permute-done.1
  19.5 0.0 copy-done.7
  19.5 4.4 %add_convert_fusion = (bf16[2048,512]{0,1:T(8,128)(2,1)}, f32[512,2048]{1,0:T(8,128)S(1)}) fusion(f32[2048]{0:T(1024)S(1)} %bitcast.53, bf16[128,2048]{0,1:T(8,128)(2,1)S(1)} %bitcast.50, bf16[256,128]{1,0:T(8,128)(2,1)S(1)} %collective-permute-done.1, bf16[256,128]{1,0:T(8,128)(2,1)S(1)} %copy-done.7, pred[]{:T(512)S(6)} %eq.2), kind=kOutput, calls=%fused_computation.5 | convolution fusion | flops 291045376 | bytes 6955009 | tf_op jit(solution)/shard_map/dot_general | solution.py:72
  24.0 2.8 %add_convert_fusion.1 = bf16[512,2048]{1,0:T(8,128)(2,1)S(1)} fusion(f32[512,2048]{1,0:T(8,128)S(1)} %get-tuple-element.11, f32[2048]{0:T(1024)S(1)} %bitcast.54), kind=kLoop, calls=%fused_computation.6 | loop fusion | flops 22020096 | bytes 6299648 | tf_op jit(solution)/shard_map/convert_element_type | solution.py:73
  26.8 0.0 copy-start
  26.8 0.0 copy-start.4
  26.8 4.4 %all-to-all-done = bf16[32,64,128]{2,1,0:T(8,128)(2,1)S(1)} async-done(((bf16[32,64,128]{2,1,0:T(8,128)(2,1)}), bf16[32,64,128]{2,1,0:T(8,128)(2,1)S(1)}, u32[]{:S(2)}, u32[]{:S(2)}) %all-to-all-start) | async-done | bytes 524320 | tf_op jit(solution)/shard_map/all_to_all | solution.py:42
  31.2 0.7 fusion.15
  31.9 0.0 copy-start.8
  31.9 26.5 %all_to_all.35 = f32[16,40,128]{2,1,0:T(8,128)S(1)} all-to-all(f32[16,40,128]{2,1,0:T(8,128)S(1)} %pad_maximum_fusion), channel_id=1, replica_groups=mesh['x'=4,'zl'=2,'y'=8,'zh'=4,'core'=2] {'zl','zh','core'}, dimensions={0} | all-to-all | bytes 655360 | tf_op jit(solution)/shard_map/all_to_all | solution.py:79
  58.5 0.8 broadcast_in_dim.18
  59.3 3.4 %all-to-all-start.2 = ((f32[16,32,128]{2,1,0:T(8,128)}), f32[16,32,128]{2,1,0:T(8,128)S(1)}, u32[]{:S(2)}, u32[]{:S(2)}) async-start(f32[16,32,128]{2,1,0:T(8,128)} %broadcast_in_dim.18), calls=%async_computation.2 | async-start | bytes 524288 | tf_op jit(solution)/shard_map/all_to_all | solution.py:42
  62.7 0.0 copy-done
  62.7 0.0 copy-done.4
  62.8 2.7 %collective-permute-start = (f32[258,128]{1,0:T(8,128)S(1)}, f32[258,128]{1,0:T(8,128)S(1)}, u32[]{:S(2)}, u32[]{:S(2)}) collective-permute-start(f32[258,128]{1,0:T(8,128)S(1)} %pad_maximum_fusion.1), channel_id=1, source_target_pairs={{0,64},{64,0},{1,65},{65,1},{2,66},{66,2},{3,67},{67,3},{4,68},{68... | collective-permute-start | bytes 396296 | tf_op jit(solution)/shard_map/ppermute | solution.py:62
  65.5 2.9 %copy.21 = bf16[2048,512]{1,0:T(8,128)(2,1)S(1)} copy(bf16[2048,512]{0,1:T(8,128)(2,1)} %get-tuple-element.10) | data formatting | bytes 4194304 | tf_op jit(solution)/shard_map/convert_element_type | solution.py:73
  68.4 0.0 copy-start.1
  68.4 0.0 copy-start.3
  68.4 4.6 %collective-permute-done = f32[258,128]{1,0:T(8,128)S(1)} collective-permute-done((f32[258,128]{1,0:T(8,128)S(1)}, f32[258,128]{1,0:T(8,128)S(1)}, u32[]{:S(2)}, u32[]{:S(2)}) %collective-permute-start) | collective-permute-done | bytes 132128 | tf_op jit(solution)/shard_map/ppermute | solution.py:62
  73.1 0.1 select_n.49
  73.2 1.0 all-to-all-done.2
  74.2 0.1 multiply_reduce_fusion
  74.3 0.6 broadcast_in_dim.21
  75.0 5.0 %all-to-all-start.3 = ((f32[32,1,128]{2,1,0:T(1,128)}), f32[32,1,128]{2,1,0:T(1,128)S(1)}, u32[]{:S(2)}, u32[]{:S(2)}) async-start(f32[32,1,128]{2,1,0:T(1,128)} %broadcast_in_dim.21), calls=%async_computation.3 | async-start | bytes 32768 | tf_op jit(solution)/shard_map/all_to_all | solution.py:42
  80.0 8.5 %all-to-all-done.3 = f32[32,1,128]{2,1,0:T(1,128)S(1)} async-done(((f32[32,1,128]{2,1,0:T(1,128)}), f32[32,1,128]{2,1,0:T(1,128)S(1)}, u32[]{:S(2)}, u32[]{:S(2)}) %all-to-all-start.3) | async-done | bytes 16416 | tf_op jit(solution)/shard_map/all_to_all | solution.py:42
  88.5 0.0 copy-done.8
  88.5 0.1 multiply_convert_fusion
  88.7 1.7 %fusion.16 = f32[32,64,128]{2,1,0:T(8,128)} fusion(bf16[32,64,512]{2,1,0:T(8,128)(2,1)S(1)} %bitcast.43, bf16[512,128,1]{1,0,2:T(8,128)(2,1)S(1)} %bitcast.49), kind=kOutput, calls=%fused_computation.39 | convolution fusion | flops 268435456 | bytes 3276800 | tf_op jit(solution)/shard_map/dot_general | solution.py:89
  90.4 3.9 %all-to-all-start.4 = ((f32[32,64,128]{2,1,0:T(8,128)}), f32[32,64,128]{2,1,0:T(8,128)S(1)}, u32[]{:S(2)}, u32[]{:S(2)}) async-start(f32[32,64,128]{2,1,0:T(8,128)} %fusion.16), calls=%async_computation.4 | async-start | bytes 2097152 | tf_op jit(solution)/shard_map/all_to_all | solution.py:92
  94.3 24.8 %all-to-all-done.4 = f32[32,64,128]{2,1,0:T(8,128)S(1)} async-done(((f32[32,64,128]{2,1,0:T(8,128)}), f32[32,64,128]{2,1,0:T(8,128)S(1)}, u32[]{:S(2)}, u32[]{:S(2)}) %all-to-all-start.4) | async-done | bytes 1048608 | tf_op jit(solution)/shard_map/all_to_all | solution.py:92
  119.1 0.1 reduce_sum.76
  119.2 0.0 copy-done.1
  119.2 0.0 copy-done.3
  119.2 0.0 copy-start.2
  119.2 0.6 broadcast_in_dim.22
  119.8 9.8 %all-to-all-start.5 = ((f32[16,1,128]{2,1,0:T(1,128)}), f32[16,1,128]{2,1,0:T(1,128)S(1)}, u32[]{:S(2)}, u32[]{:S(2)}) async-start(f32[16,1,128]{2,1,0:T(1,128)} %broadcast_in_dim.22), calls=%async_computation.5 | async-start | bytes 16384 | tf_op jit(solution)/shard_map/all_to_all | solution.py:42
  129.7 0.1 dynamic-slice
  129.7 6.8 %all-to-all-done.5 = f32[16,1,128]{2,1,0:T(1,128)S(1)} async-done(((f32[16,1,128]{2,1,0:T(1,128)}), f32[16,1,128]{2,1,0:T(1,128)S(1)}, u32[]{:S(2)}, u32[]{:S(2)}) %all-to-all-start.5) | async-done | bytes 8224 | tf_op jit(solution)/shard_map/all_to_all | solution.py:42
  136.6 0.6 broadcast_in_dim.23
  137.2 4.7 %all-to-all-start.6 = ((f32[32,1,128]{2,1,0:T(1,128)}), f32[32,1,128]{2,1,0:T(1,128)S(1)}, u32[]{:S(2)}, u32[]{:S(2)}) async-start(f32[32,1,128]{2,1,0:T(1,128)} %broadcast_in_dim.23), calls=%async_computation.6 | async-start | bytes 32768 | tf_op jit(solution)/shard_map/all_to_all | solution.py:42
  141.9 0.8 dynamic-slice_subtract_fusion
  142.7 7.8 %all-to-all-done.6 = f32[32,1,128]{2,1,0:T(1,128)S(1)} async-done(((f32[32,1,128]{2,1,0:T(1,128)}), f32[32,1,128]{2,1,0:T(1,128)S(1)}, u32[]{:S(2)}, u32[]{:S(2)}) %all-to-all-start.6) | async-done | bytes 16416 | tf_op jit(solution)/shard_map/all_to_all | solution.py:42
  150.5 0.0 copy-start.6
  150.5 0.6 multiply_add_fusion
  151.2 0.0 copy-done.2
  151.2 0.0 copy-done.6
  (20 shorter events, 0.3 us)
Async XLA Ops:
  0.6 18.9 %copy-start.7 = (bf16[256,128]{1,0:T(8,128)(2,1)S(1)}, bf16[256,128]{1,0:T(8,128)(2,1)}, u32[]{:S(2)}) copy-start(bf16[256,128]{1,0:T(8,128)(2,1)} %param.9) | copy-start | bytes 196612
  0.6 18.8 %copy-start.5 = (f32[128]{0:T(128)S(1)}, f32[128]{0:T(128)}, u32[]{:S(2)}) copy-start(f32[128]{0:T(128)} %param.16) | copy-start | bytes 1540
  0.7 18.9 %collective-permute-start.1 = (bf16[256,128]{1,0:T(8,128)(2,1)}, bf16[256,128]{1,0:T(8,128)(2,1)S(1)}, u32[]{:S(2)}, u32[]{:S(2)}) collective-permute-start(bf16[256,128]{1,0:T(8,128)(2,1)} %param.9), channel_id=1, source_target_pairs={{0,64},{64,0},{1,65},{65,1},{2,66},{66,2},{3,67},{67,3},{4,68},{68... | collective-permute-start | bytes 196616 | tf_op jit(solution)/shard_map/ppermute | solution.py:60
  7.4 23.8 %all-to-all-start = ((bf16[32,64,128]{2,1,0:T(8,128)(2,1)}), bf16[32,64,128]{2,1,0:T(8,128)(2,1)S(1)}, u32[]{:S(2)}, u32[]{:S(2)}) async-start(bf16[32,64,128]{2,1,0:T(8,128)(2,1)} %broadcast_in_dim.16), calls=%async_computation | async-start | bytes 1048576 | tf_op jit(solution)/shard_map/all_to_all | solution.py:42
  26.8 36.0 %copy-start = (f32[256,128]{1,0:T(8,128)S(1)}, f32[256,128]{1,0:T(8,128)}, u32[]{:S(2)}) copy-start(f32[256,128]{1,0:T(8,128)} %param.13) | copy-start | bytes 393220
  26.8 35.9 %copy-start.4 = (f32[256]{0:T(256)S(1)}, f32[256]{0:T(256)}, u32[]{:S(2)}) copy-start(f32[256]{0:T(256)} %param.12) | copy-start | bytes 3076
  31.9 56.6 %copy-start.8 = (f32[128]{0:T(128)S(1)}, f32[128]{0:T(128)}, u32[]{:S(2)}) copy-start(f32[128]{0:T(128)} %param.17) | copy-start | bytes 1540
  59.3 14.9 %all-to-all-start.2 = ((f32[16,32,128]{2,1,0:T(8,128)}), f32[16,32,128]{2,1,0:T(8,128)S(1)}, u32[]{:S(2)}, u32[]{:S(2)}) async-start(f32[16,32,128]{2,1,0:T(8,128)} %broadcast_in_dim.18), calls=%async_computation.2 | async-start | bytes 524288 | tf_op jit(solution)/shard_map/all_to_all | solution.py:42
  62.8 10.3 %collective-permute-start = (f32[258,128]{1,0:T(8,128)S(1)}, f32[258,128]{1,0:T(8,128)S(1)}, u32[]{:S(2)}, u32[]{:S(2)}) collective-permute-start(f32[258,128]{1,0:T(8,128)S(1)} %pad_maximum_fusion.1), channel_id=1, source_target_pairs={{0,64},{64,0},{1,65},{65,1},{2,66},{66,2},{3,67},{67,3},{4,68},{68... | collective-permute-start | bytes 396296 | tf_op jit(solution)/shard_map/ppermute | solution.py:62
  68.4 50.8 %copy-start.1 = (f32[64,128]{1,0:T(8,128)S(1)}, f32[64,128]{1,0:T(8,128)}, u32[]{:S(2)}) copy-start(f32[64,128]{1,0:T(8,128)} %param.15) | copy-start | bytes 98308
  68.4 50.8 %copy-start.3 = (f32[64,128]{1,0:T(8,128)S(1)}, f32[64,128]{1,0:T(8,128)}, u32[]{:S(2)}) copy-start(f32[64,128]{1,0:T(8,128)} %param.14) | copy-start | bytes 98308
  75.0 13.5 %all-to-all-start.3 = ((f32[32,1,128]{2,1,0:T(1,128)}), f32[32,1,128]{2,1,0:T(1,128)S(1)}, u32[]{:S(2)}, u32[]{:S(2)}) async-start(f32[32,1,128]{2,1,0:T(1,128)} %broadcast_in_dim.21), calls=%async_computation.3 | async-start | bytes 32768 | tf_op jit(solution)/shard_map/all_to_all | solution.py:42
  90.4 28.7 %all-to-all-start.4 = ((f32[32,64,128]{2,1,0:T(8,128)}), f32[32,64,128]{2,1,0:T(8,128)S(1)}, u32[]{:S(2)}, u32[]{:S(2)}) async-start(f32[32,64,128]{2,1,0:T(8,128)} %fusion.16), calls=%async_computation.4 | async-start | bytes 2097152 | tf_op jit(solution)/shard_map/all_to_all | solution.py:92
  119.2 32.0 %copy-start.2 = (f32[64,128]{1,0:T(8,128)}, f32[64,128]{1,0:T(8,128)S(1)}, u32[]{:S(2)}) copy-start(f32[64,128]{1,0:T(8,128)S(1)} %get-tuple-element.5) | copy-start | bytes 98308
  119.8 16.7 %all-to-all-start.5 = ((f32[16,1,128]{2,1,0:T(1,128)}), f32[16,1,128]{2,1,0:T(1,128)S(1)}, u32[]{:S(2)}, u32[]{:S(2)}) async-start(f32[16,1,128]{2,1,0:T(1,128)} %broadcast_in_dim.22), calls=%async_computation.5 | async-start | bytes 16384 | tf_op jit(solution)/shard_map/all_to_all | solution.py:42
  137.2 13.3 %all-to-all-start.6 = ((f32[32,1,128]{2,1,0:T(1,128)}), f32[32,1,128]{2,1,0:T(1,128)S(1)}, u32[]{:S(2)}, u32[]{:S(2)}) async-start(f32[32,1,128]{2,1,0:T(1,128)} %broadcast_in_dim.23), calls=%async_computation.6 | async-start | bytes 32768 | tf_op jit(solution)/shard_map/all_to_all | solution.py:42
  150.5 0.6 copy-start.6

commit v2 on v1

--- a/solution.py
+++ b/solution.py
@@ -57,6 +57,12 @@
     def both(mine, peer):
         return jnp.where(zl == 0, jnp.concatenate([mine, peer]), jnp.concatenate([peer, mine]))
 
+    copies = jnp.broadcast_to(direction.astype(jnp.bfloat16)[None], (n_plane, own, targets))
+    copies, descriptors, resid, row_weight, freqs, phases, direction = lax.optimization_barrier(
+        (copies, descriptors, resid, row_weight, freqs, phases, direction)
+    )
+    gathered = lax.all_to_all(copies, PLANE, 0, 0, tiled=True).reshape(-1, targets)
+
     rows_x = both(descriptors, lax.ppermute(descriptors, "zl", swap))
     packed = jnp.concatenate([resid, row_weight.reshape(-1, targets)])
     peer = lax.ppermute(packed, "zl", swap)
@@ -67,24 +73,28 @@
     freq_cols = freqs.reshape(desc, n_x, 2, -1)
     freq_cols = lax.dynamic_index_in_dim(freq_cols, zl, 2, keepdims=False).reshape(desc, -1)
     phase_cols = lax.dynamic_index_in_dim(phases.reshape(n_x, 2, -1), zl, 1, keepdims=False).reshape(-1)
-
-    gathered = spread(direction.astype(jnp.bfloat16), PLANE).reshape(-1, targets)
     angle = jnp.dot(rows_x, freq_cols, preferred_element_type=jnp.float32) + phase_cols[None, :]
     feats = scaled_cos(angle).astype(jnp.bfloat16)
+    penalty = ridge * jnp.sum(direction * direction, axis=0)
+    extra = jnp.broadcast_to(penalty[None, None], (n_column, 8, targets))
+    rows_weight = jnp.broadcast_to(rows_weight[:, None], rows_resid.shape)
+    first = zl * rows_dev
+    gathered, feats, rows_resid, rows_weight, extra, first = lax.optimization_barrier(
+        (gathered, feats, rows_resid, rows_weight, extra, first)
+    )
     partial = jnp.dot(feats, gathered, preferred_element_type=jnp.float32)
 
-    penalty = ridge * jnp.sum(direction * direction, axis=0)
-    extra = jnp.broadcast_to(penalty[None, None], (n_column, 8, targets))
     sent = jnp.concatenate([partial.reshape(n_column, -1, targets), extra], axis=1)
     came = jnp.sum(lax.all_to_all(sent, COLUMN, 0, 0, tiled=True), axis=0)
     share = came.shape[0] - 8
-    image = rows_weight[:, None] * spread(came[:share], COLUMN).reshape(-1, targets)
+    image = rows_weight * spread(came[:share], COLUMN).reshape(-1, targets)
     curvature = total_of(jnp.sum(image * image, axis=0)[None] + came[share : share + 1], PLANE)
     alpha = gamma / curvature[0]
     coef_new = coef + alpha[None, :] * direction
     rows_new = rows_resid - alpha[None, :] * image
-    weighted_b = (rows_weight[:, None] * rows_new).astype(jnp.bfloat16)
-    resid_new = lax.dynamic_slice_in_dim(rows_new, zl * rows_dev, rows_dev, 0)
+    weighted_b = (rows_weight * rows_new).astype(jnp.bfloat16)
+    resid_new = resid - alpha[None, :] * lax.dynamic_slice_in_dim(image, first, rows_dev, 0)
+    weighted_b, coef_new, resid_new = lax.optimization_barrier((weighted_b, coef_new, resid_new))
 
     terms = lax.dot_general(
         feats, weighted_b, (((0,), (0,)), ((), ())), preferred_element_type=jnp.float32

time: 152 us -> 143 us (0.941)
  blocking collectives: 26.5 us -> 96.6 us
  waiting for transfers between devices: 58 us -> 11.6 us
  starting transfers between devices: 44.2 us -> 21.9 us
  local copies, waits for them, and re-layouts: 9.03 us -> 2.49 us
  other arithmetic: 5.65 us -> 3.52 us
  matrix products: 6.81 us -> 4.83 us
    all_to_all x0 -> x4, blocking collectives: none -> 69.7 us  [the longest x3 42.1 us: spread(): return lax.all_to_all(copies, axes, 0, 0, tiled=True)]
    all_to_all x5 -> x1, starting transfers between devices: 32.6 us -> 5.33 us  [spread(): return lax.all_to_all(copies, axes, 0, 0, tiled=True)]
    all_to_all x1, waiting for transfers between devices: 24.8 us -> 3.05 us  [body(): lax.all_to_all(copies, PLANE, 0, 0, tiled=True).reshape(-1, targets)]
    all_to_all x5 -> x1, waiting for transfers between devices: 28.5 us -> 8.56 us  [spread(): return lax.all_to_all(copies, axes, 0, 0, tiled=True)]
    all_to_all x1, starting transfers between devices: 3.93 us -> 10.6 us  [body(): lax.all_to_all(copies, PLANE, 0, 0, tiled=True).reshape(-1, targets)]
    ppermute x1, waiting for transfers between devices: 4.63 us -> 0.01 us  [body(): peer = lax.ppermute(packed, 'zl', swap)]
    convert_element_type x3 -> x2, other arithmetic: 3.81 us -> 0.89 us  [the longest x1 0.85 us: body(): direction.astype(jnp.bfloat16)[None]]
    broadcast_in_dim x5 -> x4, local copies, waits for them, and re-layouts: 3.53 us -> 0.66 us  [spread(): copies = jnp.broadcast_to(value[None], (n,) + value.shape)]
  transfers between devices with their start and end apart: 8 -> 4, of which waited for: 7 -> 2; matrix products, arithmetic and copies ran while one was open for 10% -> 4% of each run, Pallas kernels for 0% -> 0%
where the time goes in v2:
time: 143 us; the launch traced here: 142 us
  blocking collectives  96.6 us (68%)
  starting transfers between devices  21.9 us (15%)
  waiting for transfers between devices  11.6 us (8%)
  matrix products  4.83 us (3%)
  other arithmetic  3.52 us (2%)
  local copies, waits for them, and re-layouts  2.49 us (2%)
    all_to_all x3, blocking collectives, spread(): return lax.all_to_all(copies, axes, 0, 0, tiled=True)  42.1 us
    all_to_all x1, blocking collectives, body(): lax.all_to_all(terms.reshape(n_plane, own, targets), PLANE, 0, 0, tiled=T...  27.6 us
    all_to_all x1, blocking collectives, body(): came = jnp.sum(lax.all_to_all(sent, COLUMN, 0, 0, tiled=True), axis=0)  26.9 us
    all_to_all x1, starting transfers between devices, body(): lax.all_to_all(copies, PLANE, 0, 0, tiled=True).reshape(-1, targets)  10.6 us
    all_to_all x1, waiting for transfers between devices, spread(): return lax.all_to_all(copies, axes, 0, 0, tiled=True)  8.56 us
    all_to_all x1, starting transfers between devices, spread(): return lax.all_to_all(copies, axes, 0, 0, tiled=True)  5.33 us
    ppermute x1, starting transfers between devices, body(): rows_x = both(descriptors, lax.ppermute(descriptors, 'zl', swap))  4 us
    dot_general x1, matrix products, body(): jnp.dot(rows_x, freq_cols, preferred_element_type=jnp.float32)  3.39 us
  transfers between devices with their start and end apart: 4, of which 2 were waited for; matrix products, arithmetic and copies ran while one was open for 4% of the time, Pallas kernels for 0%

profile of v2, /device:TPU:1, one launch (start us, length us, event | category | flops | bytes accessed | tf_op | source)
XLA Modules:
  0.0 141.9 jit_solution(15712386912383192642)
XLA Ops:
  0.6 0.0 copy-start.2
  0.6 0.0 copy-start.1
  0.7 0.0 copy-start.5
  0.7 0.8 convert_element_type.9
  1.5 0.9 broadcast_in_dim.18
  2.4 0.0 copy-start.7
  2.4 0.0 copy-start.9
  2.4 10.6 %all-to-all-start = ((bf16[32,64,128]{2,1,0:T(8,128)(2,1)}), bf16[32,64,128]{2,1,0:T(8,128)(2,1)S(1)}, u32[]{:S(2)}, u32[]{:S(2)}) async-start(bf16[32,64,128]{2,1,0:T(8,128)(2,1)} %broadcast_in_dim.18), calls=%async_computation | async-start | bytes 1048576 | tf_op jit(solution)/shard_map/all_to_all | solution.py:64
  13.1 4.0 %collective-permute-start = (bf16[256,128]{1,0:T(8,128)(2,1)}, bf16[256,128]{1,0:T(8,128)(2,1)S(1)}, u32[]{:S(2)}, u32[]{:S(2)}) collective-permute-start(bf16[256,128]{1,0:T(8,128)(2,1)} %param.9), channel_id=1, source_target_pairs={{0,64},{64,0},{1,65},{65,1},{2,66},{66,2},{3,67},{67,3},{4,68},{68... | collective-permute-start | bytes 196616 | tf_op jit(solution)/shard_map/ppermute | solution.py:66
  17.1 0.9 pad_maximum_fusion.1
  18.0 1.9 %collective-permute-start.1 = (f32[258,128]{1,0:T(8,128)S(1)}, f32[258,128]{1,0:T(8,128)S(1)}, u32[]{:S(2)}, u32[]{:S(2)}) collective-permute-start(f32[258,128]{1,0:T(8,128)S(1)} %pad_maximum_fusion.1), channel_id=1, source_target_pairs={{0,64},{64,0},{1,65},{65,1},{2,66},{66,2},{3,67},{67,3},{4,68},{68... | collective-permute-start | bytes 396296 | tf_op jit(solution)/shard_map/ppermute | solution.py:68
  19.9 0.0 copy-done.1
  20.0 0.7 copy.15
  20.6 0.0 copy-done.5
  20.7 0.0 copy-done.2
  20.7 0.0 copy-done.7
  20.8 0.0 collective-permute-done
  20.8 0.0 copy-done.9
  20.8 0.0 copy-start.6
  20.8 0.0 copy-start
  20.8 3.4 %add_convert_fusion = bf16[512,2048]{1,0:T(8,128)(2,1)S(1)} fusion(bf16[128,2048]{0,1:T(8,128)(2,1)S(1)} %bitcast.28, f32[2048]{0:T(1024)S(1)} %bitcast.32, bf16[256,128]{1,0:T(8,128)(2,1)S(1)} %collective-permute-done, bf16[256,128]{1,0:T(8,128)(2,1)S(1)} %copy-done.9, pred[]{:T(512)S(6)} %eq.2), kind=kOutput, calls=%fused_computation | convolution fusion | flops 291045376 | bytes 2760705 | tf_op jit(solution)/shard_map/dot_general | solution.py:76
  24.2 0.0 collective-permute-done.1
  24.3 0.0 copy-done.6
  24.3 0.0 copy-done
  24.3 3.1 %all-to-all-done = bf16[32,64,128]{2,1,0:T(8,128)(2,1)S(1)} async-done(((bf16[32,64,128]{2,1,0:T(8,128)(2,1)}), bf16[32,64,128]{2,1,0:T(8,128)(2,1)S(1)}, u32[]{:S(2)}, u32[]{:S(2)}) %all-to-all-start) | async-done | bytes 524320 | tf_op jit(solution)/shard_map/all_to_all | solution.py:64
  27.4 0.1 broadcast_in_dim.19
  27.5 0.7 fusion.8
  28.2 0.0 copy-start.10
  28.2 0.0 copy-start.4
  28.3 26.9 %all_to_all.35 = f32[16,40,128]{2,1,0:T(8,128)S(1)} all-to-all(f32[16,40,128]{2,1,0:T(8,128)S(1)} %pad_maximum_fusion), channel_id=1, replica_groups=mesh['x'=4,'zl'=2,'y'=8,'zh'=4,'core'=2] {'zl','zh','core'}, dimensions={0} | all-to-all | bytes 655360 | tf_op jit(solution)/shard_map/all_to_all | solution.py:88
  55.2 14.4 %all_to_all.36 = f32[16,32,128]{2,1,0:T(8,128)S(1)} all-to-all(f32[16,32,128]{2,1,0:T(8,128)S(1)} %broadcast_in_dim.21), channel_id=1, replica_groups=mesh['x'=4,'zl'=2,'y'=8,'zh'=4,'core'=2] {'zl','zh','core'}, dimensions={0} | all-to-all | bytes 524288 | tf_op jit(solution)/shard_map/all_to_all | solution.py:42
  69.7 0.1 multiply_reduce_fusion
  69.8 0.6 broadcast_in_dim.24
  70.4 5.3 %all-to-all-start.3 = ((f32[32,1,128]{2,1,0:T(1,128)}), f32[32,1,128]{2,1,0:T(1,128)S(1)}, u32[]{:S(2)}, u32[]{:S(2)}) async-start(f32[32,1,128]{2,1,0:T(1,128)} %broadcast_in_dim.24), calls=%async_computation.3 | async-start | bytes 32768 | tf_op jit(solution)/shard_map/all_to_all | solution.py:42
  75.7 8.6 %all-to-all-done.3 = f32[32,1,128]{2,1,0:T(1,128)S(1)} async-done(((f32[32,1,128]{2,1,0:T(1,128)}), f32[32,1,128]{2,1,0:T(1,128)S(1)}, u32[]{:S(2)}, u32[]{:S(2)}) %all-to-all-start.3) | async-done | bytes 16416 | tf_op jit(solution)/shard_map/all_to_all | solution.py:42
  84.3 0.0 copy-done.10
  84.3 0.0 copy-done.4
  84.4 0.0 copy-start.3
  84.4 0.7 multiply_subtract_fusion
  85.1 0.7 fusion.9
  85.8 27.6 %all_to_all.37 = f32[32,64,128]{2,1,0:T(8,128)S(1)} all-to-all(f32[32,64,128]{2,1,0:T(8,128)S(1)} %bitcast.24), channel_id=1, replica_groups=mesh['x'=4,'zl'=2,'y'=8,'zh'=4,'core'=2] {'x','y'}, dimensions={0} | all-to-all | bytes 2097152 | tf_op jit(solution)/shard_map/all_to_all | solution.py:102
  113.5 0.1 reduce_sum.76
  113.6 14.4 %all_to_all.38 = f32[16,1,128]{2,1,0:T(1,128)S(1)} all-to-all(f32[16,1,128]{2,1,0:T(1,128)S(1)} %broadcast_in_dim.25), channel_id=1, replica_groups=mesh['x'=4,'zl'=2,'y'=8,'zh'=4,'core'=2] {'zl','zh','core'}, dimensions={0} | all-to-all | bytes 16384 | tf_op jit(solution)/shard_map/all_to_all | solution.py:42
  128.1 13.2 %all_to_all.39 = f32[32,1,128]{2,1,0:T(1,128)S(1)} all-to-all(f32[32,1,128]{2,1,0:T(1,128)S(1)} %broadcast_in_dim.26), channel_id=1, replica_groups=mesh['x'=4,'zl'=2,'y'=8,'zh'=4,'core'=2] {'x','y'}, dimensions={0} | all-to-all | bytes 32768 | tf_op jit(solution)/shard_map/all_to_all | solution.py:42
  141.3 0.0 copy-start.8
  141.3 0.0 copy-done.3
  141.3 0.6 multiply_add_fusion
  141.9 0.0 copy-done.8
  (25 shorter events, 0.4 us)
Async XLA Ops:
  0.6 20.0 %copy-start.2 = (f32[64,128]{1,0:T(8,128)S(1)}, f32[64,128]{1,0:T(8,128)}, u32[]{:S(2)}) copy-start(f32[64,128]{1,0:T(8,128)} %param.15) | copy-start | bytes 98308
  0.6 19.3 %copy-start.1 = (bf16[128,4096]{1,0:T(8,128)(2,1)S(1)}, bf16[128,4096]{1,0:T(8,128)(2,1)}, u32[]{:S(2)}) copy-start(bf16[128,4096]{1,0:T(8,128)(2,1)} %param.10) | copy-start | bytes 3145732
  0.7 20.0 %copy-start.5 = (f32[4096]{0:T(1024)S(1)}, f32[4096]{0:T(1024)}, u32[]{:S(2)}) copy-start(f32[4096]{0:T(1024)} %param.11) | copy-start | bytes 49156
  2.4 18.3 %copy-start.7 = (f32[128]{0:T(128)S(1)}, f32[128]{0:T(128)}, u32[]{:S(2)}) copy-start(f32[128]{0:T(128)} %param.16) | copy-start | bytes 1540
  2.4 18.4 %copy-start.9 = (bf16[256,128]{1,0:T(8,128)(2,1)S(1)}, bf16[256,128]{1,0:T(8,128)(2,1)}, u32[]{:S(2)}) copy-start(bf16[256,128]{1,0:T(8,128)(2,1)} %param.9) | copy-start | bytes 196612
  2.4 25.0 %all-to-all-start = ((bf16[32,64,128]{2,1,0:T(8,128)(2,1)}), bf16[32,64,128]{2,1,0:T(8,128)(2,1)S(1)}, u32[]{:S(2)}, u32[]{:S(2)}) async-start(bf16[32,64,128]{2,1,0:T(8,128)(2,1)} %broadcast_in_dim.18), calls=%async_computation | async-start | bytes 1048576 | tf_op jit(solution)/shard_map/all_to_all | solution.py:64
  13.1 7.7 %collective-permute-start = (bf16[256,128]{1,0:T(8,128)(2,1)}, bf16[256,128]{1,0:T(8,128)(2,1)S(1)}, u32[]{:S(2)}, u32[]{:S(2)}) collective-permute-start(bf16[256,128]{1,0:T(8,128)(2,1)} %param.9), channel_id=1, source_target_pairs={{0,64},{64,0},{1,65},{65,1},{2,66},{66,2},{3,67},{67,3},{4,68},{68... | collective-permute-start | bytes 196616 | tf_op jit(solution)/shard_map/ppermute | solution.py:66
  18.0 6.2 %collective-permute-start.1 = (f32[258,128]{1,0:T(8,128)S(1)}, f32[258,128]{1,0:T(8,128)S(1)}, u32[]{:S(2)}, u32[]{:S(2)}) collective-permute-start(f32[258,128]{1,0:T(8,128)S(1)} %pad_maximum_fusion.1), channel_id=1, source_target_pairs={{0,64},{64,0},{1,65},{65,1},{2,66},{66,2},{3,67},{67,3},{4,68},{68... | collective-permute-start | bytes 396296 | tf_op jit(solution)/shard_map/ppermute | solution.py:68
  20.8 3.5 %copy-start.6 = (f32[256]{0:T(256)S(1)}, f32[256]{0:T(256)}, u32[]{:S(2)}) copy-start(f32[256]{0:T(256)} %param.12) | copy-start | bytes 3076
  20.8 3.5 %copy-start = (f32[256,128]{1,0:T(8,128)S(1)}, f32[256,128]{1,0:T(8,128)}, u32[]{:S(2)}) copy-start(f32[256,128]{1,0:T(8,128)} %param.13) | copy-start | bytes 393220
  28.2 56.1 %copy-start.10 = (f32[128]{0:T(128)S(1)}, f32[128]{0:T(128)}, u32[]{:S(2)}) copy-start(f32[128]{0:T(128)} %param.17) | copy-start | bytes 1540
  28.2 56.1 %copy-start.4 = (f32[64,128]{1,0:T(8,128)S(1)}, f32[64,128]{1,0:T(8,128)}, u32[]{:S(2)}) copy-start(f32[64,128]{1,0:T(8,128)} %param.14) | copy-start | bytes 98308
  70.4 13.9 %all-to-all-start.3 = ((f32[32,1,128]{2,1,0:T(1,128)}), f32[32,1,128]{2,1,0:T(1,128)S(1)}, u32[]{:S(2)}, u32[]{:S(2)}) async-start(f32[32,1,128]{2,1,0:T(1,128)} %broadcast_in_dim.24), calls=%async_computation.3 | async-start | bytes 32768 | tf_op jit(solution)/shard_map/all_to_all | solution.py:42
  84.4 56.9 %copy-start.3 = (f32[64,128]{1,0:T(8,128)}, f32[64,128]{1,0:T(8,128)S(1)}, u32[]{:S(2)}) copy-start(f32[64,128]{1,0:T(8,128)S(1)} %multiply_add_fusion.1) | copy-start | bytes 98308
  141.3 0.7 copy-start.8

commit v3 on v2

--- a/solution.py
+++ b/solution.py
@@ -24,6 +24,9 @@
     -2.707541852942086e-07,
     1.7231808202566867e-09,
 )
+
+TERM_MAX = 32000.0
+TINY = 1e-30
 
 
 def scaled_cos(angle):
@@ -78,9 +81,9 @@
     penalty = ridge * jnp.sum(direction * direction, axis=0)
     extra = jnp.broadcast_to(penalty[None, None], (n_column, 8, targets))
     rows_weight = jnp.broadcast_to(rows_weight[:, None], rows_resid.shape)
-    first = zl * rows_dev
-    gathered, feats, rows_resid, rows_weight, extra, first = lax.optimization_barrier(
-        (gathered, feats, rows_resid, rows_weight, extra, first)
+    resid_size = jnp.sum(jnp.abs(rows_weight * rows_resid), axis=0)
+    gathered, feats, rows_resid, rows_weight, extra, resid_size, lower = lax.optimization_barrier(
+        (gathered, feats, rows_resid, rows_weight, extra, resid_size, zl == 0)
     )
     partial = jnp.dot(feats, gathered, preferred_element_type=jnp.float32)
 
@@ -88,19 +91,29 @@
     came = jnp.sum(lax.all_to_all(sent, COLUMN, 0, 0, tiled=True), axis=0)
     share = came.shape[0] - 8
     image = rows_weight * spread(came[:share], COLUMN).reshape(-1, targets)
-    curvature = total_of(jnp.sum(image * image, axis=0)[None] + came[share : share + 1], PLANE)
-    alpha = gamma / curvature[0]
+    local = jnp.concatenate([
+        jnp.sum(image * image, axis=0)[None] + came[share : share + 1],
+        resid_size[None],
+        jnp.sum(jnp.abs(rows_weight * image), axis=0)[None],
+        jnp.zeros((1, targets), jnp.float32),
+    ])
+    seen = spread(local, PLANE)
+    alpha = gamma / jnp.sum(seen[:, 0], axis=0)
+    bound = jnp.max(seen[:, 1], axis=0) + jnp.abs(alpha) * jnp.max(seen[:, 2], axis=0)
+    scale = TERM_MAX / jnp.maximum(SCALE * bound, TINY)
     coef_new = coef + alpha[None, :] * direction
     rows_new = rows_resid - alpha[None, :] * image
     weighted_b = (rows_weight * rows_new).astype(jnp.bfloat16)
-    resid_new = resid - alpha[None, :] * lax.dynamic_slice_in_dim(image, first, rows_dev, 0)
+    resid_new = jnp.where(lower, rows_new[:rows_dev], rows_new[rows_dev:])
     weighted_b, coef_new, resid_new = lax.optimization_barrier((weighted_b, coef_new, resid_new))
 
     terms = lax.dot_general(
         feats, weighted_b, (((0,), (0,)), ((), ())), preferred_element_type=jnp.float32
     )
+    terms = (terms * scale[None, :]).astype(jnp.float16)
     terms = lax.all_to_all(terms.reshape(n_plane, own, targets), PLANE, 0, 0, tiled=True)
-    gradient = jnp.sum(terms, axis=0) - ridge[None, :] * coef_new
+    summed = jnp.sum(terms.astype(jnp.float32), axis=0) * (1.0 / scale)[None, :]
+    gradient = summed - ridge[None, :] * coef_new
     gamma_new = total_of(total_of(jnp.sum(gradient * gradient, axis=0)[None], COLUMN), PLANE)[0]
     direction_new = gradient + (gamma_new / gamma)[None, :] * direction
     return (coef_new, resid_new, direction_new, gamma_new)

time: 143 us -> 133 us (0.930)
  blocking collectives: 96.6 us -> 85.5 us
  waiting for transfers between devices: 11.6 us -> 14.1 us
  starting transfers between devices: 21.9 us -> 20 us
    all_to_all x1, blocking collectives: 27.6 us -> 17.3 us  [body(): lax.all_to_all(terms.reshape(n_plane, own, targets), PLANE, 0, 0, tiled=T...]
    all_to_all x1, waiting for transfers between devices: 8.56 us -> 11.2 us  [spread(): return lax.all_to_all(copies, axes, 0, 0, tiled=True)]
    all_to_all x1, starting transfers between devices: 5.33 us -> 3.43 us  [spread(): return lax.all_to_all(copies, axes, 0, 0, tiled=True)]
where the time goes in v3:
time: 133 us; the launch traced here: 132 us
  blocking collectives  85.5 us (64%)
  starting transfers between devices  20 us (15%)
  waiting for transfers between devices  14.1 us (11%)
  matrix products  4.86 us (4%)
  other arithmetic  3.78 us (3%)
  local copies, waits for them, and re-layouts  2.7 us (2%)
    all_to_all x3, blocking collectives, spread(): return lax.all_to_all(copies, axes, 0, 0, tiled=True)  41.3 us
    all_to_all x1, blocking collectives, body(): came = jnp.sum(lax.all_to_all(sent, COLUMN, 0, 0, tiled=True), axis=0)  26.9 us
    all_to_all x1, blocking collectives, body(): lax.all_to_all(terms.reshape(n_plane, own, targets), PLANE, 0, 0, tiled=T...  17.3 us
    all_to_all x1, waiting for transfers between devices, spread(): return lax.all_to_all(copies, axes, 0, 0, tiled=True)  11.2 us
    all_to_all x1, starting transfers between devices, body(): lax.all_to_all(copies, PLANE, 0, 0, tiled=True).reshape(-1, targets)  10.6 us
    ppermute x1, starting transfers between devices, body(): rows_x = both(descriptors, lax.ppermute(descriptors, 'zl', swap))  4 us
    all_to_all x1, starting transfers between devices, spread(): return lax.all_to_all(copies, axes, 0, 0, tiled=True)  3.43 us
    dot_general x1, matrix products, body(): jnp.dot(rows_x, freq_cols, preferred_element_type=jnp.float32)  3.39 us
  transfers between devices with their start and end apart: 4, of which 2 were waited for; matrix products, arithmetic and copies ran while one was open for 4% of the time, Pallas kernels for 0%

profile of v3, /device:TPU:1, one launch (start us, length us, event | category | flops | bytes accessed | tf_op | source)
XLA Modules:
  0.0 131.9 jit_solution(9757858414279070096)
XLA Ops:
  0.6 0.0 copy-start.1
  0.6 0.0 copy-start
  0.7 0.0 copy-start.5
  0.7 0.8 convert_element_type.15
  1.5 0.9 broadcast_in_dim.22
  2.4 0.0 copy-start.7
  2.4 0.0 copy-start.10
  2.4 10.6 %all-to-all-start = ((bf16[32,64,128]{2,1,0:T(8,128)(2,1)}), bf16[32,64,128]{2,1,0:T(8,128)(2,1)S(1)}, u32[]{:S(2)}, u32[]{:S(2)}) async-start(bf16[32,64,128]{2,1,0:T(8,128)(2,1)} %broadcast_in_dim.22), calls=%async_computation | async-start | bytes 1048576 | tf_op jit(solution)/shard_map/all_to_all | solution.py:67
  13.1 4.0 %collective-permute-start = (bf16[256,128]{1,0:T(8,128)(2,1)}, bf16[256,128]{1,0:T(8,128)(2,1)S(1)}, u32[]{:S(2)}, u32[]{:S(2)}) collective-permute-start(bf16[256,128]{1,0:T(8,128)(2,1)} %param.9), channel_id=1, source_target_pairs={{0,64},{64,0},{1,65},{65,1},{2,66},{66,2},{3,67},{67,3},{4,68},{68... | collective-permute-start | bytes 196616 | tf_op jit(solution)/shard_map/ppermute | solution.py:69
  17.1 0.9 pad_maximum_fusion.1
  18.0 1.9 %collective-permute-start.1 = (f32[258,128]{1,0:T(8,128)S(1)}, f32[258,128]{1,0:T(8,128)S(1)}, u32[]{:S(2)}, u32[]{:S(2)}) collective-permute-start(f32[258,128]{1,0:T(8,128)S(1)} %pad_maximum_fusion.1), channel_id=1, source_target_pairs={{0,64},{64,0},{1,65},{65,1},{2,66},{66,2},{3,67},{67,3},{4,68},{68... | collective-permute-start | bytes 396296 | tf_op jit(solution)/shard_map/ppermute | solution.py:71
  19.9 0.0 copy-done
  20.0 0.7 copy.15
  20.6 0.0 copy-done.5
  20.7 0.0 copy-done.1
  20.7 0.0 copy-done.7
  20.8 0.0 collective-permute-done
  20.8 0.0 copy-done.10
  20.8 0.0 copy-start.6
  20.8 0.0 copy-start.2
  20.8 3.4 %add_convert_fusion = bf16[512,2048]{1,0:T(8,128)(2,1)S(1)} fusion(bf16[128,2048]{0,1:T(8,128)(2,1)S(1)} %bitcast.37, f32[2048]{0:T(1024)S(1)} %bitcast.43, bf16[256,128]{1,0:T(8,128)(2,1)S(1)} %collective-permute-done, bf16[256,128]{1,0:T(8,128)(2,1)S(1)} %copy-done.10, pred[]{:T(512)S(6)} %eq.2), kind=kOutput, calls=%fused_computation | convolution fusion | flops 291045376 | bytes 2760705 | tf_op jit(solution)/shard_map/dot_general | solution.py:79
  24.2 0.0 collective-permute-done.1
  24.3 0.0 copy-done.6
  24.3 0.0 copy-done.2
  24.3 0.2 abs_reduce_fusion.1
  24.4 2.9 %all-to-all-done = bf16[32,64,128]{2,1,0:T(8,128)(2,1)S(1)} async-done(((bf16[32,64,128]{2,1,0:T(8,128)(2,1)}), bf16[32,64,128]{2,1,0:T(8,128)(2,1)S(1)}, u32[]{:S(2)}, u32[]{:S(2)}) %all-to-all-start) | async-done | bytes 524320 | tf_op jit(solution)/shard_map/all_to_all | solution.py:67
  27.4 0.1 broadcast_in_dim.23
  27.5 0.7 fusion.9
  28.2 0.0 copy-start.8
  28.2 0.0 copy-start.4
  28.3 26.9 %all_to_all.35 = f32[16,40,128]{2,1,0:T(8,128)S(1)} all-to-all(f32[16,40,128]{2,1,0:T(8,128)S(1)} %pad_maximum_fusion), channel_id=1, replica_groups=mesh['x'=4,'zl'=2,'y'=8,'zh'=4,'core'=2] {'zl','zh','core'}, dimensions={0} | all-to-all | bytes 655360 | tf_op jit(solution)/shard_map/all_to_all | solution.py:91
  55.2 0.7 broadcast_in_dim.25
  55.9 3.4 %all-to-all-start.2 = ((f32[16,32,128]{2,1,0:T(8,128)}), f32[16,32,128]{2,1,0:T(8,128)S(1)}, u32[]{:S(2)}, u32[]{:S(2)}) async-start(f32[16,32,128]{2,1,0:T(8,128)} %broadcast_in_dim.25), calls=%async_computation.2 | async-start | bytes 524288 | tf_op jit(solution)/shard_map/all_to_all | solution.py:45
  59.4 0.1 pad.3.clone
  59.4 11.2 %all-to-all-done.2 = f32[16,32,128]{2,1,0:T(8,128)S(1)} async-done(((f32[16,32,128]{2,1,0:T(8,128)}), f32[16,32,128]{2,1,0:T(8,128)S(1)}, u32[]{:S(2)}, u32[]{:S(2)}) %all-to-all-start.2) | async-done | bytes 262176 | tf_op jit(solution)/shard_map/all_to_all | solution.py:45
  70.6 0.1 multiply_reduce_fusion
  70.7 0.1 maximum_maximum_fusion
  70.8 14.4 %all_to_all.36 = f32[32,4,128]{2,1,0:T(4,128)S(1)} all-to-all(f32[32,4,128]{2,1,0:T(4,128)S(1)} %broadcast_in_dim.30), channel_id=1, replica_groups=mesh['x'=4,'zl'=2,'y'=8,'zh'=4,'core'=2] {'x','y'}, dimensions={0} | all-to-all | bytes 131072 | tf_op jit(solution)/shard_map/all_to_all | solution.py:45
  85.3 0.0 copy-done.8
  85.4 0.0 copy-done.4
  85.4 0.0 copy-start.3
  85.4 0.1 multiply_convert_fusion
  85.5 0.7 slice_select_fusion
  86.1 0.8 fusion
  86.9 17.3 %all_to_all.37 = f16[32,64,128]{2,1,0:T(8,128)(2,1)S(1)} all-to-all(f16[32,64,128]{2,1,0:T(8,128)(2,1)S(1)} %bitcast.33), channel_id=1, replica_groups=mesh['x'=4,'zl'=2,'y'=8,'zh'=4,'core'=2] {'x','y'}, dimensions={0} | all-to-all | bytes 1048576 | tf_op jit(solution)/shard_map/all_to_all | solution.py:114
  104.2 0.1 convert_reduce_fusion
  104.3 12.9 %all_to_all.38 = f32[16,1,128]{2,1,0:T(1,128)S(1)} all-to-all(f32[16,1,128]{2,1,0:T(1,128)S(1)} %broadcast_in_dim.31), channel_id=1, replica_groups=mesh['x'=4,'zl'=2,'y'=8,'zh'=4,'core'=2] {'zl','zh','core'}, dimensions={0} | all-to-all | bytes 16384 | tf_op jit(solution)/shard_map/all_to_all | solution.py:45
  117.3 13.9 %all_to_all.39 = f32[32,1,128]{2,1,0:T(1,128)S(1)} all-to-all(f32[32,1,128]{2,1,0:T(1,128)S(1)} %broadcast_in_dim.32), channel_id=1, replica_groups=mesh['x'=4,'zl'=2,'y'=8,'zh'=4,'core'=2] {'x','y'}, dimensions={0} | all-to-all | bytes 32768 | tf_op jit(solution)/shard_map/all_to_all | solution.py:45
  131.2 0.0 copy-start.9
  131.3 0.0 copy-done.3
  131.3 0.6 multiply_add_fusion
  131.9 0.0 copy-done.9
  (27 shorter events, 0.4 us)
Async XLA Ops:
  0.6 20.0 %copy-start.1 = (f32[64,128]{1,0:T(8,128)S(1)}, f32[64,128]{1,0:T(8,128)}, u32[]{:S(2)}) copy-start(f32[64,128]{1,0:T(8,128)} %param.15) | copy-start | bytes 98308
  0.6 19.3 %copy-start = (bf16[128,4096]{1,0:T(8,128)(2,1)S(1)}, bf16[128,4096]{1,0:T(8,128)(2,1)}, u32[]{:S(2)}) copy-start(bf16[128,4096]{1,0:T(8,128)(2,1)} %param.10) | copy-start | bytes 3145732
  0.7 20.0 %copy-start.5 = (f32[4096]{0:T(1024)S(1)}, f32[4096]{0:T(1024)}, u32[]{:S(2)}) copy-start(f32[4096]{0:T(1024)} %param.11) | copy-start | bytes 49156
  2.4 18.3 %copy-start.7 = (f32[128]{0:T(128)S(1)}, f32[128]{0:T(128)}, u32[]{:S(2)}) copy-start(f32[128]{0:T(128)} %param.16) | copy-start | bytes 1540
  2.4 18.4 %copy-start.10 = (bf16[256,128]{1,0:T(8,128)(2,1)S(1)}, bf16[256,128]{1,0:T(8,128)(2,1)}, u32[]{:S(2)}) copy-start(bf16[256,128]{1,0:T(8,128)(2,1)} %param.9) | copy-start | bytes 196612
  2.4 25.0 %all-to-all-start = ((bf16[32,64,128]{2,1,0:T(8,128)(2,1)}), bf16[32,64,128]{2,1,0:T(8,128)(2,1)S(1)}, u32[]{:S(2)}, u32[]{:S(2)}) async-start(bf16[32,64,128]{2,1,0:T(8,128)(2,1)} %broadcast_in_dim.22), calls=%async_computation | async-start | bytes 1048576 | tf_op jit(solution)/shard_map/all_to_all | solution.py:67
  13.1 7.7 %collective-permute-start = (bf16[256,128]{1,0:T(8,128)(2,1)}, bf16[256,128]{1,0:T(8,128)(2,1)S(1)}, u32[]{:S(2)}, u32[]{:S(2)}) collective-permute-start(bf16[256,128]{1,0:T(8,128)(2,1)} %param.9), channel_id=1, source_target_pairs={{0,64},{64,0},{1,65},{65,1},{2,66},{66,2},{3,67},{67,3},{4,68},{68... | collective-permute-start | bytes 196616 | tf_op jit(solution)/shard_map/ppermute | solution.py:69
  18.0 6.2 %collective-permute-start.1 = (f32[258,128]{1,0:T(8,128)S(1)}, f32[258,128]{1,0:T(8,128)S(1)}, u32[]{:S(2)}, u32[]{:S(2)}) collective-permute-start(f32[258,128]{1,0:T(8,128)S(1)} %pad_maximum_fusion.1), channel_id=1, source_target_pairs={{0,64},{64,0},{1,65},{65,1},{2,66},{66,2},{3,67},{67,3},{4,68},{68... | collective-permute-start | bytes 396296 | tf_op jit(solution)/shard_map/ppermute | solution.py:71
  20.8 3.5 %copy-start.6 = (f32[256]{0:T(256)S(1)}, f32[256]{0:T(256)}, u32[]{:S(2)}) copy-start(f32[256]{0:T(256)} %param.12) | copy-start | bytes 3076
  20.8 3.5 %copy-start.2 = (f32[256,128]{1,0:T(8,128)S(1)}, f32[256,128]{1,0:T(8,128)}, u32[]{:S(2)}) copy-start(f32[256,128]{1,0:T(8,128)} %param.13) | copy-start | bytes 393220
  28.2 57.1 %copy-start.8 = (f32[128]{0:T(128)S(1)}, f32[128]{0:T(128)}, u32[]{:S(2)}) copy-start(f32[128]{0:T(128)} %param.17) | copy-start | bytes 1540
  28.2 57.1 %copy-start.4 = (f32[64,128]{1,0:T(8,128)S(1)}, f32[64,128]{1,0:T(8,128)}, u32[]{:S(2)}) copy-start(f32[64,128]{1,0:T(8,128)} %param.14) | copy-start | bytes 98308
  55.9 14.7 %all-to-all-start.2 = ((f32[16,32,128]{2,1,0:T(8,128)}), f32[16,32,128]{2,1,0:T(8,128)S(1)}, u32[]{:S(2)}, u32[]{:S(2)}) async-start(f32[16,32,128]{2,1,0:T(8,128)} %broadcast_in_dim.25), calls=%async_computation.2 | async-start | bytes 524288 | tf_op jit(solution)/shard_map/all_to_all | solution.py:45
  85.4 45.9 %copy-start.3 = (f32[64,128]{1,0:T(8,128)}, f32[64,128]{1,0:T(8,128)S(1)}, u32[]{:S(2)}) copy-start(f32[64,128]{1,0:T(8,128)S(1)} %multiply_add_fusion.1) | copy-start | bytes 98308
  131.2 0.7 copy-start.9

commit v4 on v3

--- a/solution.py
+++ b/solution.py
@@ -2,6 +2,7 @@
 import jax.numpy as jnp
 import numpy as np
 from jax import lax
+from jax.experimental import pallas as pl
 from jax.sharding import Mesh, PartitionSpec as P
 
 AXES = ("x", "zl", "y", "zh", "core")
@@ -39,6 +40,11 @@
     return value
 
 
+def rounded_copies(direction_ref, copies_ref):
+    rounded = direction_ref[...].astype(copies_ref.dtype)
+    copies_ref[...] = jnp.broadcast_to(rounded[None], copies_ref.shape)
+
+
 def spread(value, axes):
     n = lax.axis_size(axes)
     copies = jnp.broadcast_to(value[None], (n,) + value.shape)
@@ -60,7 +66,11 @@
     def both(mine, peer):
         return jnp.where(zl == 0, jnp.concatenate([mine, peer]), jnp.concatenate([peer, mine]))
 
-    copies = jnp.broadcast_to(direction.astype(jnp.bfloat16)[None], (n_plane, own, targets))
+    copies = pl.pallas_call(
+        rounded_copies,
+        out_shape=jax.ShapeDtypeStruct((n_plane, own, targets), jnp.bfloat16),
+        cost_estimate=pl.CostEstimate(flops=0, transcendentals=0, bytes_accessed=4 * own * targets + 2 * n_plane * own * targets),
+    )(direction)
     copies, descriptors, resid, row_weight, freqs, phases, direction = lax.optimization_barrier(
         (copies, descriptors, resid, row_weight, freqs, phases, direction)
     )
@@ -82,8 +92,9 @@
     extra = jnp.broadcast_to(penalty[None, None], (n_column, 8, targets))
     rows_weight = jnp.broadcast_to(rows_weight[:, None], rows_resid.shape)
     resid_size = jnp.sum(jnp.abs(rows_weight * rows_resid), axis=0)
-    gathered, feats, rows_resid, rows_weight, extra, resid_size, lower = lax.optimization_barrier(
-        (gathered, feats, rows_resid, rows_weight, extra, resid_size, zl == 0)
+    kind = lax.broadcasted_iota(jnp.int32, (4, targets), 0)
+    gathered, feats, rows_resid, rows_weight, extra, resid_size, lower, kind = lax.optimization_barrier(
+        (gathered, feats, rows_resid, rows_weight, extra, resid_size, zl == 0, kind)
     )
     partial = jnp.dot(feats, gathered, preferred_element_type=jnp.float32)
 
@@ -91,12 +102,8 @@
     came = jnp.sum(lax.all_to_all(sent, COLUMN, 0, 0, tiled=True), axis=0)
     share = came.shape[0] - 8
     image = rows_weight * spread(came[:share], COLUMN).reshape(-1, targets)
-    local = jnp.concatenate([
-        jnp.sum(image * image, axis=0)[None] + came[share : share + 1],
-        resid_size[None],
-        jnp.sum(jnp.abs(rows_weight * image), axis=0)[None],
-        jnp.zeros((1, targets), jnp.float32),
-    ])
+    local = jnp.where(kind == 0, (jnp.sum(image * image, axis=0) + came[share])[None], resid_size[None])
+    local = jnp.where(kind == 2, jnp.sum(jnp.abs(rows_weight * image), axis=0)[None], local)
     seen = spread(local, PLANE)
     alpha = gamma / jnp.sum(seen[:, 0], axis=0)
     bound = jnp.max(seen[:, 1], axis=0) + jnp.abs(alpha) * jnp.max(seen[:, 2], axis=0)
@@ -105,13 +112,14 @@
     rows_new = rows_resid - alpha[None, :] * image
     weighted_b = (rows_weight * rows_new).astype(jnp.bfloat16)
     resid_new = jnp.where(lower, rows_new[:rows_dev], rows_new[rows_dev:])
-    weighted_b, coef_new, resid_new = lax.optimization_barrier((weighted_b, coef_new, resid_new))
+    weighted_b, coef_new = lax.optimization_barrier((weighted_b, coef_new))
 
     terms = lax.dot_general(
         feats, weighted_b, (((0,), (0,)), ((), ())), preferred_element_type=jnp.float32
     )
     terms = (terms * scale[None, :]).astype(jnp.float16)
     terms = lax.all_to_all(terms.reshape(n_plane, own, targets), PLANE, 0, 0, tiled=True)
+    terms, resid_new = lax.optimization_barrier((terms, resid_new))
     summed = jnp.sum(terms.astype(jnp.float32), axis=0) * (1.0 / scale)[None, :]
     gradient = summed - ridge[None, :] * coef_new
     gamma_new = total_of(total_of(jnp.sum(gradient * gradient, axis=0)[None], COLUMN), PLANE)[0]

time: 133 us -> 132 us (level)
  blocking collectives: 85.5 us -> 82.5 us
  waiting for transfers between devices: 14.1 us -> 16.1 us
  local copies, waits for them, and re-layouts: 2.7 us -> 1.01 us
  Pallas kernels: 0 us -> 1.69 us
    all_to_all x1 -> x0, blocking collectives: 17.3 us -> none  [body(): lax.all_to_all(terms.reshape(n_plane, own, targets), PLANE, 0, 0, tiled=T...]
    all_to_all x3 -> x4, blocking collectives: 41.3 us -> 55.6 us  [spread(): return lax.all_to_all(copies, axes, 0, 0, tiled=True)]
    all_to_all x1, waiting for transfers between devices: 11.2 us -> 13.1 us  [body(): lax.all_to_all(terms.reshape(n_plane, own, targets), PLANE, 0, 0, tiled=T...]
    pallas_call x0 -> x1, Pallas kernels: none -> 1.69 us  [body(): pl.pallas_call(rounded_copies, out_shape=jax.ShapeDtypeStruct((n_plane, o...]
  transfers between devices with their start and end apart: 4 -> 4, of which waited for: 2 -> 2; matrix products, arithmetic and copies ran while one was open for 4% -> 5% of each run, Pallas kernels for 0% -> 0%
where the time goes in v4:
time: 132 us; the launch traced here: 131 us
  blocking collectives  82.5 us (62%)
  starting transfers between devices  20.4 us (15%)
  waiting for transfers between devices  16.1 us (12%)
  matrix products  5.65 us (4%)
  other arithmetic  2.87 us (2%)
  Pallas kernels  1.69 us (1%)
    all_to_all x4, blocking collectives, spread(): return lax.all_to_all(copies, axes, 0, 0, tiled=True)  55.6 us
    all_to_all x1, blocking collectives, body(): came = jnp.sum(lax.all_to_all(sent, COLUMN, 0, 0, tiled=True), axis=0)  26.9 us
    all_to_all x1, waiting for transfers between devices, body(): lax.all_to_all(terms.reshape(n_plane, own, targets), PLANE, 0, 0, tiled=T...  13.1 us
    all_to_all x1, starting transfers between devices, body(): lax.all_to_all(copies, PLANE, 0, 0, tiled=True).reshape(-1, targets)  10.6 us
    ppermute x1, starting transfers between devices, body(): rows_x = both(descriptors, lax.ppermute(descriptors, 'zl', swap))  4 us
    all_to_all x1, starting transfers between devices, body(): lax.all_to_all(terms.reshape(n_plane, own, targets), PLANE, 0, 0, tiled=T...  3.89 us
    dot_general x1, matrix products, body(): jnp.dot(rows_x, freq_cols, preferred_element_type=jnp.float32)  3.39 us
    all_to_all x1, waiting for transfers between devices, body(): lax.all_to_all(copies, PLANE, 0, 0, tiled=True).reshape(-1, targets)  2.93 us
  transfers between devices with their start and end apart: 4, of which 2 were waited for; matrix products, arithmetic and copies ran while one was open for 5% of the time, Pallas kernels for 0%

profile of v4, /device:TPU:1, one launch (start us, length us, event | category | flops | bytes accessed | tf_op | source)
XLA Modules:
  0.0 131.3 jit_solution(1608735313110118678)
XLA Ops:
  0.6 0.0 copy-start.1
  0.6 0.0 copy-start
  0.7 0.0 copy-start.5
  0.7 1.7 %shard_map.120 = bf16[32,64,128]{2,1,0:T(8,128)(2,1)} custom-call(f32[64,128]{1,0:T(8,128)} %direction_ref.1), custom_call_target="tpu_custom_call" | custom-call | bytes 557056 | tf_op jit(solution)/shard_map/pallas_call | solution.py:69
  2.4 0.0 copy-start.7
  2.4 0.0 copy-start.10
  2.4 10.6 %all-to-all-start = ((bf16[32,64,128]{2,1,0:T(8,128)(2,1)}), bf16[32,64,128]{2,1,0:T(8,128)(2,1)S(1)}, u32[]{:S(2)}, u32[]{:S(2)}) async-start(bf16[32,64,128]{2,1,0:T(8,128)(2,1)} %shard_map.120), calls=%async_computation | async-start | bytes 1048576 | tf_op jit(solution)/shard_map/all_to_all | solution.py:77
  13.0 4.0 %collective-permute-start = (bf16[256,128]{1,0:T(8,128)(2,1)}, bf16[256,128]{1,0:T(8,128)(2,1)S(1)}, u32[]{:S(2)}, u32[]{:S(2)}) collective-permute-start(bf16[256,128]{1,0:T(8,128)(2,1)} %param.9), channel_id=1, source_target_pairs={{0,64},{64,0},{1,65},{65,1},{2,66},{66,2},{3,67},{67,3},{4,68},{68... | collective-permute-start | bytes 196616 | tf_op jit(solution)/shard_map/ppermute | solution.py:79
  17.0 0.9 pad_maximum_fusion.1
  17.9 1.9 %collective-permute-start.1 = (f32[258,128]{1,0:T(8,128)S(1)}, f32[258,128]{1,0:T(8,128)S(1)}, u32[]{:S(2)}, u32[]{:S(2)}) collective-permute-start(f32[258,128]{1,0:T(8,128)S(1)} %pad_maximum_fusion.1), channel_id=1, source_target_pairs={{0,64},{64,0},{1,65},{65,1},{2,66},{66,2},{3,67},{67,3},{4,68},{68... | collective-permute-start | bytes 396296 | tf_op jit(solution)/shard_map/ppermute | solution.py:81
  19.9 0.0 copy-done
  19.9 0.7 copy.15
  20.6 0.0 copy-done.5
  20.6 0.0 copy-done.1
  20.7 0.0 copy-done.7
  20.7 0.0 collective-permute-done
  20.7 0.0 copy-done.10
  20.7 0.0 copy-start.6
  20.7 0.0 copy-start.2
  20.8 3.4 %add_convert_fusion = bf16[512,2048]{1,0:T(8,128)(2,1)S(1)} fusion(bf16[128,2048]{0,1:T(8,128)(2,1)S(1)} %bitcast.35, f32[2048]{0:T(1024)S(1)} %bitcast.41, bf16[256,128]{1,0:T(8,128)(2,1)S(1)} %collective-permute-done, bf16[256,128]{1,0:T(8,128)(2,1)S(1)} %copy-done.10, pred[]{:T(512)S(6)} %eq.18), kind=kOutput, calls=%fused_computation | convolution fusion | flops 291045376 | bytes 2760705 | tf_op jit(solution)/shard_map/dot_general | solution.py:89
  24.2 0.0 collective-permute-done.1
  24.2 0.0 copy-done.6
  24.2 0.0 copy-done.2
  24.2 0.2 abs_reduce_fusion.1
  24.4 2.9 %all-to-all-done = bf16[32,64,128]{2,1,0:T(8,128)(2,1)S(1)} async-done(((bf16[32,64,128]{2,1,0:T(8,128)(2,1)}), bf16[32,64,128]{2,1,0:T(8,128)(2,1)S(1)}, u32[]{:S(2)}, u32[]{:S(2)}) %all-to-all-start) | async-done | bytes 524320 | tf_op jit(solution)/shard_map/all_to_all | solution.py:77
  27.3 0.1 broadcast_in_dim.38
  27.5 0.7 fusion.10
  28.2 0.0 copy-start.8
  28.2 0.0 copy-start.4
  28.2 26.9 %all_to_all.35 = f32[16,40,128]{2,1,0:T(8,128)S(1)} all-to-all(f32[16,40,128]{2,1,0:T(8,128)S(1)} %pad_maximum_fusion), channel_id=1, replica_groups=mesh['x'=4,'zl'=2,'y'=8,'zh'=4,'core'=2] {'zl','zh','core'}, dimensions={0} | all-to-all | bytes 655360 | tf_op jit(solution)/shard_map/all_to_all | solution.py:102
  55.2 14.4 %all_to_all.36 = f32[16,32,128]{2,1,0:T(8,128)S(1)} all-to-all(f32[16,32,128]{2,1,0:T(8,128)S(1)} %broadcast_in_dim.40), channel_id=1, replica_groups=mesh['x'=4,'zl'=2,'y'=8,'zh'=4,'core'=2] {'zl','zh','core'}, dimensions={0} | all-to-all | bytes 524288 | tf_op jit(solution)/shard_map/all_to_all | solution.py:51
  69.6 0.1 abs_reduce_fusion
  69.7 14.0 %all_to_all.37 = f32[32,4,128]{2,1,0:T(4,128)S(1)} all-to-all(f32[32,4,128]{2,1,0:T(4,128)S(1)} %broadcast_in_dim.45), channel_id=1, replica_groups=mesh['x'=4,'zl'=2,'y'=8,'zh'=4,'core'=2] {'x','y'}, dimensions={0} | all-to-all | bytes 131072 | tf_op jit(solution)/shard_map/all_to_all | solution.py:51
  83.8 0.0 copy-done.8
  83.9 0.0 copy-done.4
  83.9 0.0 copy-start.3
  83.9 0.1 multiply_convert_fusion
  84.0 1.6 %fusion = f16[2048,128]{1,0:T(8,128)(2,1)} fusion(bf16[512,2048]{1,0:T(8,128)(2,1)S(1)} %add_convert_fusion, bf16[512,128]{1,0:T(8,128)(2,1)S(1)} %get-tuple-element.38, f32[128]{0:T(128)S(1)} %broadcast_divide_fusion), kind=kOutput, calls=%fused_computation.2 | convolution fusion | flops 268959744 | bytes 2753024 | tf_op jit(solution)/shard_map/dot_general | solution.py:117
  85.5 3.9 %all-to-all-start.4 = ((f16[32,64,128]{2,1,0:T(8,128)(2,1)}), f16[32,64,128]{2,1,0:T(8,128)(2,1)S(1)}, u32[]{:S(2)}, u32[]{:S(2)}) async-start(f16[32,64,128]{2,1,0:T(8,128)(2,1)} %bitcast.13), calls=%async_computation.4 | async-start | bytes 1048576 | tf_op jit(solution)/shard_map/all_to_all | solution.py:121
  89.4 0.7 slice_select_fusion
  90.1 13.1 %all-to-all-done.4 = f16[32,64,128]{2,1,0:T(8,128)(2,1)S(1)} async-done(((f16[32,64,128]{2,1,0:T(8,128)(2,1)}), f16[32,64,128]{2,1,0:T(8,128)(2,1)S(1)}, u32[]{:S(2)}, u32[]{:S(2)}) %all-to-all-start.4) | async-done | bytes 524320 | tf_op jit(solution)/shard_map/all_to_all | solution.py:121
  103.2 0.1 convert_reduce_fusion
  103.4 13.9 %all_to_all.38 = f32[16,1,128]{2,1,0:T(1,128)S(1)} all-to-all(f32[16,1,128]{2,1,0:T(1,128)S(1)} %broadcast_in_dim.46), channel_id=1, replica_groups=mesh['x'=4,'zl'=2,'y'=8,'zh'=4,'core'=2] {'zl','zh','core'}, dimensions={0} | all-to-all | bytes 16384 | tf_op jit(solution)/shard_map/all_to_all | solution.py:51
  117.3 13.3 %all_to_all.39 = f32[32,1,128]{2,1,0:T(1,128)S(1)} all-to-all(f32[32,1,128]{2,1,0:T(1,128)S(1)} %broadcast_in_dim.47), channel_id=1, replica_groups=mesh['x'=4,'zl'=2,'y'=8,'zh'=4,'core'=2] {'x','y'}, dimensions={0} | all-to-all | bytes 32768 | tf_op jit(solution)/shard_map/all_to_all | solution.py:51
  130.6 0.0 copy-start.9
  130.6 0.0 copy-done.3
  130.6 0.6 multiply_add_fusion
  131.3 0.0 copy-done.9
  (30 shorter events, 0.4 us)
Async XLA Ops:
  0.6 20.0 %copy-start.1 = (f32[64,128]{1,0:T(8,128)S(1)}, f32[64,128]{1,0:T(8,128)}, u32[]{:S(2)}) copy-start(f32[64,128]{1,0:T(8,128)} %direction_ref.1) | copy-start | bytes 98308
  0.6 19.2 %copy-start = (bf16[128,4096]{1,0:T(8,128)(2,1)S(1)}, bf16[128,4096]{1,0:T(8,128)(2,1)}, u32[]{:S(2)}) copy-start(bf16[128,4096]{1,0:T(8,128)(2,1)} %param.10) | copy-start | bytes 3145732
  0.7 19.9 %copy-start.5 = (f32[4096]{0:T(1024)S(1)}, f32[4096]{0:T(1024)}, u32[]{:S(2)}) copy-start(f32[4096]{0:T(1024)} %param.11) | copy-start | bytes 49156
  2.4 18.3 %copy-start.7 = (f32[128]{0:T(128)S(1)}, f32[128]{0:T(128)}, u32[]{:S(2)}) copy-start(f32[128]{0:T(128)} %param.16) | copy-start | bytes 1540
  2.4 18.4 %copy-start.10 = (bf16[256,128]{1,0:T(8,128)(2,1)S(1)}, bf16[256,128]{1,0:T(8,128)(2,1)}, u32[]{:S(2)}) copy-start(bf16[256,128]{1,0:T(8,128)(2,1)} %param.9) | copy-start | bytes 196612
  2.4 25.0 %all-to-all-start = ((bf16[32,64,128]{2,1,0:T(8,128)(2,1)}), bf16[32,64,128]{2,1,0:T(8,128)(2,1)S(1)}, u32[]{:S(2)}, u32[]{:S(2)}) async-start(bf16[32,64,128]{2,1,0:T(8,128)(2,1)} %shard_map.120), calls=%async_computation | async-start | bytes 1048576 | tf_op jit(solution)/shard_map/all_to_all | solution.py:77
  13.0 7.7 %collective-permute-start = (bf16[256,128]{1,0:T(8,128)(2,1)}, bf16[256,128]{1,0:T(8,128)(2,1)S(1)}, u32[]{:S(2)}, u32[]{:S(2)}) collective-permute-start(bf16[256,128]{1,0:T(8,128)(2,1)} %param.9), channel_id=1, source_target_pairs={{0,64},{64,0},{1,65},{65,1},{2,66},{66,2},{3,67},{67,3},{4,68},{68... | collective-permute-start | bytes 196616 | tf_op jit(solution)/shard_map/ppermute | solution.py:79
  17.9 6.2 %collective-permute-start.1 = (f32[258,128]{1,0:T(8,128)S(1)}, f32[258,128]{1,0:T(8,128)S(1)}, u32[]{:S(2)}, u32[]{:S(2)}) collective-permute-start(f32[258,128]{1,0:T(8,128)S(1)} %pad_maximum_fusion.1), channel_id=1, source_target_pairs={{0,64},{64,0},{1,65},{65,1},{2,66},{66,2},{3,67},{67,3},{4,68},{68... | collective-permute-start | bytes 396296 | tf_op jit(solution)/shard_map/ppermute | solution.py:81
  20.7 3.5 %copy-start.6 = (f32[256]{0:T(256)S(1)}, f32[256]{0:T(256)}, u32[]{:S(2)}) copy-start(f32[256]{0:T(256)} %param.12) | copy-start | bytes 3076
  20.7 3.5 %copy-start.2 = (f32[256,128]{1,0:T(8,128)S(1)}, f32[256,128]{1,0:T(8,128)}, u32[]{:S(2)}) copy-start(f32[256,128]{1,0:T(8,128)} %param.13) | copy-start | bytes 393220
  28.2 55.7 %copy-start.8 = (f32[128]{0:T(128)S(1)}, f32[128]{0:T(128)}, u32[]{:S(2)}) copy-start(f32[128]{0:T(128)} %param.17) | copy-start | bytes 1540
  28.2 55.7 %copy-start.4 = (f32[64,128]{1,0:T(8,128)S(1)}, f32[64,128]{1,0:T(8,128)}, u32[]{:S(2)}) copy-start(f32[64,128]{1,0:T(8,128)} %param.14) | copy-start | bytes 98308
  83.9 46.7 %copy-start.3 = (f32[64,128]{1,0:T(8,128)}, f32[64,128]{1,0:T(8,128)S(1)}, u32[]{:S(2)}) copy-start(f32[64,128]{1,0:T(8,128)S(1)} %multiply_add_fusion.1) | copy-start | bytes 98308
  85.5 17.7 %all-to-all-start.4 = ((f16[32,64,128]{2,1,0:T(8,128)(2,1)}), f16[32,64,128]{2,1,0:T(8,128)(2,1)S(1)}, u32[]{:S(2)}, u32[]{:S(2)}) async-start(f16[32,64,128]{2,1,0:T(8,128)(2,1)} %bitcast.13), calls=%async_computation.4 | async-start | bytes 1048576 | tf_op jit(solution)/shard_map/all_to_all | solution.py:121
  130.6 0.7 copy-start.9

commit v5 on v4

--- a/solution.py
+++ b/solution.py
@@ -11,6 +11,11 @@
 FEAT = ("zh", "core")
 PLANE = ("x", "y")
 COLUMN = ("zl", "zh", "core")
+LATE_ZL, LATE_ZH = 1, 2
+
+PLANE_ORDER = [((x + 2) % 4) * 8 + (y + 4) % 8 for x in range(4) for y in range(8)]
+COLUMN_ORDER = [((i // 8 + LATE_ZL) % 2) * 8 + ((i // 2 + LATE_ZH) % 4) * 2 + i % 2 for i in range(16)]
+ORDERS = {PLANE: PLANE_ORDER, COLUMN: COLUMN_ORDER}
 
 SCALE = 2.0**-7
 TURN = 1.0 / (2.0 * np.pi)
@@ -45,14 +50,23 @@
     copies_ref[...] = jnp.broadcast_to(rounded[None], copies_ref.shape)
 
 
+def exchange(blocks, axes):
+    return lax.all_to_all(blocks, axes, 0, 0, axis_index_groups=[ORDERS[axes]], tiled=True)
+
+
 def spread(value, axes):
     n = lax.axis_size(axes)
     copies = jnp.broadcast_to(value[None], (n,) + value.shape)
-    return lax.all_to_all(copies, axes, 0, 0, tiled=True)
+    return exchange(copies, axes)
 
 
 def total_of(row, axes):
     return jnp.sum(spread(row, axes), axis=0)
+
+
+def listed(cols, own):
+    cols = jnp.roll(cols, -2, axis=1)
+    return jnp.roll(cols, -4 * own, axis=2).reshape(cols.shape[0], -1)
 
 
 def body(descriptors, freqs, phases, row_weight, resid, coef, direction, ridge, gamma):
@@ -74,7 +88,7 @@
     copies, descriptors, resid, row_weight, freqs, phases, direction = lax.optimization_barrier(
         (copies, descriptors, resid, row_weight, freqs, phases, direction)
     )
-    gathered = lax.all_to_all(copies, PLANE, 0, 0, tiled=True).reshape(-1, targets)
+    gathered = exchange(copies, PLANE).reshape(-1, targets)
 
     rows_x = both(descriptors, lax.ppermute(descriptors, "zl", swap))
     packed = jnp.concatenate([resid, row_weight.reshape(-1, targets)])
@@ -84,8 +98,9 @@
 
     n_x = lax.axis_size("x")
     freq_cols = freqs.reshape(desc, n_x, 2, -1)
-    freq_cols = lax.dynamic_index_in_dim(freq_cols, zl, 2, keepdims=False).reshape(desc, -1)
-    phase_cols = lax.dynamic_index_in_dim(phases.reshape(n_x, 2, -1), zl, 1, keepdims=False).reshape(-1)
+    freq_cols = listed(lax.dynamic_index_in_dim(freq_cols, zl, 2, keepdims=False), own)
+    phase_cols = lax.dynamic_index_in_dim(phases.reshape(n_x, 2, -1), zl, 1, keepdims=False)
+    phase_cols = listed(phase_cols[None], own)[0]
     angle = jnp.dot(rows_x, freq_cols, preferred_element_type=jnp.float32) + phase_cols[None, :]
     feats = scaled_cos(angle).astype(jnp.bfloat16)
     penalty = ridge * jnp.sum(direction * direction, axis=0)
@@ -99,7 +114,7 @@
     partial = jnp.dot(feats, gathered, preferred_element_type=jnp.float32)
 
     sent = jnp.concatenate([partial.reshape(n_column, -1, targets), extra], axis=1)
-    came = jnp.sum(lax.all_to_all(sent, COLUMN, 0, 0, tiled=True), axis=0)
+    came = jnp.sum(exchange(sent, COLUMN), axis=0)
     share = came.shape[0] - 8
     image = rows_weight * spread(came[:share], COLUMN).reshape(-1, targets)
     local = jnp.where(kind == 0, (jnp.sum(image * image, axis=0) + came[share])[None], resid_size[None])
@@ -118,7 +133,7 @@
         feats, weighted_b, (((0,), (0,)), ((), ())), preferred_element_type=jnp.float32
     )
     terms = (terms * scale[None, :]).astype(jnp.float16)
-    terms = lax.all_to_all(terms.reshape(n_plane, own, targets), PLANE, 0, 0, tiled=True)
+    terms = exchange(terms.reshape(n_plane, own, targets), PLANE)
     terms, resid_new = lax.optimization_barrier((terms, resid_new))
     summed = jnp.sum(terms.astype(jnp.float32), axis=0) * (1.0 / scale)[None, :]
     gradient = summed - ridge[None, :] * coef_new

time: 132 us -> 125 us (0.947)
  blocking collectives: 82.5 us -> 70.5 us
  starting transfers between devices: 20.4 us -> 29 us
  waiting for transfers between devices: 16.1 us -> 10.5 us
    all_to_all x5, blocking collectives: 82.5 us -> 70.5 us  [exchange(): lax.all_to_all(blocks, axes, 0, 0, axis_index_groups=[ORDERS[axes]], tile...]
    all_to_all x2, starting transfers between devices: 14.5 us -> 23 us  [exchange(): lax.all_to_all(blocks, axes, 0, 0, axis_index_groups=[ORDERS[axes]], tile...]
    all_to_all x2, waiting for transfers between devices: 16.1 us -> 10.5 us  [exchange(): lax.all_to_all(blocks, axes, 0, 0, axis_index_groups=[ORDERS[axes]], tile...]
  transfers between devices with their start and end apart: 4 -> 4, of which waited for: 2 -> 1; matrix products, arithmetic and copies ran while one was open for 5% -> 6% of each run, Pallas kernels for 0% -> 0%
where the time goes in v5:
time: 125 us; the launch traced here: 124 us
  blocking collectives  70.5 us (56%)
  starting transfers between devices  29 us (23%)
  waiting for transfers between devices  10.5 us (8%)
  matrix products  6.42 us (5%)
  other arithmetic  2.95 us (2%)
  local copies, waits for them, and re-layouts  1.86 us (1%)
  Pallas kernels  1.7 us (1%)
    all_to_all x5, blocking collectives, exchange(): lax.all_to_all(blocks, axes, 0, 0, axis_index_groups=[ORDERS[axes]], tile...  70.5 us
    all_to_all x2, starting transfers between devices, exchange(): lax.all_to_all(blocks, axes, 0, 0, axis_index_groups=[ORDERS[axes]], tile...  23 us
    all_to_all x2, waiting for transfers between devices, exchange(): lax.all_to_all(blocks, axes, 0, 0, axis_index_groups=[ORDERS[axes]], tile...  10.5 us
    dot_general x1, matrix products, body(): jnp.dot(rows_x, freq_cols, preferred_element_type=jnp.float32)  4.16 us
    ppermute x1, starting transfers between devices, body(): rows_x = both(descriptors, lax.ppermute(descriptors, 'zl', swap))  4 us
  transfers between devices with their start and end apart: 4, of which 1 were waited for; matrix products, arithmetic and copies ran while one was open for 6% of the time, Pallas kernels for 0%

profile of v5, /device:TPU:1, one launch (start us, length us, event | category | flops | bytes accessed | tf_op | source)
XLA Modules:
  0.0 123.9 jit_solution(6045603888523369987)
XLA Ops:
  0.6 0.0 copy-start
  0.6 1.7 %shard_map.120 = bf16[32,64,128]{2,1,0:T(8,128)(2,1)} custom-call(f32[64,128]{1,0:T(8,128)} %direction_ref.1), custom_call_target="tpu_custom_call" | custom-call | bytes 557056 | tf_op jit(solution)/shard_map/pallas_call | solution.py:83
  2.3 12.5 %all-to-all-start = ((bf16[32,64,128]{2,1,0:T(8,128)(2,1)}), bf16[32,64,128]{2,1,0:T(8,128)(2,1)S(1)}, u32[]{:S(2)}, u32[]{:S(2)}) async-start(bf16[32,64,128]{2,1,0:T(8,128)(2,1)} %shard_map.120), calls=%async_computation | async-start | bytes 1048576 | tf_op jit(solution)/shard_map/all_to_all | solution.py:54
  14.8 4.0 %collective-permute-start = (bf16[256,128]{1,0:T(8,128)(2,1)}, bf16[256,128]{1,0:T(8,128)(2,1)}, u32[]{:S(2)}, u32[]{:S(2)}) collective-permute-start(bf16[256,128]{1,0:T(8,128)(2,1)} %param.9), channel_id=1, source_target_pairs={{0,64},{64,0},{1,65},{65,1},{2,66},{66,2},{3,67},{67,3},{4,68},{68... | collective-permute-start | bytes 196616 | tf_op jit(solution)/shard_map/ppermute | solution.py:93
  18.9 0.9 pad_maximum_fusion.2
  19.8 1.9 %collective-permute-start.1 = (f32[258,128]{1,0:T(8,128)S(1)}, f32[258,128]{1,0:T(8,128)S(1)}, u32[]{:S(2)}, u32[]{:S(2)}) collective-permute-start(f32[258,128]{1,0:T(8,128)S(1)} %pad_maximum_fusion.2), channel_id=1, source_target_pairs={{0,64},{64,0},{1,65},{65,1},{2,66},{66,2},{3,67},{67,3},{4,68},{68... | collective-permute-start | bytes 396296 | tf_op jit(solution)/shard_map/ppermute | solution.py:95
  21.7 0.0 copy-done
  21.7 0.7 copy.19
  22.5 0.2 copy.20
  22.7 0.0 copy-start.5
  22.7 0.0 copy-start.1
  22.7 0.0 copy-start.7
  22.7 0.0 copy-start.10
  22.9 0.3 copy.21
  23.1 0.3 copy-done.5
  23.4 0.0 copy-done.1
  23.5 0.0 copy-done.7
  23.5 0.0 collective-permute-done
  23.5 0.0 copy-done.10
  23.6 0.0 copy-start.6
  23.6 0.0 copy-start.2
  23.6 4.2 %add_convert_fusion = bf16[512,2048]{1,0:T(8,128)(2,1)S(1)} fusion(bf16[128,2048]{0,1:T(8,128)(2,1)S(1)} %bitcast.39, f32[2048]{0:T(1024)S(1)} %bitcast.45, bf16[256,128]{1,0:T(8,128)(2,1)} %collective-permute-done, bf16[256,128]{1,0:T(8,128)(2,1)S(1)} %copy-done.10, pred[]{:T(512)S(6)} %eq.18), kind=kOutput, calls=%fused_computation | convolution fusion | flops 291045376 | bytes 2760705 | tf_op jit(solution)/shard_map/dot_general | solution.py:104
  27.7 0.0 collective-permute-done.1
  27.8 0.0 copy-done.6
  27.8 0.0 copy-done.2
  27.8 0.2 abs_reduce_fusion.1
  28.0 0.0 all-to-all-done
  28.0 0.1 broadcast_in_dim.41
  28.1 0.7 fusion.16
  28.9 0.0 copy-start.8
  28.9 0.0 copy-start.4
  28.9 22.3 %all_to_all.35 = f32[16,40,128]{2,1,0:T(8,128)S(1)} all-to-all(f32[16,40,128]{2,1,0:T(8,128)S(1)} %pad_maximum_fusion.1), channel_id=1, replica_groups={{68,69,70,71,64,65,66,67,4,5,6,7,0,1,2,3},{76,77,78,79,72,73,74,75,12,1..., dimensions={0} | all-to-all | bytes 655360 | tf_op jit(solution)/shard_map/all_to_all | solution.py:54
  51.2 13.9 %all_to_all.36 = f32[16,32,128]{2,1,0:T(8,128)S(1)} all-to-all(f32[16,32,128]{2,1,0:T(8,128)S(1)} %broadcast_in_dim.43), channel_id=1, replica_groups={{68,69,70,71,64,65,66,67,4,5,6,7,0,1,2,3},{76,77,78,79,72,73,74,75,12,1..., dimensions={0} | all-to-all | bytes 524288 | tf_op jit(solution)/shard_map/all_to_all | solution.py:54
  65.2 0.1 abs_reduce_fusion
  65.3 11.3 %all_to_all.37 = f32[32,4,128]{2,1,0:T(4,128)S(1)} all-to-all(f32[32,4,128]{2,1,0:T(4,128)S(1)} %broadcast_in_dim.48), channel_id=1, replica_groups={{288,296,304,312,256,264,272,280,416,424,432,440,384,392,400,408,32,40,..., dimensions={0} | all-to-all | bytes 131072 | tf_op jit(solution)/shard_map/all_to_all | solution.py:54
  76.7 0.0 copy-done.8
  76.7 0.0 copy-done.4
  76.8 0.0 copy-start.3
  76.8 0.1 multiply_convert_fusion
  76.8 1.6 %fusion = f16[2048,128]{1,0:T(8,128)(2,1)} fusion(bf16[512,2048]{1,0:T(8,128)(2,1)S(1)} %add_convert_fusion, bf16[512,128]{1,0:T(8,128)(2,1)S(1)} %get-tuple-element.38, f32[128]{0:T(128)S(1)} %broadcast_divide_fusion), kind=kOutput, calls=%fused_computation.2 | convolution fusion | flops 268959744 | bytes 2753024 | tf_op jit(solution)/shard_map/dot_general | solution.py:132
  78.4 10.5 %all-to-all-start.4 = ((f16[32,64,128]{2,1,0:T(8,128)(2,1)}), f16[32,64,128]{2,1,0:T(8,128)(2,1)S(1)}, u32[]{:S(2)}, u32[]{:S(2)}) async-start(f16[32,64,128]{2,1,0:T(8,128)(2,1)} %bitcast.15), calls=%async_computation.4 | async-start | bytes 1048576 | tf_op jit(solution)/shard_map/all_to_all | solution.py:54
  88.9 0.7 slice_select_fusion
  89.6 10.5 %all-to-all-done.4 = f16[32,64,128]{2,1,0:T(8,128)(2,1)S(1)} async-done(((f16[32,64,128]{2,1,0:T(8,128)(2,1)}), f16[32,64,128]{2,1,0:T(8,128)(2,1)S(1)}, u32[]{:S(2)}, u32[]{:S(2)}) %all-to-all-start.4) | async-done | bytes 524320 | tf_op jit(solution)/shard_map/all_to_all | solution.py:54
  100.1 0.1 convert_reduce_fusion
  100.2 11.4 %all_to_all.38 = f32[16,1,128]{2,1,0:T(1,128)S(1)} all-to-all(f32[16,1,128]{2,1,0:T(1,128)S(1)} %broadcast_in_dim.49), channel_id=1, replica_groups={{68,69,70,71,64,65,66,67,4,5,6,7,0,1,2,3},{76,77,78,79,72,73,74,75,12,1..., dimensions={0} | all-to-all | bytes 16384 | tf_op jit(solution)/shard_map/all_to_all | solution.py:54
  111.7 11.5 %all_to_all.39 = f32[32,1,128]{2,1,0:T(1,128)S(1)} all-to-all(f32[32,1,128]{2,1,0:T(1,128)S(1)} %broadcast_in_dim.50), channel_id=1, replica_groups={{288,296,304,312,256,264,272,280,416,424,432,440,384,392,400,408,32,40,..., dimensions={0} | all-to-all | bytes 32768 | tf_op jit(solution)/shard_map/all_to_all | solution.py:54
  123.3 0.0 copy-start.9
  123.3 0.0 copy-done.3
  123.3 0.6 multiply_add_fusion
  123.9 0.0 copy-done.9
  (36 shorter events, 0.6 us)
Async XLA Ops:
  0.6 21.1 %copy-start = (bf16[128,4096]{1,0:T(8,128)(2,1)S(1)}, bf16[128,4096]{1,0:T(8,128)(2,1)}, u32[]{:S(2)}) copy-start(bf16[128,4096]{1,0:T(8,128)(2,1)} %param.10) | copy-start | bytes 3145732
  2.3 25.6 %all-to-all-start = ((bf16[32,64,128]{2,1,0:T(8,128)(2,1)}), bf16[32,64,128]{2,1,0:T(8,128)(2,1)S(1)}, u32[]{:S(2)}, u32[]{:S(2)}) async-start(bf16[32,64,128]{2,1,0:T(8,128)(2,1)} %shard_map.120), calls=%async_computation | async-start | bytes 1048576 | tf_op jit(solution)/shard_map/all_to_all | solution.py:54
  14.8 8.7 %collective-permute-start = (bf16[256,128]{1,0:T(8,128)(2,1)}, bf16[256,128]{1,0:T(8,128)(2,1)}, u32[]{:S(2)}, u32[]{:S(2)}) collective-permute-start(bf16[256,128]{1,0:T(8,128)(2,1)} %param.9), channel_id=1, source_target_pairs={{0,64},{64,0},{1,65},{65,1},{2,66},{66,2},{3,67},{67,3},{4,68},{68... | collective-permute-start | bytes 196616 | tf_op jit(solution)/shard_map/ppermute | solution.py:93
  19.8 8.0 %collective-permute-start.1 = (f32[258,128]{1,0:T(8,128)S(1)}, f32[258,128]{1,0:T(8,128)S(1)}, u32[]{:S(2)}, u32[]{:S(2)}) collective-permute-start(f32[258,128]{1,0:T(8,128)S(1)} %pad_maximum_fusion.2), channel_id=1, source_target_pairs={{0,64},{64,0},{1,65},{65,1},{2,66},{66,2},{3,67},{67,3},{4,68},{68... | collective-permute-start | bytes 396296 | tf_op jit(solution)/shard_map/ppermute | solution.py:95
  22.7 0.7 copy-start.5
  22.7 0.8 copy-start.1
  22.7 0.8 copy-start.7
  22.7 0.9 copy-start.10
  23.6 4.2 %copy-start.6 = (f32[256]{0:T(256)S(1)}, f32[256]{0:T(256)}, u32[]{:S(2)}) copy-start(f32[256]{0:T(256)} %param.12) | copy-start | bytes 3076
  23.6 4.2 %copy-start.2 = (f32[256,128]{1,0:T(8,128)S(1)}, f32[256,128]{1,0:T(8,128)}, u32[]{:S(2)}) copy-start(f32[256,128]{1,0:T(8,128)} %param.13) | copy-start | bytes 393220
  28.9 47.9 %copy-start.8 = (f32[128]{0:T(128)S(1)}, f32[128]{0:T(128)}, u32[]{:S(2)}) copy-start(f32[128]{0:T(128)} %param.17) | copy-start | bytes 1540
  28.9 47.9 %copy-start.4 = (f32[64,128]{1,0:T(8,128)S(1)}, f32[64,128]{1,0:T(8,128)}, u32[]{:S(2)}) copy-start(f32[64,128]{1,0:T(8,128)} %param.14) | copy-start | bytes 98308
  76.8 46.5 %copy-start.3 = (f32[64,128]{1,0:T(8,128)}, f32[64,128]{1,0:T(8,128)S(1)}, u32[]{:S(2)}) copy-start(f32[64,128]{1,0:T(8,128)S(1)} %multiply_add_fusion.1) | copy-start | bytes 98308
  78.4 21.7 %all-to-all-start.4 = ((f16[32,64,128]{2,1,0:T(8,128)(2,1)}), f16[32,64,128]{2,1,0:T(8,128)(2,1)S(1)}, u32[]{:S(2)}, u32[]{:S(2)}) async-start(f16[32,64,128]{2,1,0:T(8,128)(2,1)} %bitcast.15), calls=%async_computation.4 | async-start | bytes 1048576 | tf_op jit(solution)/shard_map/all_to_all | solution.py:54
  123.3 0.7 copy-start.9

commit v6 on v5

--- a/solution.py
+++ b/solution.py
@@ -45,9 +45,13 @@
     return value
 
 
-def rounded_copies(direction_ref, copies_ref):
+def first_sends(direction_ref, descriptors_ref, resid_ref, weight_ref, copies_ref, packed_ref):
     rounded = direction_ref[...].astype(copies_ref.dtype)
     copies_ref[...] = jnp.broadcast_to(rounded[None], copies_ref.shape)
+    n = resid_ref.shape[0]
+    packed_ref[0:n] = descriptors_ref[...].astype(packed_ref.dtype)
+    packed_ref[n : 2 * n] = resid_ref[...]
+    packed_ref[2 * n :] = weight_ref[...]
 
 
 def exchange(blocks, axes):
@@ -80,21 +84,27 @@
     def both(mine, peer):
         return jnp.where(zl == 0, jnp.concatenate([mine, peer]), jnp.concatenate([peer, mine]))
 
-    copies = pl.pallas_call(
-        rounded_copies,
-        out_shape=jax.ShapeDtypeStruct((n_plane, own, targets), jnp.bfloat16),
-        cost_estimate=pl.CostEstimate(flops=0, transcendentals=0, bytes_accessed=4 * own * targets + 2 * n_plane * own * targets),
-    )(direction)
-    copies, descriptors, resid, row_weight, freqs, phases, direction = lax.optimization_barrier(
-        (copies, descriptors, resid, row_weight, freqs, phases, direction)
+    weight_rows = row_weight.reshape(-1, targets)
+    packed_shape = (2 * rows_dev + weight_rows.shape[0], targets)
+    copies, packed = pl.pallas_call(
+        first_sends,
+        out_shape=(
+            jax.ShapeDtypeStruct((n_plane, own, targets), jnp.bfloat16),
+            jax.ShapeDtypeStruct(packed_shape, jnp.float32),
+        ),
+        cost_estimate=pl.CostEstimate(
+            flops=0, transcendentals=0, bytes_accessed=2 * n_plane * own * targets + 8 * packed_shape[0] * targets
+        ),
+    )(direction, descriptors, resid, weight_rows)
+    copies, packed, descriptors, resid, row_weight, freqs, phases, direction = lax.optimization_barrier(
+        (copies, packed, descriptors, resid, row_weight, freqs, phases, direction)
     )
     gathered = exchange(copies, PLANE).reshape(-1, targets)
 
-    rows_x = both(descriptors, lax.ppermute(descriptors, "zl", swap))
-    packed = jnp.concatenate([resid, row_weight.reshape(-1, targets)])
     peer = lax.ppermute(packed, "zl", swap)
-    rows_resid = both(resid, peer[:rows_dev])
-    rows_weight = both(row_weight, peer[rows_dev:].reshape(-1))
+    rows_x = both(descriptors, peer[:rows_dev].astype(jnp.bfloat16))
+    rows_resid = both(resid, peer[rows_dev : 2 * rows_dev])
+    rows_weight = both(row_weight, peer[2 * rows_dev :].reshape(-1))
 
     n_x = lax.axis_size("x")
     freq_cols = freqs.reshape(desc, n_x, 2, -1)

time: 125 us -> 126 us (level)
  starting transfers between devices: 29 us -> 27 us
  blocking collectives: 70.5 us -> 72.2 us
  waiting for transfers between devices: 10.5 us -> 12 us
    ppermute x1 -> x0, starting transfers between devices: 4 us -> none  [body(): rows_x = both(descriptors, lax.ppermute(descriptors, 'zl', swap))]
    ppermute x1, starting transfers between devices: 1.92 us -> 4 us  [body(): peer = lax.ppermute(packed, 'zl', swap)]
    all_to_all x5, blocking collectives: 70.5 us -> 72.2 us  [exchange(): lax.all_to_all(blocks, axes, 0, 0, axis_index_groups=[ORDERS[axes]], tile...]
    ppermute x1, waiting for transfers between devices: 0.01 us -> 1.48 us  [body(): peer = lax.ppermute(packed, 'zl', swap)]
  transfers between devices with their start and end apart: 4 -> 3, of which waited for: 1 -> 2; matrix products, arithmetic and copies ran while one was open for 6% -> 5% of each run, Pallas kernels for 0% -> 0%
where the time goes in v6:
time: 126 us; the launch traced here: 125 us
  blocking collectives  72.2 us (57%)
  starting transfers between devices  27 us (21%)
  waiting for transfers between devices  12 us (10%)
  matrix products  5.65 us (4%)
  local copies, waits for them, and re-layouts  2.82 us (2%)
  other arithmetic  2.02 us (2%)
  Pallas kernels  1.91 us (2%)
    all_to_all x5, blocking collectives, exchange(): lax.all_to_all(blocks, axes, 0, 0, axis_index_groups=[ORDERS[axes]], tile...  72.2 us
    all_to_all x2, starting transfers between devices, exchange(): lax.all_to_all(blocks, axes, 0, 0, axis_index_groups=[ORDERS[axes]], tile...  23 us
    all_to_all x2, waiting for transfers between devices, exchange(): lax.all_to_all(blocks, axes, 0, 0, axis_index_groups=[ORDERS[axes]], tile...  10.5 us
    ppermute x1, starting transfers between devices, body(): peer = lax.ppermute(packed, 'zl', swap)  4 us
    dot_general x1, matrix products, body(): jnp.dot(rows_x, freq_cols, preferred_element_type=jnp.float32)  3.39 us
  transfers between devices with their start and end apart: 3, of which 2 were waited for; matrix products, arithmetic and copies ran while one was open for 5% of the time, Pallas kernels for 0%

profile of v6, /device:TPU:1, one launch (start us, length us, event | category | flops | bytes accessed | tf_op | source)
XLA Modules:
  0.0 124.7 jit_solution(17204301869140683054)
XLA Ops:
  0.6 1.9 %shard_map.120 = (bf16[32,64,128]{2,1,0:T(8,128)(2,1)}, f32[514,128]{1,0:T(8,128)}) custom-call(f32[64,128]{1,0:T(8,128)} %direction_ref.1, bf16[256,128]{1,0:T(8,128)(2,1)} %descriptors_ref.1, f32[256,128]{1,0:T(8,128)} %resid_ref.1, f32[2,128]{1,0:T(2,128)} %bitcast.46), custom_call_target="tpu_custom_call" | custom-call | bytes 1050624 | tf_op jit(solution)/shard_map/pallas_call | solution.py:89
  2.5 12.5 %all-to-all-start = ((bf16[32,64,128]{2,1,0:T(8,128)(2,1)}), bf16[32,64,128]{2,1,0:T(8,128)(2,1)S(1)}, u32[]{:S(2)}, u32[]{:S(2)}) async-start(bf16[32,64,128]{2,1,0:T(8,128)(2,1)} %get-tuple-element.28), calls=%async_computation | async-start | bytes 1048576 | tf_op jit(solution)/shard_map/all_to_all | solution.py:58
  15.1 4.0 %collective-permute-start = (f32[514,128]{1,0:T(8,128)}, f32[514,128]{1,0:T(8,128)S(1)}, u32[]{:S(2)}, u32[]{:S(2)}) collective-permute-start(f32[514,128]{1,0:T(8,128)} %get-tuple-element.30), channel_id=1, source_target_pairs={{0,64},{64,0},{1,65},{65,1},{2,66},{66,2},{3,67},{67,3},{4,68},{68... | collective-permute-start | bytes 789512 | tf_op jit(solution)/shard_map/ppermute | solution.py:104
  19.1 1.6 %copy.19 = bf16[128,4096]{0,1:T(8,128)(2,1)S(1)} copy(bf16[128,4096]{1,0:T(8,128)(2,1)} %param.10) | data formatting | bytes 2097152 | tf_op jit(solution)/shard_map/optimization_barrier | solution.py:99
  20.7 0.0 copy-start.5
  20.8 0.0 copy-start
  20.8 0.2 copy.20
  21.0 0.0 copy-start.7
  21.0 0.0 copy-start.6
  21.1 0.0 copy-start.1
  21.1 0.0 copy-start.3
  21.2 0.3 copy-done.5
  21.5 0.0 copy-done
  21.5 0.3 copy.21
  21.8 0.0 copy-done.7
  21.9 1.5 %collective-permute-done = f32[514,128]{1,0:T(8,128)S(1)} collective-permute-done((f32[514,128]{1,0:T(8,128)}, f32[514,128]{1,0:T(8,128)S(1)}, u32[]{:S(2)}, u32[]{:S(2)}) %collective-permute-start) | collective-permute-done | bytes 263200 | tf_op jit(solution)/shard_map/ppermute | solution.py:104
  23.4 0.0 copy-done.6
  23.4 0.0 copy-done.1
  23.4 0.2 abs_reduce_fusion.1
  23.6 0.0 copy-done.3
  23.6 3.4 %add_convert_fusion = bf16[512,2048]{1,0:T(8,128)(2,1)S(1)} fusion(bf16[128,2048]{0,1:T(8,128)(2,1)S(1)} %bitcast.39, f32[2048]{0:T(1024)S(1)} %bitcast.45, bf16[256,128]{1,0:T(8,128)(2,1)S(1)} %slice.118, bf16[256,128]{1,0:T(8,128)(2,1)S(1)} %copy-done.3, pred[]{:T(512)S(6)} %eq.18), kind=kOutput, calls=%fused_computation | convolution fusion | flops 291045376 | bytes 2760705 | tf_op jit(solution)/shard_map/dot_general | solution.py:114
  27.0 0.0 all-to-all-done
  27.0 0.1 broadcast_in_dim.41
  27.1 0.7 fusion.16
  27.9 0.0 copy-start.8
  27.9 0.0 copy-start.4
  27.9 24.0 %all_to_all.35 = f32[16,40,128]{2,1,0:T(8,128)S(1)} all-to-all(f32[16,40,128]{2,1,0:T(8,128)S(1)} %pad_maximum_fusion.1), channel_id=1, replica_groups={{68,69,70,71,64,65,66,67,4,5,6,7,0,1,2,3},{76,77,78,79,72,73,74,75,12,1..., dimensions={0} | all-to-all | bytes 655360 | tf_op jit(solution)/shard_map/all_to_all | solution.py:58
  52.0 13.9 %all_to_all.36 = f32[16,32,128]{2,1,0:T(8,128)S(1)} all-to-all(f32[16,32,128]{2,1,0:T(8,128)S(1)} %broadcast_in_dim.43), channel_id=1, replica_groups={{68,69,70,71,64,65,66,67,4,5,6,7,0,1,2,3},{76,77,78,79,72,73,74,75,12,1..., dimensions={0} | all-to-all | bytes 524288 | tf_op jit(solution)/shard_map/all_to_all | solution.py:58
  65.9 0.1 abs_reduce_fusion
  66.0 11.3 %all_to_all.37 = f32[32,4,128]{2,1,0:T(4,128)S(1)} all-to-all(f32[32,4,128]{2,1,0:T(4,128)S(1)} %broadcast_in_dim.48), channel_id=1, replica_groups={{288,296,304,312,256,264,272,280,416,424,432,440,384,392,400,408,32,40,..., dimensions={0} | all-to-all | bytes 131072 | tf_op jit(solution)/shard_map/all_to_all | solution.py:58
  77.5 0.0 copy-done.8
  77.5 0.0 copy-done.4
  77.5 0.0 copy-start.2
  77.5 0.1 multiply_convert_fusion
  77.6 1.6 %fusion = f16[2048,128]{1,0:T(8,128)(2,1)} fusion(bf16[512,2048]{1,0:T(8,128)(2,1)S(1)} %add_convert_fusion, bf16[512,128]{1,0:T(8,128)(2,1)S(1)} %get-tuple-element.44, f32[128]{0:T(128)S(1)} %broadcast_divide_fusion), kind=kOutput, calls=%fused_computation.2 | convolution fusion | flops 268959744 | bytes 2753024 | tf_op jit(solution)/shard_map/dot_general | solution.py:142
  79.1 10.5 %all-to-all-start.4 = ((f16[32,64,128]{2,1,0:T(8,128)(2,1)}), f16[32,64,128]{2,1,0:T(8,128)(2,1)S(1)}, u32[]{:S(2)}, u32[]{:S(2)}) async-start(f16[32,64,128]{2,1,0:T(8,128)(2,1)} %bitcast.15), calls=%async_computation.4 | async-start | bytes 1048576 | tf_op jit(solution)/shard_map/all_to_all | solution.py:58
  89.7 0.7 slice_select_fusion
  90.3 10.5 %all-to-all-done.4 = f16[32,64,128]{2,1,0:T(8,128)(2,1)S(1)} async-done(((f16[32,64,128]{2,1,0:T(8,128)(2,1)}), f16[32,64,128]{2,1,0:T(8,128)(2,1)S(1)}, u32[]{:S(2)}, u32[]{:S(2)}) %all-to-all-start.4) | async-done | bytes 524320 | tf_op jit(solution)/shard_map/all_to_all | solution.py:58
  100.9 0.1 convert_reduce_fusion
  101.0 11.4 %all_to_all.38 = f32[16,1,128]{2,1,0:T(1,128)S(1)} all-to-all(f32[16,1,128]{2,1,0:T(1,128)S(1)} %broadcast_in_dim.49), channel_id=1, replica_groups={{68,69,70,71,64,65,66,67,4,5,6,7,0,1,2,3},{76,77,78,79,72,73,74,75,12,1..., dimensions={0} | all-to-all | bytes 16384 | tf_op jit(solution)/shard_map/all_to_all | solution.py:58
  112.5 11.5 %all_to_all.39 = f32[32,1,128]{2,1,0:T(1,128)S(1)} all-to-all(f32[32,1,128]{2,1,0:T(1,128)S(1)} %broadcast_in_dim.50), channel_id=1, replica_groups={{288,296,304,312,256,264,272,280,416,424,432,440,384,392,400,408,32,40,..., dimensions={0} | all-to-all | bytes 32768 | tf_op jit(solution)/shard_map/all_to_all | solution.py:58
  124.0 0.0 copy-start.9
  124.0 0.0 copy-done.2
  124.0 0.6 multiply_add_fusion
  124.7 0.0 copy-done.9
  (37 shorter events, 0.6 us)
Async XLA Ops:
  2.5 24.4 %all-to-all-start = ((bf16[32,64,128]{2,1,0:T(8,128)(2,1)}), bf16[32,64,128]{2,1,0:T(8,128)(2,1)S(1)}, u32[]{:S(2)}, u32[]{:S(2)}) async-start(bf16[32,64,128]{2,1,0:T(8,128)(2,1)} %get-tuple-element.28), calls=%async_computation | async-start | bytes 1048576 | tf_op jit(solution)/shard_map/all_to_all | solution.py:58
  15.1 8.3 %collective-permute-start = (f32[514,128]{1,0:T(8,128)}, f32[514,128]{1,0:T(8,128)S(1)}, u32[]{:S(2)}, u32[]{:S(2)}) collective-permute-start(f32[514,128]{1,0:T(8,128)} %get-tuple-element.30), channel_id=1, source_target_pairs={{0,64},{64,0},{1,65},{65,1},{2,66},{66,2},{3,67},{67,3},{4,68},{68... | collective-permute-start | bytes 789512 | tf_op jit(solution)/shard_map/ppermute | solution.py:104
  20.7 0.7 copy-start.5
  20.8 0.8 copy-start
  21.0 0.8 copy-start.7
  21.0 2.3 %copy-start.6 = (f32[256]{0:T(256)S(1)}, f32[256]{0:T(256)}, u32[]{:S(2)}) copy-start(f32[256]{0:T(256)} %param.12) | copy-start | bytes 3076
  21.1 2.4 %copy-start.1 = (f32[256,128]{1,0:T(8,128)S(1)}, f32[256,128]{1,0:T(8,128)}, u32[]{:S(2)}) copy-start(f32[256,128]{1,0:T(8,128)} %resid_ref.1) | copy-start | bytes 393220
  21.1 2.5 %copy-start.3 = (bf16[256,128]{1,0:T(8,128)(2,1)S(1)}, bf16[256,128]{1,0:T(8,128)(2,1)}, u32[]{:S(2)}) copy-start(bf16[256,128]{1,0:T(8,128)(2,1)} %descriptors_ref.1) | copy-start | bytes 196612
  27.9 49.6 %copy-start.8 = (f32[128]{0:T(128)S(1)}, f32[128]{0:T(128)}, u32[]{:S(2)}) copy-start(f32[128]{0:T(128)} %param.17) | copy-start | bytes 1540
  27.9 49.6 %copy-start.4 = (f32[64,128]{1,0:T(8,128)S(1)}, f32[64,128]{1,0:T(8,128)}, u32[]{:S(2)}) copy-start(f32[64,128]{1,0:T(8,128)} %param.14) | copy-start | bytes 98308
  77.5 46.5 %copy-start.2 = (f32[64,128]{1,0:T(8,128)}, f32[64,128]{1,0:T(8,128)S(1)}, u32[]{:S(2)}) copy-start(f32[64,128]{1,0:T(8,128)S(1)} %multiply_add_fusion.1) | copy-start | bytes 98308
  79.1 21.7 %all-to-all-start.4 = ((f16[32,64,128]{2,1,0:T(8,128)(2,1)}), f16[32,64,128]{2,1,0:T(8,128)(2,1)S(1)}, u32[]{:S(2)}, u32[]{:S(2)}) async-start(f16[32,64,128]{2,1,0:T(8,128)(2,1)} %bitcast.15), calls=%async_computation.4 | async-start | bytes 1048576 | tf_op jit(solution)/shard_map/all_to_all | solution.py:58
  124.0 0.7 copy-start.9

commit v7 on v5

--- a/solution.py
+++ b/solution.py
@@ -93,7 +93,7 @@
     rows_x = both(descriptors, lax.ppermute(descriptors, "zl", swap))
     packed = jnp.concatenate([resid, row_weight.reshape(-1, targets)])
     peer = lax.ppermute(packed, "zl", swap)
-    rows_resid = both(resid, peer[:rows_dev])
+    own_resid, peer_resid = resid, peer[:rows_dev]
     rows_weight = both(row_weight, peer[rows_dev:].reshape(-1))
 
     n_x = lax.axis_size("x")
@@ -105,11 +105,11 @@
     feats = scaled_cos(angle).astype(jnp.bfloat16)
     penalty = ridge * jnp.sum(direction * direction, axis=0)
     extra = jnp.broadcast_to(penalty[None, None], (n_column, 8, targets))
-    rows_weight = jnp.broadcast_to(rows_weight[:, None], rows_resid.shape)
-    resid_size = jnp.sum(jnp.abs(rows_weight * rows_resid), axis=0)
+    rows_weight = jnp.broadcast_to(rows_weight[:, None], (2 * rows_dev, targets))
+    resid_size = jnp.sum(jnp.abs(rows_weight * both(own_resid, peer_resid)), axis=0)
     kind = lax.broadcasted_iota(jnp.int32, (4, targets), 0)
-    gathered, feats, rows_resid, rows_weight, extra, resid_size, lower, kind = lax.optimization_barrier(
-        (gathered, feats, rows_resid, rows_weight, extra, resid_size, zl == 0, kind)
+    gathered, feats, own_resid, peer_resid, rows_weight, extra, resid_size, lower, kind = lax.optimization_barrier(
+        (gathered, feats, own_resid, peer_resid, rows_weight, extra, resid_size, zl == 0, kind)
     )
     partial = jnp.dot(feats, gathered, preferred_element_type=jnp.float32)
 
@@ -124,17 +124,19 @@
     bound = jnp.max(seen[:, 1], axis=0) + jnp.abs(alpha) * jnp.max(seen[:, 2], axis=0)
     scale = TERM_MAX / jnp.maximum(SCALE * bound, TINY)
     coef_new = coef + alpha[None, :] * direction
-    rows_new = rows_resid - alpha[None, :] * image
+    own_image = jnp.where(lower, image[:rows_dev], image[rows_dev:])
+    peer_image = jnp.where(lower, image[rows_dev:], image[:rows_dev])
+    resid_new = lax.optimization_barrier(own_resid - alpha[None, :] * own_image)
+    peer_new = peer_resid - alpha[None, :] * peer_image
+    rows_new = jnp.where(lower, jnp.concatenate([resid_new, peer_new]), jnp.concatenate([peer_new, resid_new]))
     weighted_b = (rows_weight * rows_new).astype(jnp.bfloat16)
-    resid_new = jnp.where(lower, rows_new[:rows_dev], rows_new[rows_dev:])
-    weighted_b, coef_new = lax.optimization_barrier((weighted_b, coef_new))
+    weighted_b, coef_new, resid_new = lax.optimization_barrier((weighted_b, coef_new, resid_new))
 
     terms = lax.dot_general(
         feats, weighted_b, (((0,), (0,)), ((), ())), preferred_element_type=jnp.float32
     )
     terms = (terms * scale[None, :]).astype(jnp.float16)
     terms = exchange(terms.reshape(n_plane, own, targets), PLANE)
-    terms, resid_new = lax.optimization_barrier((terms, resid_new))
     summed = jnp.sum(terms.astype(jnp.float32), axis=0) * (1.0 / scale)[None, :]
     gradient = summed - ridge[None, :] * coef_new
     gamma_new = total_of(total_of(jnp.sum(gradient * gradient, axis=0)[None], COLUMN), PLANE)[0]

time: 125 us -> 125 us (level)
  blocking collectives: 70.5 us -> 91.4 us
  starting transfers between devices: 29 us -> 18.4 us
  waiting for transfers between devices: 10.5 us -> 0.01 us
  local copies, waits for them, and re-layouts: 1.86 us -> 3.43 us
    all_to_all x5 -> x6, blocking collectives: 70.5 us -> 91.4 us  [exchange(): lax.all_to_all(blocks, axes, 0, 0, axis_index_groups=[ORDERS[axes]], tile...]
    all_to_all x2 -> x1, starting transfers between devices: 23 us -> 12.5 us  [exchange(): lax.all_to_all(blocks, axes, 0, 0, axis_index_groups=[ORDERS[axes]], tile...]
    all_to_all x2 -> x1, waiting for transfers between devices: 10.5 us -> 0.01 us  [exchange(): lax.all_to_all(blocks, axes, 0, 0, axis_index_groups=[ORDERS[axes]], tile...]
  transfers between devices with their start and end apart: 4 -> 3, of which waited for: 1 -> 0; matrix products, arithmetic and copies ran while one was open for 6% -> 7% of each run, Pallas kernels for 0% -> 0%
where the time goes in v7:
time: 125 us; the launch traced here: 124 us
  blocking collectives  91.4 us (73%)
  starting transfers between devices  18.4 us (15%)
  matrix products  5.62 us (4%)
  local copies, waits for them, and re-layouts  3.43 us (3%)
  other arithmetic  2.3 us (2%)
  Pallas kernels  1.7 us (1%)
    all_to_all x6, blocking collectives, exchange(): lax.all_to_all(blocks, axes, 0, 0, axis_index_groups=[ORDERS[axes]], tile...  91.4 us
    all_to_all x1, starting transfers between devices, exchange(): lax.all_to_all(blocks, axes, 0, 0, axis_index_groups=[ORDERS[axes]], tile...  12.5 us
    dot_general x1, matrix products, body(): jnp.dot(rows_x, freq_cols, preferred_element_type=jnp.float32)  4.16 us
    ppermute x1, starting transfers between devices, body(): rows_x = both(descriptors, lax.ppermute(descriptors, 'zl', swap))  4 us
  transfers between devices with their start and end apart: 3, of which 0 were waited for; matrix products, arithmetic and copies ran while one was open for 7% of the time, Pallas kernels for 0%

profile of v7, /device:TPU:1, one launch (start us, length us, event | category | flops | bytes accessed | tf_op | source)
XLA Modules:
  0.0 123.9 jit_solution(6140117198583642492)
XLA Ops:
  0.6 0.0 copy-start.1
  0.6 1.7 %shard_map.120 = bf16[32,64,128]{2,1,0:T(8,128)(2,1)} custom-call(f32[64,128]{1,0:T(8,128)} %direction_ref.1), custom_call_target="tpu_custom_call" | custom-call | bytes 557056 | tf_op jit(solution)/shard_map/pallas_call | solution.py:83
  2.3 12.5 %all-to-all-start = ((bf16[32,64,128]{2,1,0:T(8,128)(2,1)}), bf16[32,64,128]{2,1,0:T(8,128)(2,1)S(1)}, u32[]{:S(2)}, u32[]{:S(2)}) async-start(bf16[32,64,128]{2,1,0:T(8,128)(2,1)} %shard_map.120), calls=%async_computation | async-start | bytes 1048576 | tf_op jit(solution)/shard_map/all_to_all | solution.py:54
  14.8 4.0 %collective-permute-start = (bf16[256,128]{1,0:T(8,128)(2,1)}, bf16[256,128]{1,0:T(8,128)(2,1)}, u32[]{:S(2)}, u32[]{:S(2)}) collective-permute-start(bf16[256,128]{1,0:T(8,128)(2,1)} %param.9), channel_id=1, source_target_pairs={{0,64},{64,0},{1,65},{65,1},{2,66},{66,2},{3,67},{67,3},{4,68},{68... | collective-permute-start | bytes 196616 | tf_op jit(solution)/shard_map/ppermute | solution.py:93
  18.9 0.9 pad_maximum_fusion.2
  19.8 1.9 %collective-permute-start.1 = (f32[258,128]{1,0:T(8,128)S(1)}, f32[258,128]{1,0:T(8,128)}, u32[]{:S(2)}, u32[]{:S(2)}) collective-permute-start(f32[258,128]{1,0:T(8,128)S(1)} %pad_maximum_fusion.2), channel_id=1, source_target_pairs={{0,64},{64,0},{1,65},{65,1},{2,66},{66,2},{3,67},{67,3},{4,68},{68... | collective-permute-start | bytes 396296 | tf_op jit(solution)/shard_map/ppermute | solution.py:95
  21.7 0.0 copy-done.1
  21.7 0.7 copy.19
  22.5 0.2 copy.20
  22.7 0.0 copy-start.6
  22.7 0.0 copy-start.2
  22.7 0.0 copy-start.8
  22.7 0.0 copy-start.11
  22.9 0.3 copy.21
  23.1 0.3 copy-done.6
  23.4 0.0 copy-done.2
  23.5 0.0 copy-done.8
  23.5 0.0 collective-permute-done
  23.5 0.0 copy-done.11
  23.6 0.0 copy-start.7
  23.6 0.0 copy-start
  23.6 4.2 %add_convert_fusion = bf16[512,2048]{1,0:T(8,128)(2,1)S(1)} fusion(bf16[128,2048]{0,1:T(8,128)(2,1)S(1)} %bitcast.34, f32[2048]{0:T(1024)S(1)} %bitcast.40, bf16[256,128]{1,0:T(8,128)(2,1)} %collective-permute-done, bf16[256,128]{1,0:T(8,128)(2,1)S(1)} %copy-done.11, pred[]{:T(512)S(6)} %eq.18), kind=kOutput, calls=%fused_computation | convolution fusion | flops 291045376 | bytes 2760705 | tf_op jit(solution)/shard_map/dot_general | solution.py:104
  27.7 0.0 collective-permute-done.1
  27.8 0.9 slice.86
  28.7 0.7 slice_bitcast_fusion
  29.3 0.0 copy-done.7
  29.4 0.0 copy-done
  29.4 0.2 fusion.5
  29.5 0.0 all-to-all-done
  29.5 0.1 broadcast_in_dim.41
  29.7 0.7 fusion.21
  30.4 0.0 copy-start.9
  30.4 0.0 copy-start.5
  30.4 22.3 %all_to_all.35 = f32[16,40,128]{2,1,0:T(8,128)S(1)} all-to-all(f32[16,40,128]{2,1,0:T(8,128)S(1)} %pad_maximum_fusion.1), channel_id=1, replica_groups={{68,69,70,71,64,65,66,67,4,5,6,7,0,1,2,3},{76,77,78,79,72,73,74,75,12,1..., dimensions={0} | all-to-all | bytes 655360 | tf_op jit(solution)/shard_map/all_to_all | solution.py:54
  52.8 13.9 %all_to_all.36 = f32[16,32,128]{2,1,0:T(8,128)S(1)} all-to-all(f32[16,32,128]{2,1,0:T(8,128)S(1)} %broadcast_in_dim.43), channel_id=1, replica_groups={{68,69,70,71,64,65,66,67,4,5,6,7,0,1,2,3},{76,77,78,79,72,73,74,75,12,1..., dimensions={0} | all-to-all | bytes 524288 | tf_op jit(solution)/shard_map/all_to_all | solution.py:54
  66.7 0.1 abs_reduce_fusion
  66.8 11.3 %all_to_all.37 = f32[32,4,128]{2,1,0:T(4,128)S(1)} all-to-all(f32[32,4,128]{2,1,0:T(4,128)S(1)} %broadcast_in_dim.48), channel_id=1, replica_groups={{288,296,304,312,256,264,272,280,416,424,432,440,384,392,400,408,32,40,..., dimensions={0} | all-to-all | bytes 131072 | tf_op jit(solution)/shard_map/all_to_all | solution.py:54
  78.2 0.0 copy-done.9
  78.3 0.0 copy-start.3
  78.3 0.0 copy-done.5
  78.3 0.0 copy-start.4
  78.4 0.8 fusion
  79.2 0.0 copy-done.3
  79.2 20.9 %all_to_all.38 = f16[32,64,128]{2,1,0:T(8,128)(2,1)S(1)} all-to-all(f16[32,64,128]{2,1,0:T(8,128)(2,1)S(1)} %bitcast.29), channel_id=1, replica_groups={{288,296,304,312,256,264,272,280,416,424,432,440,384,392,400,408,32,40,..., dimensions={0} | all-to-all | bytes 1048576 | tf_op jit(solution)/shard_map/all_to_all | solution.py:54
  100.1 0.1 convert_reduce_fusion
  100.2 11.3 %all_to_all.39 = f32[16,1,128]{2,1,0:T(1,128)S(1)} all-to-all(f32[16,1,128]{2,1,0:T(1,128)S(1)} %broadcast_in_dim.49), channel_id=1, replica_groups={{68,69,70,71,64,65,66,67,4,5,6,7,0,1,2,3},{76,77,78,79,72,73,74,75,12,1..., dimensions={0} | all-to-all | bytes 16384 | tf_op jit(solution)/shard_map/all_to_all | solution.py:54
  111.5 11.8 %all_to_all.40 = f32[32,1,128]{2,1,0:T(1,128)S(1)} all-to-all(f32[32,1,128]{2,1,0:T(1,128)S(1)} %broadcast_in_dim.50), channel_id=1, replica_groups={{288,296,304,312,256,264,272,280,416,424,432,440,384,392,400,408,32,40,..., dimensions={0} | all-to-all | bytes 32768 | tf_op jit(solution)/shard_map/all_to_all | solution.py:54
  123.3 0.0 copy-start.10
  123.3 0.0 copy-done.4
  123.3 0.6 multiply_add_fusion
  123.9 0.0 copy-done.10
  (36 shorter events, 0.6 us)
Async XLA Ops:
  0.6 21.1 %copy-start.1 = (bf16[128,4096]{1,0:T(8,128)(2,1)S(1)}, bf16[128,4096]{1,0:T(8,128)(2,1)}, u32[]{:S(2)}) copy-start(bf16[128,4096]{1,0:T(8,128)(2,1)} %param.10) | copy-start | bytes 3145732
  2.3 27.2 %all-to-all-start = ((bf16[32,64,128]{2,1,0:T(8,128)(2,1)}), bf16[32,64,128]{2,1,0:T(8,128)(2,1)S(1)}, u32[]{:S(2)}, u32[]{:S(2)}) async-start(bf16[32,64,128]{2,1,0:T(8,128)(2,1)} %shard_map.120), calls=%async_computation | async-start | bytes 1048576 | tf_op jit(solution)/shard_map/all_to_all | solution.py:54
  14.8 8.7 %collective-permute-start = (bf16[256,128]{1,0:T(8,128)(2,1)}, bf16[256,128]{1,0:T(8,128)(2,1)}, u32[]{:S(2)}, u32[]{:S(2)}) collective-permute-start(bf16[256,128]{1,0:T(8,128)(2,1)} %param.9), channel_id=1, source_target_pairs={{0,64},{64,0},{1,65},{65,1},{2,66},{66,2},{3,67},{67,3},{4,68},{68... | collective-permute-start | bytes 196616 | tf_op jit(solution)/shard_map/ppermute | solution.py:93
  19.8 8.0 %collective-permute-start.1 = (f32[258,128]{1,0:T(8,128)S(1)}, f32[258,128]{1,0:T(8,128)}, u32[]{:S(2)}, u32[]{:S(2)}) collective-permute-start(f32[258,128]{1,0:T(8,128)S(1)} %pad_maximum_fusion.2), channel_id=1, source_target_pairs={{0,64},{64,0},{1,65},{65,1},{2,66},{66,2},{3,67},{67,3},{4,68},{68... | collective-permute-start | bytes 396296 | tf_op jit(solution)/shard_map/ppermute | solution.py:95
  22.7 0.7 copy-start.6
  22.7 0.8 copy-start.2
  22.7 0.8 copy-start.8
  22.7 0.9 copy-start.11
  23.6 5.8 %copy-start.7 = (f32[256]{0:T(256)S(1)}, f32[256]{0:T(256)}, u32[]{:S(2)}) copy-start(f32[256]{0:T(256)} %param.12) | copy-start | bytes 3076
  23.6 5.8 %copy-start = (f32[256,128]{1,0:T(8,128)S(1)}, f32[256,128]{1,0:T(8,128)}, u32[]{:S(2)}) copy-start(f32[256,128]{1,0:T(8,128)} %param.13) | copy-start | bytes 393220
  30.4 47.9 %copy-start.9 = (f32[128]{0:T(128)S(1)}, f32[128]{0:T(128)}, u32[]{:S(2)}) copy-start(f32[128]{0:T(128)} %param.17) | copy-start | bytes 1540
  30.4 47.9 %copy-start.5 = (f32[64,128]{1,0:T(8,128)S(1)}, f32[64,128]{1,0:T(8,128)}, u32[]{:S(2)}) copy-start(f32[64,128]{1,0:T(8,128)} %param.14) | copy-start | bytes 98308
  78.3 0.9 copy-start.3
  78.3 44.9 %copy-start.4 = (f32[64,128]{1,0:T(8,128)}, f32[64,128]{1,0:T(8,128)S(1)}, u32[]{:S(2)}) copy-start(f32[64,128]{1,0:T(8,128)S(1)} %multiply_add_fusion.1) | copy-start | bytes 98308
  123.3 0.7 copy-start.10

commit v8 on v6

--- a/solution.py
+++ b/solution.py
@@ -78,11 +78,12 @@
     targets = resid.shape[1]
     own = direction.shape[0]
     zl = lax.axis_index("zl")
+    lower = zl == 0
     swap = [(0, 1), (1, 0)]
     n_plane, n_column = lax.axis_size(PLANE), lax.axis_size(COLUMN)
 
-    def both(mine, peer):
-        return jnp.where(zl == 0, jnp.concatenate([mine, peer]), jnp.concatenate([peer, mine]))
+    def halves(first, second):
+        return jnp.where(lower, first, second), jnp.where(lower, second, first)
 
     weight_rows = row_weight.reshape(-1, targets)
     packed_shape = (2 * rows_dev + weight_rows.shape[0], targets)
@@ -102,49 +103,64 @@
     gathered = exchange(copies, PLANE).reshape(-1, targets)
 
     peer = lax.ppermute(packed, "zl", swap)
-    rows_x = both(descriptors, peer[:rows_dev].astype(jnp.bfloat16))
-    rows_resid = both(resid, peer[rows_dev : 2 * rows_dev])
-    rows_weight = both(row_weight, peer[2 * rows_dev :].reshape(-1))
+    peer_x = peer[:rows_dev].astype(jnp.bfloat16)
+    peer_resid = peer[rows_dev : 2 * rows_dev]
 
     n_x = lax.axis_size("x")
     freq_cols = freqs.reshape(desc, n_x, 2, -1)
     freq_cols = listed(lax.dynamic_index_in_dim(freq_cols, zl, 2, keepdims=False), own)
     phase_cols = lax.dynamic_index_in_dim(phases.reshape(n_x, 2, -1), zl, 1, keepdims=False)
     phase_cols = listed(phase_cols[None], own)[0]
-    angle = jnp.dot(rows_x, freq_cols, preferred_element_type=jnp.float32) + phase_cols[None, :]
-    feats = scaled_cos(angle).astype(jnp.bfloat16)
+
+    def features(block_x):
+        angle = jnp.dot(block_x, freq_cols, preferred_element_type=jnp.float32) + phase_cols[None, :]
+        return scaled_cos(angle).astype(jnp.bfloat16)
+
+    own_feats = features(descriptors)
+    peer_feats = features(peer_x)
     penalty = ridge * jnp.sum(direction * direction, axis=0)
     extra = jnp.broadcast_to(penalty[None, None], (n_column, 8, targets))
-    rows_weight = jnp.broadcast_to(rows_weight[:, None], rows_resid.shape)
-    resid_size = jnp.sum(jnp.abs(rows_weight * rows_resid), axis=0)
+    own_weight = jnp.broadcast_to(row_weight[:, None], resid.shape)
+    peer_weight = jnp.broadcast_to(peer[2 * rows_dev :].reshape(-1)[:, None], resid.shape)
+    resid_size = jnp.sum(jnp.abs(own_weight * resid), axis=0) + jnp.sum(jnp.abs(peer_weight * peer_resid), axis=0)
     kind = lax.broadcasted_iota(jnp.int32, (4, targets), 0)
-    gathered, feats, rows_resid, rows_weight, extra, resid_size, lower, kind = lax.optimization_barrier(
-        (gathered, feats, rows_resid, rows_weight, extra, resid_size, zl == 0, kind)
+    (gathered, own_feats, peer_feats, own_resid, peer_resid, own_weight, peer_weight, extra, resid_size, lower, kind) = (
+        lax.optimization_barrier(
+            (gathered, own_feats, peer_feats, resid, peer_resid, own_weight, peer_weight, extra, resid_size, lower, kind)
+        )
     )
-    partial = jnp.dot(feats, gathered, preferred_element_type=jnp.float32)
+    partial = halves(
+        jnp.dot(own_feats, gathered, preferred_element_type=jnp.float32),
+        jnp.dot(peer_feats, gathered, preferred_element_type=jnp.float32),
+    )
+    partial = jnp.concatenate(partial)
 
     sent = jnp.concatenate([partial.reshape(n_column, -1, targets), extra], axis=1)
     came = jnp.sum(exchange(sent, COLUMN), axis=0)
     share = came.shape[0] - 8
-    image = rows_weight * spread(came[:share], COLUMN).reshape(-1, targets)
-    local = jnp.where(kind == 0, (jnp.sum(image * image, axis=0) + came[share])[None], resid_size[None])
-    local = jnp.where(kind == 2, jnp.sum(jnp.abs(rows_weight * image), axis=0)[None], local)
+    rows = spread(came[:share], COLUMN).reshape(-1, targets)
+    own_image, peer_image = halves(rows[:rows_dev], rows[rows_dev:])
+    own_image, peer_image = own_weight * own_image, peer_weight * peer_image
+    squares = jnp.sum(own_image * own_image + peer_image * peer_image, axis=0)
+    image_size = jnp.sum(jnp.abs(own_weight * own_image) + jnp.abs(peer_weight * peer_image), axis=0)
+    local = jnp.where(kind == 0, (squares + came[share])[None], resid_size[None])
+    local = jnp.where(kind == 2, image_size[None], local)
     seen = spread(local, PLANE)
     alpha = gamma / jnp.sum(seen[:, 0], axis=0)
     bound = jnp.max(seen[:, 1], axis=0) + jnp.abs(alpha) * jnp.max(seen[:, 2], axis=0)
     scale = TERM_MAX / jnp.maximum(SCALE * bound, TINY)
     coef_new = coef + alpha[None, :] * direction
-    rows_new = rows_resid - alpha[None, :] * image
-    weighted_b = (rows_weight * rows_new).astype(jnp.bfloat16)
-    resid_new = jnp.where(lower, rows_new[:rows_dev], rows_new[rows_dev:])
-    weighted_b, coef_new = lax.optimization_barrier((weighted_b, coef_new))
+    resid_new = lax.optimization_barrier(own_resid - alpha[None, :] * own_image)
+    own_b = (own_weight * resid_new).astype(jnp.bfloat16)
+    peer_b = (peer_weight * (peer_resid - alpha[None, :] * peer_image)).astype(jnp.bfloat16)
+    own_b, peer_b, coef_new, resid_new = lax.optimization_barrier((own_b, peer_b, coef_new, resid_new))
 
-    terms = lax.dot_general(
-        feats, weighted_b, (((0,), (0,)), ((), ())), preferred_element_type=jnp.float32
-    )
+    def down(feats, weighted_b):
+        return lax.dot_general(feats, weighted_b, (((0,), (0,)), ((), ())), preferred_element_type=jnp.float32)
+
+    terms = down(own_feats, own_b) + down(peer_feats, peer_b)
     terms = (terms * scale[None, :]).astype(jnp.float16)
     terms = exchange(terms.reshape(n_plane, own, targets), PLANE)
-    terms, resid_new = lax.optimization_barrier((terms, resid_new))
     summed = jnp.sum(terms.astype(jnp.float32), axis=0) * (1.0 / scale)[None, :]
     gradient = summed - ridge[None, :] * coef_new
     gamma_new = total_of(total_of(jnp.sum(gradient * gradient, axis=0)[None], COLUMN), PLANE)[0]

time: 126 us -> 126 us (level)
  blocking collectives: 72.2 us -> 93.3 us
  waiting for transfers between devices: 12 us -> 0.61 us
  starting transfers between devices: 27 us -> 16.5 us
    all_to_all x5 -> x6, blocking collectives: 72.2 us -> 93.3 us  [exchange(): lax.all_to_all(blocks, axes, 0, 0, axis_index_groups=[ORDERS[axes]], tile...]
    all_to_all x2 -> x1, starting transfers between devices: 23 us -> 12.5 us  [exchange(): lax.all_to_all(blocks, axes, 0, 0, axis_index_groups=[ORDERS[axes]], tile...]
    all_to_all x2 -> x1, waiting for transfers between devices: 10.5 us -> 0.01 us  [exchange(): lax.all_to_all(blocks, axes, 0, 0, axis_index_groups=[ORDERS[axes]], tile...]
    dot_general x3 -> x6, matrix products: 5.65 us -> 5.92 us  [the longest x2 4.07 us: features(): jnp.dot(block_x, freq_cols, preferred_element_type=jnp.float32)]
  transfers between devices with their start and end apart: 3 -> 2, of which waited for: 2 -> 1; matrix products, arithmetic and copies ran while one was open for 5% -> 6% of each run, Pallas kernels for 0% -> 0%
where the time goes in v8:
time: 126 us; the launch traced here: 124 us
  blocking collectives  93.3 us (74%)
  starting transfers between devices  16.5 us (13%)
  matrix products  5.92 us (5%)
  local copies, waits for them, and re-layouts  2.79 us (2%)
  other arithmetic  2.35 us (2%)
  Pallas kernels  1.98 us (2%)
    all_to_all x6, blocking collectives, exchange(): lax.all_to_all(blocks, axes, 0, 0, axis_index_groups=[ORDERS[axes]], tile...  93.3 us
    all_to_all x1, starting transfers between devices, exchange(): lax.all_to_all(blocks, axes, 0, 0, axis_index_groups=[ORDERS[axes]], tile...  12.5 us
    dot_general x2, matrix products, features(): jnp.dot(block_x, freq_cols, preferred_element_type=jnp.float32)  4.07 us
    ppermute x1, starting transfers between devices, body(): peer = lax.ppermute(packed, 'zl', swap)  4 us
  transfers between devices with their start and end apart: 2, of which 1 were waited for; matrix products, arithmetic and copies ran while one was open for 6% of the time, Pallas kernels for 0%

profile of v8, /device:TPU:1, one launch (start us, length us, event | category | flops | bytes accessed | tf_op | source)
XLA Modules:
  0.0 124.5 jit_solution(5452710413252969127)
XLA Ops:
  0.6 0.0 copy-start.1
  0.6 2.0 %shard_map.120 = (bf16[32,64,128]{2,1,0:T(8,128)(2,1)}, f32[514,128]{1,0:T(8,128)}) custom-call(f32[64,128]{1,0:T(8,128)} %direction_ref.1, bf16[256,128]{1,0:T(8,128)(2,1)} %descriptors_ref.1, f32[256,128]{1,0:T(8,128)} %resid_ref.1, f32[2,128]{1,0:T(2,128)} %bitcast.61), custom_call_target="tpu_custom_call" | custom-call | bytes 1050624 | tf_op jit(solution)/shard_map/pallas_call | solution.py:90
  2.6 12.5 %all-to-all-start = ((bf16[32,64,128]{2,1,0:T(8,128)(2,1)}), bf16[32,64,128]{2,1,0:T(8,128)(2,1)S(1)}, u32[]{:S(2)}, u32[]{:S(2)}) async-start(bf16[32,64,128]{2,1,0:T(8,128)(2,1)} %get-tuple-element.31), calls=%async_computation | async-start | bytes 1048576 | tf_op jit(solution)/shard_map/all_to_all | solution.py:58
  15.1 4.0 %collective-permute-start = (f32[514,128]{1,0:T(8,128)}, f32[514,128]{1,0:T(8,128)}, u32[]{:S(2)}, u32[]{:S(2)}) collective-permute-start(f32[514,128]{1,0:T(8,128)} %get-tuple-element.35), channel_id=1, source_target_pairs={{0,64},{64,0},{1,65},{65,1},{2,66},{66,2},{3,67},{67,3},{4,68},{68... | collective-permute-start | bytes 789512 | tf_op jit(solution)/shard_map/ppermute | solution.py:105
  19.1 0.0 copy-done.1
  19.2 0.7 copy.19
  19.9 0.2 copy.20
  20.2 0.0 copy-start.7
  20.2 0.0 copy-start.5
  20.3 0.3 copy.21
  20.5 0.4 copy-done.7
  21.0 0.1 copy-done.5
  21.0 0.0 copy-start.3
  21.0 0.0 copy-start.9
  21.0 0.0 copy-start
  21.0 0.0 copy-start.8
  21.1 1.6 %add_convert_fusion.1 = bf16[256,2048]{1,0:T(8,128)(2,1)S(1)} fusion(bf16[256,128]{1,0:T(8,128)(2,1)S(1)} %copy-done.5, bf16[128,2048]{0,1:T(8,128)(2,1)S(1)} %bitcast.54, f32[2048]{0:T(1024)S(1)} %bitcast.62), kind=kOutput, calls=%fused_computation.6 | convolution fusion | flops 145227776 | bytes 1646592 | tf_op jit(solution)/shard_map/dot_general | solution.py:116
  22.6 0.0 copy-done.3
  22.7 0.0 copy-done.9
  22.7 0.0 copy-done
  22.7 0.0 copy-done.8
  22.7 0.1 abs_reduce_fusion.1
  22.8 0.6 collective-permute-done
  23.4 0.7 slice_bitcast_fusion
  24.1 1.0 abs_reduce_fusion
  25.1 2.5 %add_convert_fusion = bf16[256,2048]{1,0:T(8,128)(2,1)S(1)} fusion(bf16[128,2048]{0,1:T(8,128)(2,1)S(1)} %bitcast.55, f32[2048]{0:T(1024)S(1)} %bitcast.63, f32[514,128]{1,0:T(8,128)} %collective-permute-done), kind=kOutput, calls=%fused_computation.5 | convolution fusion | flops 145227776 | bytes 1646592 | tf_op jit(solution)/shard_map/dot_general | solution.py:116
  27.6 0.0 all-to-all-done
  27.7 0.1 broadcast_in_dim.45
  27.7 0.1 broadcast_in_dim.47
  27.9 0.4 fusion.10
  28.3 0.4 broadcast_select_fusion.1
  28.8 24.1 %all_to_all.35 = f32[16,40,128]{2,1,0:T(8,128)S(1)} all-to-all(f32[16,40,128]{2,1,0:T(8,128)S(1)} %pad_maximum_fusion.1), channel_id=1, replica_groups={{68,69,70,71,64,65,66,67,4,5,6,7,0,1,2,3},{76,77,78,79,72,73,74,75,12,1..., dimensions={0} | all-to-all | bytes 655360 | tf_op jit(solution)/shard_map/all_to_all | solution.py:58
  52.9 0.0 copy-start.10
  53.0 13.9 %all_to_all.36 = f32[16,32,128]{2,1,0:T(8,128)S(1)} all-to-all(f32[16,32,128]{2,1,0:T(8,128)S(1)} %broadcast_in_dim.49), channel_id=1, replica_groups={{68,69,70,71,64,65,66,67,4,5,6,7,0,1,2,3},{76,77,78,79,72,73,74,75,12,1..., dimensions={0} | all-to-all | bytes 524288 | tf_op jit(solution)/shard_map/all_to_all | solution.py:58
  66.9 0.0 copy-start.6
  67.0 0.1 add_reduce_fusion.1
  67.1 11.3 %all_to_all.37 = f32[32,4,128]{2,1,0:T(4,128)S(1)} all-to-all(f32[32,4,128]{2,1,0:T(4,128)S(1)} %broadcast_in_dim.54), channel_id=1, replica_groups={{288,296,304,312,256,264,272,280,416,424,432,440,384,392,400,408,32,40,..., dimensions={0} | all-to-all | bytes 131072 | tf_op jit(solution)/shard_map/all_to_all | solution.py:58
  78.5 0.0 copy-done.10
  78.6 0.0 copy-start.2
  78.6 0.0 copy-done.6
  78.6 0.0 copy-start.4
  78.6 0.5 fusion.11
  79.1 0.1 copy-done.2
  79.2 0.5 fusion.1
  79.7 20.9 %all_to_all.38 = f16[32,64,128]{2,1,0:T(8,128)(2,1)S(1)} all-to-all(f16[32,64,128]{2,1,0:T(8,128)(2,1)S(1)} %bitcast.52), channel_id=1, replica_groups={{288,296,304,312,256,264,272,280,416,424,432,440,384,392,400,408,32,40,..., dimensions={0} | all-to-all | bytes 1048576 | tf_op jit(solution)/shard_map/all_to_all | solution.py:58
  100.6 0.1 convert_reduce_fusion
  100.7 11.3 %all_to_all.39 = f32[16,1,128]{2,1,0:T(1,128)S(1)} all-to-all(f32[16,1,128]{2,1,0:T(1,128)S(1)} %broadcast_in_dim.92), channel_id=1, replica_groups={{68,69,70,71,64,65,66,67,4,5,6,7,0,1,2,3},{76,77,78,79,72,73,74,75,12,1..., dimensions={0} | all-to-all | bytes 16384 | tf_op jit(solution)/shard_map/all_to_all | solution.py:58
  112.0 11.8 %all_to_all.40 = f32[32,1,128]{2,1,0:T(1,128)S(1)} all-to-all(f32[32,1,128]{2,1,0:T(1,128)S(1)} %broadcast_in_dim.93), channel_id=1, replica_groups={{288,296,304,312,256,264,272,280,416,424,432,440,384,392,400,408,32,40,..., dimensions={0} | all-to-all | bytes 32768 | tf_op jit(solution)/shard_map/all_to_all | solution.py:58
  123.8 0.0 copy-start.11
  123.8 0.0 copy-done.4
  123.8 0.6 multiply_add_fusion
  124.5 0.0 copy-done.11
  (38 shorter events, 0.6 us)
Async XLA Ops:
  0.6 18.5 %copy-start.1 = (bf16[128,4096]{1,0:T(8,128)(2,1)S(1)}, bf16[128,4096]{1,0:T(8,128)(2,1)}, u32[]{:S(2)}) copy-start(bf16[128,4096]{1,0:T(8,128)(2,1)} %param.10) | copy-start | bytes 3145732
  2.6 25.0 %all-to-all-start = ((bf16[32,64,128]{2,1,0:T(8,128)(2,1)}), bf16[32,64,128]{2,1,0:T(8,128)(2,1)S(1)}, u32[]{:S(2)}, u32[]{:S(2)}) async-start(bf16[32,64,128]{2,1,0:T(8,128)(2,1)} %get-tuple-element.31), calls=%async_computation | async-start | bytes 1048576 | tf_op jit(solution)/shard_map/all_to_all | solution.py:58
  15.1 8.3 %collective-permute-start = (f32[514,128]{1,0:T(8,128)}, f32[514,128]{1,0:T(8,128)}, u32[]{:S(2)}, u32[]{:S(2)}) collective-permute-start(f32[514,128]{1,0:T(8,128)} %get-tuple-element.35), channel_id=1, source_target_pairs={{0,64},{64,0},{1,65},{65,1},{2,66},{66,2},{3,67},{67,3},{4,68},{68... | collective-permute-start | bytes 789512 | tf_op jit(solution)/shard_map/ppermute | solution.py:105
  20.2 0.7 copy-start.7
  20.2 0.8 copy-start.5
  21.0 1.6 %copy-start.3 = (f32[64,128]{1,0:T(8,128)S(1)}, f32[64,128]{1,0:T(8,128)}, u32[]{:S(2)}) copy-start(f32[64,128]{1,0:T(8,128)} %direction_ref.1) | copy-start | bytes 98308
  21.0 1.6 %copy-start.9 = (f32[128]{0:T(128)S(1)}, f32[128]{0:T(128)}, u32[]{:S(2)}) copy-start(f32[128]{0:T(128)} %param.16) | copy-start | bytes 1540
  21.0 1.7 %copy-start = (f32[256,128]{1,0:T(8,128)S(1)}, f32[256,128]{1,0:T(8,128)}, u32[]{:S(2)}) copy-start(f32[256,128]{1,0:T(8,128)} %resid_ref.1) | copy-start | bytes 393220
  21.0 1.7 %copy-start.8 = (f32[256]{0:T(256)S(1)}, f32[256]{0:T(256)}, u32[]{:S(2)}) copy-start(f32[256]{0:T(256)} %param.12) | copy-start | bytes 3076
  52.9 25.5 %copy-start.10 = (f32[128]{0:T(128)S(1)}, f32[128]{0:T(128)}, u32[]{:S(2)}) copy-start(f32[128]{0:T(128)} %param.17) | copy-start | bytes 1540
  66.9 11.7 %copy-start.6 = (f32[64,128]{1,0:T(8,128)S(1)}, f32[64,128]{1,0:T(8,128)}, u32[]{:S(2)}) copy-start(f32[64,128]{1,0:T(8,128)} %param.14) | copy-start | bytes 98308
  78.6 0.7 copy-start.2
  78.6 45.2 %copy-start.4 = (f32[64,128]{1,0:T(8,128)}, f32[64,128]{1,0:T(8,128)S(1)}, u32[]{:S(2)}) copy-start(f32[64,128]{1,0:T(8,128)S(1)} %multiply_add_fusion.1) | copy-start | bytes 98308
  123.8 0.7 copy-start.11

commit v9 on v5

--- a/solution.py
+++ b/solution.py
@@ -105,7 +105,7 @@
     feats = scaled_cos(angle).astype(jnp.bfloat16)
     penalty = ridge * jnp.sum(direction * direction, axis=0)
     extra = jnp.broadcast_to(penalty[None, None], (n_column, 8, targets))
-    rows_weight = jnp.broadcast_to(rows_weight[:, None], rows_resid.shape)
+    rows_weight = jnp.broadcast_to(rows_weight[:, None], (2 * rows_dev, targets))
     resid_size = jnp.sum(jnp.abs(rows_weight * rows_resid), axis=0)
     kind = lax.broadcasted_iota(jnp.int32, (4, targets), 0)
     gathered, feats, rows_resid, rows_weight, extra, resid_size, lower, kind = lax.optimization_barrier(
@@ -125,16 +125,17 @@
     scale = TERM_MAX / jnp.maximum(SCALE * bound, TINY)
     coef_new = coef + alpha[None, :] * direction
     rows_new = rows_resid - alpha[None, :] * image
+    resid_new = lax.optimization_barrier(jnp.where(lower, rows_new[:rows_dev], rows_new[rows_dev:]))
+    peer_new = jnp.where(lower, rows_new[rows_dev:], rows_new[:rows_dev])
+    rows_new = jnp.where(lower, jnp.concatenate([resid_new, peer_new]), jnp.concatenate([peer_new, resid_new]))
     weighted_b = (rows_weight * rows_new).astype(jnp.bfloat16)
-    resid_new = jnp.where(lower, rows_new[:rows_dev], rows_new[rows_dev:])
-    weighted_b, coef_new = lax.optimization_barrier((weighted_b, coef_new))
+    weighted_b, coef_new, resid_new = lax.optimization_barrier((weighted_b, coef_new, resid_new))
 
     terms = lax.dot_general(
         feats, weighted_b, (((0,), (0,)), ((), ())), preferred_element_type=jnp.float32
     )
     terms = (terms * scale[None, :]).astype(jnp.float16)
     terms = exchange(terms.reshape(n_plane, own, targets), PLANE)
-    terms, resid_new = lax.optimization_barrier((terms, resid_new))
     summed = jnp.sum(terms.astype(jnp.float32), axis=0) * (1.0 / scale)[None, :]
     gradient = summed - ridge[None, :] * coef_new
     gamma_new = total_of(total_of(jnp.sum(gradient * gradient, axis=0)[None], COLUMN), PLANE)[0]

time: 125 us -> 124 us (level)
  blocking collectives: 70.5 us -> 91.4 us
  starting transfers between devices: 29 us -> 18.4 us
  waiting for transfers between devices: 10.5 us -> 0.01 us
    all_to_all x5 -> x6, blocking collectives: 70.5 us -> 91.4 us  [exchange(): lax.all_to_all(blocks, axes, 0, 0, axis_index_groups=[ORDERS[axes]], tile...]
    all_to_all x2 -> x1, starting transfers between devices: 23 us -> 12.5 us  [exchange(): lax.all_to_all(blocks, axes, 0, 0, axis_index_groups=[ORDERS[axes]], tile...]
    all_to_all x2 -> x1, waiting for transfers between devices: 10.5 us -> 0.01 us  [exchange(): lax.all_to_all(blocks, axes, 0, 0, axis_index_groups=[ORDERS[axes]], tile...]
  transfers between devices with their start and end apart: 4 -> 3, of which waited for: 1 -> 0; matrix products, arithmetic and copies ran while one was open for 6% -> 5% of each run, Pallas kernels for 0% -> 0%
where the time goes in v9:
time: 124 us; the launch traced here: 122 us
  blocking collectives  91.4 us (74%)
  starting transfers between devices  18.4 us (15%)
  matrix products  5.62 us (5%)
  other arithmetic  2.32 us (2%)
  local copies, waits for them, and re-layouts  1.86 us (2%)
  Pallas kernels  1.7 us (1%)
    all_to_all x6, blocking collectives, exchange(): lax.all_to_all(blocks, axes, 0, 0, axis_index_groups=[ORDERS[axes]], tile...  91.4 us
    all_to_all x1, starting transfers between devices, exchange(): lax.all_to_all(blocks, axes, 0, 0, axis_index_groups=[ORDERS[axes]], tile...  12.5 us
    dot_general x1, matrix products, body(): jnp.dot(rows_x, freq_cols, preferred_element_type=jnp.float32)  4.16 us
    ppermute x1, starting transfers between devices, body(): rows_x = both(descriptors, lax.ppermute(descriptors, 'zl', swap))  4 us
  transfers between devices with their start and end apart: 3, of which 0 were waited for; matrix products, arithmetic and copies ran while one was open for 5% of the time, Pallas kernels for 0%

profile of v9, /device:TPU:1, one launch (start us, length us, event | category | flops | bytes accessed | tf_op | source)
XLA Modules:
  0.0 122.4 jit_solution(10620590873836946497)
XLA Ops:
  0.6 0.0 copy-start
  0.6 1.7 %shard_map.120 = bf16[32,64,128]{2,1,0:T(8,128)(2,1)} custom-call(f32[64,128]{1,0:T(8,128)} %direction_ref.1), custom_call_target="tpu_custom_call" | custom-call | bytes 557056 | tf_op jit(solution)/shard_map/pallas_call | solution.py:83
  2.3 12.5 %all-to-all-start = ((bf16[32,64,128]{2,1,0:T(8,128)(2,1)}), bf16[32,64,128]{2,1,0:T(8,128)(2,1)S(1)}, u32[]{:S(2)}, u32[]{:S(2)}) async-start(bf16[32,64,128]{2,1,0:T(8,128)(2,1)} %shard_map.120), calls=%async_computation | async-start | bytes 1048576 | tf_op jit(solution)/shard_map/all_to_all | solution.py:54
  14.8 4.0 %collective-permute-start = (bf16[256,128]{1,0:T(8,128)(2,1)}, bf16[256,128]{1,0:T(8,128)(2,1)}, u32[]{:S(2)}, u32[]{:S(2)}) collective-permute-start(bf16[256,128]{1,0:T(8,128)(2,1)} %param.9), channel_id=1, source_target_pairs={{0,64},{64,0},{1,65},{65,1},{2,66},{66,2},{3,67},{67,3},{4,68},{68... | collective-permute-start | bytes 196616 | tf_op jit(solution)/shard_map/ppermute | solution.py:93
  18.9 0.9 pad_maximum_fusion.2
  19.8 1.9 %collective-permute-start.1 = (f32[258,128]{1,0:T(8,128)S(1)}, f32[258,128]{1,0:T(8,128)S(1)}, u32[]{:S(2)}, u32[]{:S(2)}) collective-permute-start(f32[258,128]{1,0:T(8,128)S(1)} %pad_maximum_fusion.2), channel_id=1, source_target_pairs={{0,64},{64,0},{1,65},{65,1},{2,66},{66,2},{3,67},{67,3},{4,68},{68... | collective-permute-start | bytes 396296 | tf_op jit(solution)/shard_map/ppermute | solution.py:95
  21.7 0.0 copy-done
  21.7 0.7 copy.19
  22.5 0.2 copy.20
  22.7 0.0 copy-start.6
  22.7 0.0 copy-start.1
  22.7 0.0 copy-start.8
  22.7 0.0 copy-start.11
  22.9 0.3 copy.21
  23.1 0.3 copy-done.6
  23.4 0.0 copy-done.1
  23.5 0.0 copy-done.8
  23.5 0.0 collective-permute-done
  23.5 0.0 copy-done.11
  23.6 0.0 copy-start.7
  23.6 0.0 copy-start.3
  23.6 4.2 %add_convert_fusion = bf16[512,2048]{1,0:T(8,128)(2,1)S(1)} fusion(bf16[128,2048]{0,1:T(8,128)(2,1)S(1)} %bitcast.39, f32[2048]{0:T(1024)S(1)} %bitcast.45, bf16[256,128]{1,0:T(8,128)(2,1)} %collective-permute-done, bf16[256,128]{1,0:T(8,128)(2,1)S(1)} %copy-done.11, pred[]{:T(512)S(6)} %eq.18), kind=kOutput, calls=%fused_computation | convolution fusion | flops 291045376 | bytes 2760705 | tf_op jit(solution)/shard_map/dot_general | solution.py:104
  27.7 0.0 collective-permute-done.1
  27.8 0.0 copy-done.7
  27.8 0.0 copy-done.3
  27.8 0.2 abs_reduce_fusion.1
  28.0 0.0 all-to-all-done
  28.0 0.1 broadcast_in_dim.41
  28.1 0.7 fusion.18
  28.9 0.0 copy-start.9
  28.9 0.0 copy-start.5
  28.9 22.3 %all_to_all.35 = f32[16,40,128]{2,1,0:T(8,128)S(1)} all-to-all(f32[16,40,128]{2,1,0:T(8,128)S(1)} %pad_maximum_fusion.1), channel_id=1, replica_groups={{68,69,70,71,64,65,66,67,4,5,6,7,0,1,2,3},{76,77,78,79,72,73,74,75,12,1..., dimensions={0} | all-to-all | bytes 655360 | tf_op jit(solution)/shard_map/all_to_all | solution.py:54
  51.2 13.9 %all_to_all.36 = f32[16,32,128]{2,1,0:T(8,128)S(1)} all-to-all(f32[16,32,128]{2,1,0:T(8,128)S(1)} %broadcast_in_dim.43), channel_id=1, replica_groups={{68,69,70,71,64,65,66,67,4,5,6,7,0,1,2,3},{76,77,78,79,72,73,74,75,12,1..., dimensions={0} | all-to-all | bytes 524288 | tf_op jit(solution)/shard_map/all_to_all | solution.py:54
  65.2 0.1 abs_reduce_fusion
  65.3 11.3 %all_to_all.37 = f32[32,4,128]{2,1,0:T(4,128)S(1)} all-to-all(f32[32,4,128]{2,1,0:T(4,128)S(1)} %broadcast_in_dim.48), channel_id=1, replica_groups={{288,296,304,312,256,264,272,280,416,424,432,440,384,392,400,408,32,40,..., dimensions={0} | all-to-all | bytes 131072 | tf_op jit(solution)/shard_map/all_to_all | solution.py:54
  76.7 0.0 copy-done.9
  76.8 0.0 copy-start.2
  76.8 0.0 copy-done.5
  76.8 0.0 copy-start.4
  76.9 0.8 fusion
  77.7 0.0 copy-done.2
  77.7 20.9 %all_to_all.38 = f16[32,64,128]{2,1,0:T(8,128)(2,1)S(1)} all-to-all(f16[32,64,128]{2,1,0:T(8,128)(2,1)S(1)} %bitcast.34), channel_id=1, replica_groups={{288,296,304,312,256,264,272,280,416,424,432,440,384,392,400,408,32,40,..., dimensions={0} | all-to-all | bytes 1048576 | tf_op jit(solution)/shard_map/all_to_all | solution.py:54
  98.6 0.1 convert_reduce_fusion
  98.7 11.3 %all_to_all.39 = f32[16,1,128]{2,1,0:T(1,128)S(1)} all-to-all(f32[16,1,128]{2,1,0:T(1,128)S(1)} %broadcast_in_dim.49), channel_id=1, replica_groups={{68,69,70,71,64,65,66,67,4,5,6,7,0,1,2,3},{76,77,78,79,72,73,74,75,12,1..., dimensions={0} | all-to-all | bytes 16384 | tf_op jit(solution)/shard_map/all_to_all | solution.py:54
  110.0 11.8 %all_to_all.40 = f32[32,1,128]{2,1,0:T(1,128)S(1)} all-to-all(f32[32,1,128]{2,1,0:T(1,128)S(1)} %broadcast_in_dim.50), channel_id=1, replica_groups={{288,296,304,312,256,264,272,280,416,424,432,440,384,392,400,408,32,40,..., dimensions={0} | all-to-all | bytes 32768 | tf_op jit(solution)/shard_map/all_to_all | solution.py:54
  121.8 0.0 copy-start.10
  121.8 0.0 copy-done.4
  121.8 0.6 multiply_add_fusion
  122.4 0.0 copy-done.10
  (39 shorter events, 0.7 us)
Async XLA Ops:
  0.6 21.1 %copy-start = (bf16[128,4096]{1,0:T(8,128)(2,1)S(1)}, bf16[128,4096]{1,0:T(8,128)(2,1)}, u32[]{:S(2)}) copy-start(bf16[128,4096]{1,0:T(8,128)(2,1)} %param.10) | copy-start | bytes 3145732
  2.3 25.6 %all-to-all-start = ((bf16[32,64,128]{2,1,0:T(8,128)(2,1)}), bf16[32,64,128]{2,1,0:T(8,128)(2,1)S(1)}, u32[]{:S(2)}, u32[]{:S(2)}) async-start(bf16[32,64,128]{2,1,0:T(8,128)(2,1)} %shard_map.120), calls=%async_computation | async-start | bytes 1048576 | tf_op jit(solution)/shard_map/all_to_all | solution.py:54
  14.8 8.7 %collective-permute-start = (bf16[256,128]{1,0:T(8,128)(2,1)}, bf16[256,128]{1,0:T(8,128)(2,1)}, u32[]{:S(2)}, u32[]{:S(2)}) collective-permute-start(bf16[256,128]{1,0:T(8,128)(2,1)} %param.9), channel_id=1, source_target_pairs={{0,64},{64,0},{1,65},{65,1},{2,66},{66,2},{3,67},{67,3},{4,68},{68... | collective-permute-start | bytes 196616 | tf_op jit(solution)/shard_map/ppermute | solution.py:93
  19.8 8.0 %collective-permute-start.1 = (f32[258,128]{1,0:T(8,128)S(1)}, f32[258,128]{1,0:T(8,128)S(1)}, u32[]{:S(2)}, u32[]{:S(2)}) collective-permute-start(f32[258,128]{1,0:T(8,128)S(1)} %pad_maximum_fusion.2), channel_id=1, source_target_pairs={{0,64},{64,0},{1,65},{65,1},{2,66},{66,2},{3,67},{67,3},{4,68},{68... | collective-permute-start | bytes 396296 | tf_op jit(solution)/shard_map/ppermute | solution.py:95
  22.7 0.7 copy-start.6
  22.7 0.8 copy-start.1
  22.7 0.8 copy-start.8
  22.7 0.9 copy-start.11
  23.6 4.2 %copy-start.7 = (f32[256]{0:T(256)S(1)}, f32[256]{0:T(256)}, u32[]{:S(2)}) copy-start(f32[256]{0:T(256)} %param.12) | copy-start | bytes 3076
  23.6 4.2 %copy-start.3 = (f32[256,128]{1,0:T(8,128)S(1)}, f32[256,128]{1,0:T(8,128)}, u32[]{:S(2)}) copy-start(f32[256,128]{1,0:T(8,128)} %param.13) | copy-start | bytes 393220
  28.9 47.9 %copy-start.9 = (f32[128]{0:T(128)S(1)}, f32[128]{0:T(128)}, u32[]{:S(2)}) copy-start(f32[128]{0:T(128)} %param.17) | copy-start | bytes 1540
  28.9 47.9 %copy-start.5 = (f32[64,128]{1,0:T(8,128)S(1)}, f32[64,128]{1,0:T(8,128)}, u32[]{:S(2)}) copy-start(f32[64,128]{1,0:T(8,128)} %param.14) | copy-start | bytes 98308
  76.8 0.9 copy-start.2
  76.8 44.9 %copy-start.4 = (f32[64,128]{1,0:T(8,128)}, f32[64,128]{1,0:T(8,128)S(1)}, u32[]{:S(2)}) copy-start(f32[64,128]{1,0:T(8,128)S(1)} %multiply_add_fusion.1) | copy-start | bytes 98308
  121.8 0.7 copy-start.10

commit v10 on v9

--- a/solution.py
+++ b/solution.py
@@ -2,7 +2,6 @@
 import jax.numpy as jnp
 import numpy as np
 from jax import lax
-from jax.experimental import pallas as pl
 from jax.sharding import Mesh, PartitionSpec as P
 
 AXES = ("x", "zl", "y", "zh", "core")
@@ -45,11 +44,6 @@
     return value
 
 
-def rounded_copies(direction_ref, copies_ref):
-    rounded = direction_ref[...].astype(copies_ref.dtype)
-    copies_ref[...] = jnp.broadcast_to(rounded[None], copies_ref.shape)
-
-
 def exchange(blocks, axes):
     return lax.all_to_all(blocks, axes, 0, 0, axis_index_groups=[ORDERS[axes]], tiled=True)
 
@@ -80,11 +74,8 @@
     def both(mine, peer):
         return jnp.where(zl == 0, jnp.concatenate([mine, peer]), jnp.concatenate([peer, mine]))
 
-    copies = pl.pallas_call(
-        rounded_copies,
-        out_shape=jax.ShapeDtypeStruct((n_plane, own, targets), jnp.bfloat16),
-        cost_estimate=pl.CostEstimate(flops=0, transcendentals=0, bytes_accessed=4 * own * targets + 2 * n_plane * own * targets),
-    )(direction)
+    every = lax.broadcasted_iota(jnp.int32, (n_plane, own, targets), 0) >= -zl
+    copies = jnp.where(every, direction[None], 0.0).astype(jnp.bfloat16)
     copies, descriptors, resid, row_weight, freqs, phases, direction = lax.optimization_barrier(
         (copies, descriptors, resid, row_weight, freqs, phases, direction)
     )

time: 124 us -> 124 us (level)
  other arithmetic: 2.32 us -> 4.1 us
  Pallas kernels: 1.7 us -> 0 us
    convert_element_type x0 -> x1, other arithmetic: none -> 1.78 us  [body(): copies = jnp.where(every, direction[None], 0.0).astype(jnp.bfloat16)]
    pallas_call x1 -> x0, Pallas kernels: 1.7 us -> none  [body(): pl.pallas_call(rounded_copies, out_shape=jax.ShapeDtypeStruct((n_plane, o...]
where the time goes in v10:
time: 124 us; the launch traced here: 123 us
  blocking collectives  91.4 us (74%)
  starting transfers between devices  18.4 us (15%)
  matrix products  5.68 us (5%)
  other arithmetic  4.1 us (3%)
  local copies, waits for them, and re-layouts  1.84 us (1%)
    all_to_all x6, blocking collectives, exchange(): lax.all_to_all(blocks, axes, 0, 0, axis_index_groups=[ORDERS[axes]], tile...  91.4 us
    all_to_all x1, starting transfers between devices, exchange(): lax.all_to_all(blocks, axes, 0, 0, axis_index_groups=[ORDERS[axes]], tile...  12.5 us
    dot_general x1, matrix products, body(): jnp.dot(rows_x, freq_cols, preferred_element_type=jnp.float32)  4.21 us
    ppermute x1, starting transfers between devices, body(): rows_x = both(descriptors, lax.ppermute(descriptors, 'zl', swap))  4 us
  transfers between devices with their start and end apart: 3, of which 0 were waited for; matrix products, arithmetic and copies ran while one was open for 5% of the time, Pallas kernels for 0%

profile of v10, /device:TPU:1, one launch (start us, length us, event | category | flops | bytes accessed | tf_op | source)
XLA Modules:
  0.0 122.6 jit_solution(847712795980133138)
XLA Ops:
  0.6 0.0 copy-start
  0.7 1.8 %select_convert_fusion = bf16[32,64,128]{2,1,0:T(8,128)(2,1)} fusion(f32[64,128]{1,0:T(8,128)} %param.15, pred[32]{0:T(512)(128)(4,1)S(1)} %iota_compare_fusion), kind=kLoop, calls=%fused_computation.4 | loop fusion | flops 262144 | bytes 557088 | tf_op jit(solution)/shard_map/convert_element_type | solution.py:78
  2.4 12.5 %all-to-all-start = ((bf16[32,64,128]{2,1,0:T(8,128)(2,1)}), bf16[32,64,128]{2,1,0:T(8,128)(2,1)S(1)}, u32[]{:S(2)}, u32[]{:S(2)}) async-start(bf16[32,64,128]{2,1,0:T(8,128)(2,1)} %select_convert_fusion), calls=%async_computation | async-start | bytes 1048576 | tf_op jit(solution)/shard_map/all_to_all | solution.py:48
  15.0 4.0 %collective-permute-start = (bf16[256,128]{1,0:T(8,128)(2,1)}, bf16[256,128]{1,0:T(8,128)(2,1)}, u32[]{:S(2)}, u32[]{:S(2)}) collective-permute-start(bf16[256,128]{1,0:T(8,128)(2,1)} %param.9), channel_id=1, source_target_pairs={{0,64},{64,0},{1,65},{65,1},{2,66},{66,2},{3,67},{67,3},{4,68},{68... | collective-permute-start | bytes 196616 | tf_op jit(solution)/shard_map/ppermute | solution.py:84
  19.0 0.9 pad_maximum_fusion.2
  19.9 1.9 %collective-permute-start.1 = (f32[258,128]{1,0:T(8,128)S(1)}, f32[258,128]{1,0:T(8,128)S(1)}, u32[]{:S(2)}, u32[]{:S(2)}) collective-permute-start(f32[258,128]{1,0:T(8,128)S(1)} %pad_maximum_fusion.2), channel_id=1, source_target_pairs={{0,64},{64,0},{1,65},{65,1},{2,66},{66,2},{3,67},{67,3},{4,68},{68... | collective-permute-start | bytes 396296 | tf_op jit(solution)/shard_map/ppermute | solution.py:86
  21.8 0.0 copy-done
  21.8 0.7 copy.19
  22.6 0.2 copy.20
  22.8 0.0 copy-start.6
  22.8 0.0 copy-start.1
  22.8 0.0 copy-start.8
  22.9 0.3 copy.21
  23.2 0.3 copy-done.6
  23.5 0.0 copy-done.1
  23.6 0.0 copy-done.8
  23.6 0.0 collective-permute-done
  23.6 0.0 copy-start.7
  23.7 0.0 copy-start.3
  23.7 4.2 %add_convert_fusion = bf16[512,2048]{1,0:T(8,128)(2,1)S(1)} fusion(bf16[128,2048]{0,1:T(8,128)(2,1)S(1)} %bitcast.39, f32[2048]{0:T(1024)S(1)} %bitcast.45, bf16[256,128]{1,0:T(8,128)(2,1)} %collective-permute-done, bf16[256,128]{1,0:T(8,128)(2,1)} %param.9, pred[]{:T(512)S(6)} %eq.18), kind=kOutput, calls=%fused_computation | convolution fusion | flops 291045376 | bytes 2760705 | tf_op jit(solution)/shard_map/dot_general | solution.py:95
  27.9 0.0 collective-permute-done.1
  27.9 0.0 copy-done.7
  27.9 0.0 copy-done.3
  28.0 0.2 abs_reduce_fusion.1
  28.1 0.0 all-to-all-done
  28.1 0.1 broadcast_in_dim.55
  28.3 0.7 fusion.18
  29.0 0.0 copy-start.9
  29.0 0.0 copy-start.5
  29.0 22.3 %all_to_all.35 = f32[16,40,128]{2,1,0:T(8,128)S(1)} all-to-all(f32[16,40,128]{2,1,0:T(8,128)S(1)} %pad_maximum_fusion.1), channel_id=1, replica_groups={{68,69,70,71,64,65,66,67,4,5,6,7,0,1,2,3},{76,77,78,79,72,73,74,75,12,1..., dimensions={0} | all-to-all | bytes 655360 | tf_op jit(solution)/shard_map/all_to_all | solution.py:48
  51.4 13.9 %all_to_all.36 = f32[16,32,128]{2,1,0:T(8,128)S(1)} all-to-all(f32[16,32,128]{2,1,0:T(8,128)S(1)} %broadcast_in_dim.57), channel_id=1, replica_groups={{68,69,70,71,64,65,66,67,4,5,6,7,0,1,2,3},{76,77,78,79,72,73,74,75,12,1..., dimensions={0} | all-to-all | bytes 524288 | tf_op jit(solution)/shard_map/all_to_all | solution.py:48
  65.3 0.1 abs_reduce_fusion
  65.4 11.3 %all_to_all.37 = f32[32,4,128]{2,1,0:T(4,128)S(1)} all-to-all(f32[32,4,128]{2,1,0:T(4,128)S(1)} %broadcast_in_dim.96), channel_id=1, replica_groups={{288,296,304,312,256,264,272,280,416,424,432,440,384,392,400,408,32,40,..., dimensions={0} | all-to-all | bytes 131072 | tf_op jit(solution)/shard_map/all_to_all | solution.py:48
  76.9 0.0 copy-done.9
  76.9 0.0 copy-start.2
  77.0 0.0 copy-done.5
  77.0 0.0 copy-start.4
  77.1 0.8 fusion
  77.8 0.0 copy-done.2
  77.8 20.9 %all_to_all.38 = f16[32,64,128]{2,1,0:T(8,128)(2,1)S(1)} all-to-all(f16[32,64,128]{2,1,0:T(8,128)(2,1)S(1)} %bitcast.34), channel_id=1, replica_groups={{288,296,304,312,256,264,272,280,416,424,432,440,384,392,400,408,32,40,..., dimensions={0} | all-to-all | bytes 1048576 | tf_op jit(solution)/shard_map/all_to_all | solution.py:48
  98.7 0.1 convert_reduce_fusion
  98.8 11.3 %all_to_all.39 = f32[16,1,128]{2,1,0:T(1,128)S(1)} all-to-all(f32[16,1,128]{2,1,0:T(1,128)S(1)} %broadcast_in_dim.97), channel_id=1, replica_groups={{68,69,70,71,64,65,66,67,4,5,6,7,0,1,2,3},{76,77,78,79,72,73,74,75,12,1..., dimensions={0} | all-to-all | bytes 16384 | tf_op jit(solution)/shard_map/all_to_all | solution.py:48
  110.1 11.8 %all_to_all.40 = f32[32,1,128]{2,1,0:T(1,128)S(1)} all-to-all(f32[32,1,128]{2,1,0:T(1,128)S(1)} %broadcast_in_dim.98), channel_id=1, replica_groups={{288,296,304,312,256,264,272,280,416,424,432,440,384,392,400,408,32,40,..., dimensions={0} | all-to-all | bytes 32768 | tf_op jit(solution)/shard_map/all_to_all | solution.py:48
  121.9 0.0 copy-start.10
  121.9 0.0 copy-done.4
  121.9 0.6 multiply_add_fusion
  122.6 0.0 copy-done.10
  (40 shorter events, 0.7 us)
Async XLA Ops:
  0.6 21.2 %copy-start = (bf16[128,4096]{1,0:T(8,128)(2,1)S(1)}, bf16[128,4096]{1,0:T(8,128)(2,1)}, u32[]{:S(2)}) copy-start(bf16[128,4096]{1,0:T(8,128)(2,1)} %param.10) | copy-start | bytes 3145732
  2.4 25.7 %all-to-all-start = ((bf16[32,64,128]{2,1,0:T(8,128)(2,1)}), bf16[32,64,128]{2,1,0:T(8,128)(2,1)S(1)}, u32[]{:S(2)}, u32[]{:S(2)}) async-start(bf16[32,64,128]{2,1,0:T(8,128)(2,1)} %select_convert_fusion), calls=%async_computation | async-start | bytes 1048576 | tf_op jit(solution)/shard_map/all_to_all | solution.py:48
  15.0 8.7 %collective-permute-start = (bf16[256,128]{1,0:T(8,128)(2,1)}, bf16[256,128]{1,0:T(8,128)(2,1)}, u32[]{:S(2)}, u32[]{:S(2)}) collective-permute-start(bf16[256,128]{1,0:T(8,128)(2,1)} %param.9), channel_id=1, source_target_pairs={{0,64},{64,0},{1,65},{65,1},{2,66},{66,2},{3,67},{67,3},{4,68},{68... | collective-permute-start | bytes 196616 | tf_op jit(solution)/shard_map/ppermute | solution.py:84
  19.9 8.0 %collective-permute-start.1 = (f32[258,128]{1,0:T(8,128)S(1)}, f32[258,128]{1,0:T(8,128)S(1)}, u32[]{:S(2)}, u32[]{:S(2)}) collective-permute-start(f32[258,128]{1,0:T(8,128)S(1)} %pad_maximum_fusion.2), channel_id=1, source_target_pairs={{0,64},{64,0},{1,65},{65,1},{2,66},{66,2},{3,67},{67,3},{4,68},{68... | collective-permute-start | bytes 396296 | tf_op jit(solution)/shard_map/ppermute | solution.py:86
  22.8 0.7 copy-start.6
  22.8 0.8 copy-start.1
  22.8 0.8 copy-start.8
  23.6 4.3 %copy-start.7 = (f32[256]{0:T(256)S(1)}, f32[256]{0:T(256)}, u32[]{:S(2)}) copy-start(f32[256]{0:T(256)} %param.12) | copy-start | bytes 3076
  23.7 4.3 %copy-start.3 = (f32[256,128]{1,0:T(8,128)S(1)}, f32[256,128]{1,0:T(8,128)}, u32[]{:S(2)}) copy-start(f32[256,128]{1,0:T(8,128)} %param.13) | copy-start | bytes 393220
  29.0 47.9 %copy-start.9 = (f32[128]{0:T(128)S(1)}, f32[128]{0:T(128)}, u32[]{:S(2)}) copy-start(f32[128]{0:T(128)} %param.17) | copy-start | bytes 1540
  29.0 47.9 %copy-start.5 = (f32[64,128]{1,0:T(8,128)S(1)}, f32[64,128]{1,0:T(8,128)}, u32[]{:S(2)}) copy-start(f32[64,128]{1,0:T(8,128)} %param.14) | copy-start | bytes 98308
  76.9 0.9 copy-start.2
  77.0 44.9 %copy-start.4 = (f32[64,128]{1,0:T(8,128)}, f32[64,128]{1,0:T(8,128)S(1)}, u32[]{:S(2)}) copy-start(f32[64,128]{1,0:T(8,128)S(1)} %multiply_add_fusion.1) | copy-start | bytes 98308
  121.9 0.7 copy-start.10

commit v11 on v9

--- a/solution.py
+++ b/solution.py
@@ -138,7 +138,7 @@
     terms = exchange(terms.reshape(n_plane, own, targets), PLANE)
     summed = jnp.sum(terms.astype(jnp.float32), axis=0) * (1.0 / scale)[None, :]
     gradient = summed - ridge[None, :] * coef_new
-    gamma_new = total_of(total_of(jnp.sum(gradient * gradient, axis=0)[None], COLUMN), PLANE)[0]
+    gamma_new = total_of(total_of(jnp.sum(gradient * gradient, axis=0)[None], PLANE), COLUMN)[0]
     direction_new = gradient + (gamma_new / gamma)[None, :] * direction
     return (coef_new, resid_new, direction_new, gamma_new)
 

time: 124 us -> 124 us (level); the launches traced: 122 us -> 124 us
  blocking collectives: 91.4 us -> 92.8 us
    all_to_all x6, blocking collectives: 91.4 us -> 92.8 us  [exchange(): lax.all_to_all(blocks, axes, 0, 0, axis_index_groups=[ORDERS[axes]], tile...]
where the time goes in v11:
time: 124 us
  blocking collectives  92.8 us (75%)
  starting transfers between devices  18.4 us (15%)
  matrix products  5.62 us (5%)
  other arithmetic  2.32 us (2%)
  local copies, waits for them, and re-layouts  1.86 us (2%)
  Pallas kernels  1.7 us (1%)
    all_to_all x6, blocking collectives, exchange(): lax.all_to_all(blocks, axes, 0, 0, axis_index_groups=[ORDERS[axes]], tile...  92.8 us
    all_to_all x1, starting transfers between devices, exchange(): lax.all_to_all(blocks, axes, 0, 0, axis_index_groups=[ORDERS[axes]], tile...  12.5 us
    dot_general x1, matrix products, body(): jnp.dot(rows_x, freq_cols, preferred_element_type=jnp.float32)  4.16 us
    ppermute x1, starting transfers between devices, body(): rows_x = both(descriptors, lax.ppermute(descriptors, 'zl', swap))  4 us
  transfers between devices with their start and end apart: 3, of which 0 were waited for; matrix products, arithmetic and copies ran while one was open for 5% of the time, Pallas kernels for 0%

profile of v11, /device:TPU:1, one launch (start us, length us, event | category | flops | bytes accessed | tf_op | source)
XLA Modules:
  0.0 123.9 jit_solution(6971470104339300589)
XLA Ops:
  0.6 0.0 copy-start
  0.6 1.7 %shard_map.120 = bf16[32,64,128]{2,1,0:T(8,128)(2,1)} custom-call(f32[64,128]{1,0:T(8,128)} %direction_ref.1), custom_call_target="tpu_custom_call" | custom-call | bytes 557056 | tf_op jit(solution)/shard_map/pallas_call | solution.py:83
  2.3 12.5 %all-to-all-start = ((bf16[32,64,128]{2,1,0:T(8,128)(2,1)}), bf16[32,64,128]{2,1,0:T(8,128)(2,1)S(1)}, u32[]{:S(2)}, u32[]{:S(2)}) async-start(bf16[32,64,128]{2,1,0:T(8,128)(2,1)} %shard_map.120), calls=%async_computation | async-start | bytes 1048576 | tf_op jit(solution)/shard_map/all_to_all | solution.py:54
  14.8 4.0 %collective-permute-start = (bf16[256,128]{1,0:T(8,128)(2,1)}, bf16[256,128]{1,0:T(8,128)(2,1)}, u32[]{:S(2)}, u32[]{:S(2)}) collective-permute-start(bf16[256,128]{1,0:T(8,128)(2,1)} %param.9), channel_id=1, source_target_pairs={{0,64},{64,0},{1,65},{65,1},{2,66},{66,2},{3,67},{67,3},{4,68},{68... | collective-permute-start | bytes 196616 | tf_op jit(solution)/shard_map/ppermute | solution.py:93
  18.9 0.9 pad_maximum_fusion.2
  19.8 1.9 %collective-permute-start.1 = (f32[258,128]{1,0:T(8,128)S(1)}, f32[258,128]{1,0:T(8,128)S(1)}, u32[]{:S(2)}, u32[]{:S(2)}) collective-permute-start(f32[258,128]{1,0:T(8,128)S(1)} %pad_maximum_fusion.2), channel_id=1, source_target_pairs={{0,64},{64,0},{1,65},{65,1},{2,66},{66,2},{3,67},{67,3},{4,68},{68... | collective-permute-start | bytes 396296 | tf_op jit(solution)/shard_map/ppermute | solution.py:95
  21.7 0.0 copy-done
  21.7 0.7 copy.19
  22.5 0.2 copy.20
  22.7 0.0 copy-start.6
  22.7 0.0 copy-start.1
  22.7 0.0 copy-start.8
  22.7 0.0 copy-start.11
  22.9 0.3 copy.21
  23.1 0.3 copy-done.6
  23.4 0.0 copy-done.1
  23.5 0.0 copy-done.8
  23.5 0.0 collective-permute-done
  23.5 0.0 copy-done.11
  23.6 0.0 copy-start.7
  23.6 0.0 copy-start.3
  23.6 4.2 %add_convert_fusion = bf16[512,2048]{1,0:T(8,128)(2,1)S(1)} fusion(bf16[128,2048]{0,1:T(8,128)(2,1)S(1)} %bitcast.39, f32[2048]{0:T(1024)S(1)} %bitcast.45, bf16[256,128]{1,0:T(8,128)(2,1)} %collective-permute-done, bf16[256,128]{1,0:T(8,128)(2,1)S(1)} %copy-done.11, pred[]{:T(512)S(6)} %eq.18), kind=kOutput, calls=%fused_computation | convolution fusion | flops 291045376 | bytes 2760705 | tf_op jit(solution)/shard_map/dot_general | solution.py:104
  27.7 0.0 collective-permute-done.1
  27.8 0.0 copy-done.7
  27.8 0.0 copy-done.3
  27.8 0.2 abs_reduce_fusion.1
  28.0 0.0 all-to-all-done
  28.0 0.1 broadcast_in_dim.41
  28.1 0.7 fusion.18
  28.9 0.0 copy-start.9
  28.9 0.0 copy-start.5
  28.9 22.3 %all_to_all.35 = f32[16,40,128]{2,1,0:T(8,128)S(1)} all-to-all(f32[16,40,128]{2,1,0:T(8,128)S(1)} %pad_maximum_fusion.1), channel_id=1, replica_groups={{68,69,70,71,64,65,66,67,4,5,6,7,0,1,2,3},{76,77,78,79,72,73,74,75,12,1..., dimensions={0} | all-to-all | bytes 655360 | tf_op jit(solution)/shard_map/all_to_all | solution.py:54
  51.2 13.9 %all_to_all.36 = f32[16,32,128]{2,1,0:T(8,128)S(1)} all-to-all(f32[16,32,128]{2,1,0:T(8,128)S(1)} %broadcast_in_dim.43), channel_id=1, replica_groups={{68,69,70,71,64,65,66,67,4,5,6,7,0,1,2,3},{76,77,78,79,72,73,74,75,12,1..., dimensions={0} | all-to-all | bytes 524288 | tf_op jit(solution)/shard_map/all_to_all | solution.py:54
  65.2 0.1 abs_reduce_fusion
  65.3 11.3 %all_to_all.37 = f32[32,4,128]{2,1,0:T(4,128)S(1)} all-to-all(f32[32,4,128]{2,1,0:T(4,128)S(1)} %broadcast_in_dim.48), channel_id=1, replica_groups={{288,296,304,312,256,264,272,280,416,424,432,440,384,392,400,408,32,40,..., dimensions={0} | all-to-all | bytes 131072 | tf_op jit(solution)/shard_map/all_to_all | solution.py:54
  76.7 0.0 copy-done.9
  76.8 0.0 copy-start.2
  76.8 0.0 copy-done.5
  76.8 0.0 copy-start.4
  76.9 0.8 fusion
  77.7 0.0 copy-done.2
  77.7 20.9 %all_to_all.38 = f16[32,64,128]{2,1,0:T(8,128)(2,1)S(1)} all-to-all(f16[32,64,128]{2,1,0:T(8,128)(2,1)S(1)} %bitcast.34), channel_id=1, replica_groups={{288,296,304,312,256,264,272,280,416,424,432,440,384,392,400,408,32,40,..., dimensions={0} | all-to-all | bytes 1048576 | tf_op jit(solution)/shard_map/all_to_all | solution.py:54
  98.6 0.1 convert_reduce_fusion
  98.7 11.4 %all_to_all.39 = f32[32,1,128]{2,1,0:T(1,128)S(1)} all-to-all(f32[32,1,128]{2,1,0:T(1,128)S(1)} %broadcast_in_dim.49), channel_id=1, replica_groups={{288,296,304,312,256,264,272,280,416,424,432,440,384,392,400,408,32,40,..., dimensions={0} | all-to-all | bytes 32768 | tf_op jit(solution)/shard_map/all_to_all | solution.py:54
  110.1 13.1 %all_to_all.40 = f32[16,1,128]{2,1,0:T(1,128)S(1)} all-to-all(f32[16,1,128]{2,1,0:T(1,128)S(1)} %broadcast_in_dim.50), channel_id=1, replica_groups={{68,69,70,71,64,65,66,67,4,5,6,7,0,1,2,3},{76,77,78,79,72,73,74,75,12,1..., dimensions={0} | all-to-all | bytes 16384 | tf_op jit(solution)/shard_map/all_to_all | solution.py:54
  123.2 0.0 copy-start.10
  123.2 0.0 copy-done.4
  123.2 0.6 multiply_add_fusion
  123.9 0.0 copy-done.10
  (39 shorter events, 0.7 us)
Async XLA Ops:
  0.6 21.1 %copy-start = (bf16[128,4096]{1,0:T(8,128)(2,1)S(1)}, bf16[128,4096]{1,0:T(8,128)(2,1)}, u32[]{:S(2)}) copy-start(bf16[128,4096]{1,0:T(8,128)(2,1)} %param.10) | copy-start | bytes 3145732
  2.3 25.6 %all-to-all-start = ((bf16[32,64,128]{2,1,0:T(8,128)(2,1)}), bf16[32,64,128]{2,1,0:T(8,128)(2,1)S(1)}, u32[]{:S(2)}, u32[]{:S(2)}) async-start(bf16[32,64,128]{2,1,0:T(8,128)(2,1)} %shard_map.120), calls=%async_computation | async-start | bytes 1048576 | tf_op jit(solution)/shard_map/all_to_all | solution.py:54
  14.8 8.7 %collective-permute-start = (bf16[256,128]{1,0:T(8,128)(2,1)}, bf16[256,128]{1,0:T(8,128)(2,1)}, u32[]{:S(2)}, u32[]{:S(2)}) collective-permute-start(bf16[256,128]{1,0:T(8,128)(2,1)} %param.9), channel_id=1, source_target_pairs={{0,64},{64,0},{1,65},{65,1},{2,66},{66,2},{3,67},{67,3},{4,68},{68... | collective-permute-start | bytes 196616 | tf_op jit(solution)/shard_map/ppermute | solution.py:93
  19.8 8.0 %collective-permute-start.1 = (f32[258,128]{1,0:T(8,128)S(1)}, f32[258,128]{1,0:T(8,128)S(1)}, u32[]{:S(2)}, u32[]{:S(2)}) collective-permute-start(f32[258,128]{1,0:T(8,128)S(1)} %pad_maximum_fusion.2), channel_id=1, source_target_pairs={{0,64},{64,0},{1,65},{65,1},{2,66},{66,2},{3,67},{67,3},{4,68},{68... | collective-permute-start | bytes 396296 | tf_op jit(solution)/shard_map/ppermute | solution.py:95
  22.7 0.7 copy-start.6
  22.7 0.8 copy-start.1
  22.7 0.8 copy-start.8
  22.7 0.9 copy-start.11
  23.6 4.2 %copy-start.7 = (f32[256]{0:T(256)S(1)}, f32[256]{0:T(256)}, u32[]{:S(2)}) copy-start(f32[256]{0:T(256)} %param.12) | copy-start | bytes 3076
  23.6 4.2 %copy-start.3 = (f32[256,128]{1,0:T(8,128)S(1)}, f32[256,128]{1,0:T(8,128)}, u32[]{:S(2)}) copy-start(f32[256,128]{1,0:T(8,128)} %param.13) | copy-start | bytes 393220
  28.9 47.9 %copy-start.9 = (f32[128]{0:T(128)S(1)}, f32[128]{0:T(128)}, u32[]{:S(2)}) copy-start(f32[128]{0:T(128)} %param.17) | copy-start | bytes 1540
  28.9 47.9 %copy-start.5 = (f32[64,128]{1,0:T(8,128)S(1)}, f32[64,128]{1,0:T(8,128)}, u32[]{:S(2)}) copy-start(f32[64,128]{1,0:T(8,128)} %param.14) | copy-start | bytes 98308
  76.8 0.9 copy-start.2
  76.8 46.4 %copy-start.4 = (f32[64,128]{1,0:T(8,128)}, f32[64,128]{1,0:T(8,128)S(1)}, u32[]{:S(2)}) copy-start(f32[64,128]{1,0:T(8,128)S(1)} %multiply_add_fusion.1) | copy-start | bytes 98308
  123.2 0.7 copy-start.10

commit v12 on v9

--- a/solution.py
+++ b/solution.py
@@ -19,8 +19,6 @@
 
 SCALE = 2.0**-7
 TURN = 1.0 / (2.0 * np.pi)
-TURN_HI = 6.28125
-TURN_LO = 2.0 * np.pi - 6.28125
 COS = (
     1.0,
     -0.49999988079071045,
@@ -31,17 +29,18 @@
     1.7231808202566867e-09,
 )
 
+TURN_COS = [c * SCALE * (2.0 * np.pi) ** (2 * i) for i, c in enumerate(COS)]
 TERM_MAX = 32000.0
 TINY = 1e-30
 
 
 def scaled_cos(angle):
-    turns = jnp.round(angle * jnp.float32(TURN))
-    rest = (angle - turns * jnp.float32(TURN_HI)) - turns * jnp.float32(TURN_LO)
+    turns = angle * jnp.float32(TURN)
+    rest = turns - jnp.round(turns)
     square = rest * rest
-    value = jnp.float32(COS[-1] * SCALE)
-    for c in COS[-2::-1]:
-        value = value * square + jnp.float32(c * SCALE)
+    value = jnp.float32(TURN_COS[-1])
+    for c in TURN_COS[-2::-1]:
+        value = value * square + jnp.float32(c)
     return value
 
 

time: 124 us -> 123 us (level)
  no operation moved by 1% of the time
where the time goes in v12:
time: 123 us; the launch traced here: 122 us
  blocking collectives  91.6 us (74%)
  starting transfers between devices  18.4 us (15%)
  matrix products  5.25 us (4%)
  other arithmetic  2.32 us (2%)
  local copies, waits for them, and re-layouts  1.86 us (2%)
  Pallas kernels  1.7 us (1%)
    all_to_all x6, blocking collectives, exchange(): lax.all_to_all(blocks, axes, 0, 0, axis_index_groups=[ORDERS[axes]], tile...  91.6 us
    all_to_all x1, starting transfers between devices, exchange(): lax.all_to_all(blocks, axes, 0, 0, axis_index_groups=[ORDERS[axes]], tile...  12.5 us
    ppermute x1, starting transfers between devices, body(): rows_x = both(descriptors, lax.ppermute(descriptors, 'zl', swap))  4 us
    dot_general x1, matrix products, body(): jnp.dot(rows_x, freq_cols, preferred_element_type=jnp.float32)  3.78 us
  transfers between devices with their start and end apart: 3, of which 0 were waited for; matrix products, arithmetic and copies ran while one was open for 5% of the time, Pallas kernels for 0%

profile of v12, /device:TPU:1, one launch (start us, length us, event | category | flops | bytes accessed | tf_op | source)
XLA Modules:
  0.0 122.3 jit_solution(1287663261661985698)
XLA Ops:
  0.6 0.0 copy-start
  0.6 1.7 %shard_map.120 = bf16[32,64,128]{2,1,0:T(8,128)(2,1)} custom-call(f32[64,128]{1,0:T(8,128)} %direction_ref.1), custom_call_target="tpu_custom_call" | custom-call | bytes 557056 | tf_op jit(solution)/shard_map/pallas_call | solution.py:82
  2.3 12.5 %all-to-all-start = ((bf16[32,64,128]{2,1,0:T(8,128)(2,1)}), bf16[32,64,128]{2,1,0:T(8,128)(2,1)S(1)}, u32[]{:S(2)}, u32[]{:S(2)}) async-start(bf16[32,64,128]{2,1,0:T(8,128)(2,1)} %shard_map.120), calls=%async_computation | async-start | bytes 1048576 | tf_op jit(solution)/shard_map/all_to_all | solution.py:53
  14.8 4.0 %collective-permute-start = (bf16[256,128]{1,0:T(8,128)(2,1)}, bf16[256,128]{1,0:T(8,128)(2,1)}, u32[]{:S(2)}, u32[]{:S(2)}) collective-permute-start(bf16[256,128]{1,0:T(8,128)(2,1)} %param.9), channel_id=1, source_target_pairs={{0,64},{64,0},{1,65},{65,1},{2,66},{66,2},{3,67},{67,3},{4,68},{68... | collective-permute-start | bytes 196616 | tf_op jit(solution)/shard_map/ppermute | solution.py:92
  18.9 0.9 pad_maximum_fusion.2
  19.8 1.9 %collective-permute-start.1 = (f32[258,128]{1,0:T(8,128)S(1)}, f32[258,128]{1,0:T(8,128)S(1)}, u32[]{:S(2)}, u32[]{:S(2)}) collective-permute-start(f32[258,128]{1,0:T(8,128)S(1)} %pad_maximum_fusion.2), channel_id=1, source_target_pairs={{0,64},{64,0},{1,65},{65,1},{2,66},{66,2},{3,67},{67,3},{4,68},{68... | collective-permute-start | bytes 396296 | tf_op jit(solution)/shard_map/ppermute | solution.py:94
  21.7 0.0 copy-done
  21.7 0.7 copy.19
  22.5 0.2 copy.20
  22.7 0.0 copy-start.6
  22.7 0.0 copy-start.1
  22.7 0.0 copy-start.8
  22.7 0.0 copy-start.11
  22.9 0.3 copy.21
  23.1 0.3 copy-done.6
  23.4 0.0 copy-done.1
  23.5 0.0 copy-done.8
  23.5 0.0 collective-permute-done
  23.5 0.0 copy-done.11
  23.6 0.0 copy-start.7
  23.6 0.0 copy-start.3
  23.6 3.8 %add_convert_fusion = bf16[512,2048]{1,0:T(8,128)(2,1)S(1)} fusion(bf16[128,2048]{0,1:T(8,128)(2,1)S(1)} %bitcast.39, f32[2048]{0:T(1024)S(1)} %bitcast.45, bf16[256,128]{1,0:T(8,128)(2,1)} %collective-permute-done, bf16[256,128]{1,0:T(8,128)(2,1)S(1)} %copy-done.11, pred[]{:T(512)S(6)} %eq.18), kind=kOutput, calls=%fused_computation.2 | convolution fusion | flops 287899648 | bytes 2760705 | tf_op jit(solution)/shard_map/dot_general | solution.py:103
  27.4 0.0 collective-permute-done.1
  27.4 0.0 copy-done.7
  27.4 0.0 copy-done.3
  27.4 0.2 abs_reduce_fusion.1
  27.6 0.0 all-to-all-done
  27.6 0.1 broadcast_in_dim.41
  27.8 0.7 fusion.19
  28.5 0.0 copy-start.9
  28.5 0.0 copy-start.5
  28.5 22.3 %all_to_all.35 = f32[16,40,128]{2,1,0:T(8,128)S(1)} all-to-all(f32[16,40,128]{2,1,0:T(8,128)S(1)} %pad_maximum_fusion.1), channel_id=1, replica_groups={{68,69,70,71,64,65,66,67,4,5,6,7,0,1,2,3},{76,77,78,79,72,73,74,75,12,1..., dimensions={0} | all-to-all | bytes 655360 | tf_op jit(solution)/shard_map/all_to_all | solution.py:53
  50.9 13.9 %all_to_all.36 = f32[16,32,128]{2,1,0:T(8,128)S(1)} all-to-all(f32[16,32,128]{2,1,0:T(8,128)S(1)} %broadcast_in_dim.43), channel_id=1, replica_groups={{68,69,70,71,64,65,66,67,4,5,6,7,0,1,2,3},{76,77,78,79,72,73,74,75,12,1..., dimensions={0} | all-to-all | bytes 524288 | tf_op jit(solution)/shard_map/all_to_all | solution.py:53
  64.8 0.1 abs_reduce_fusion
  64.9 11.6 %all_to_all.37 = f32[32,4,128]{2,1,0:T(4,128)S(1)} all-to-all(f32[32,4,128]{2,1,0:T(4,128)S(1)} %broadcast_in_dim.48), channel_id=1, replica_groups={{288,296,304,312,256,264,272,280,416,424,432,440,384,392,400,408,32,40,..., dimensions={0} | all-to-all | bytes 131072 | tf_op jit(solution)/shard_map/all_to_all | solution.py:53
  76.6 0.0 copy-done.9
  76.7 0.0 copy-start.2
  76.7 0.0 copy-done.5
  76.7 0.0 copy-start.4
  76.8 0.8 fusion.1
  77.5 0.0 copy-done.2
  77.5 20.9 %all_to_all.38 = f16[32,64,128]{2,1,0:T(8,128)(2,1)S(1)} all-to-all(f16[32,64,128]{2,1,0:T(8,128)(2,1)S(1)} %bitcast.34), channel_id=1, replica_groups={{288,296,304,312,256,264,272,280,416,424,432,440,384,392,400,408,32,40,..., dimensions={0} | all-to-all | bytes 1048576 | tf_op jit(solution)/shard_map/all_to_all | solution.py:53
  98.4 0.1 convert_reduce_fusion
  98.6 11.3 %all_to_all.39 = f32[16,1,128]{2,1,0:T(1,128)S(1)} all-to-all(f32[16,1,128]{2,1,0:T(1,128)S(1)} %broadcast_in_dim.49), channel_id=1, replica_groups={{68,69,70,71,64,65,66,67,4,5,6,7,0,1,2,3},{76,77,78,79,72,73,74,75,12,1..., dimensions={0} | all-to-all | bytes 16384 | tf_op jit(solution)/shard_map/all_to_all | solution.py:53
  109.8 11.8 %all_to_all.40 = f32[32,1,128]{2,1,0:T(1,128)S(1)} all-to-all(f32[32,1,128]{2,1,0:T(1,128)S(1)} %broadcast_in_dim.50), channel_id=1, replica_groups={{288,296,304,312,256,264,272,280,416,424,432,440,384,392,400,408,32,40,..., dimensions={0} | all-to-all | bytes 32768 | tf_op jit(solution)/shard_map/all_to_all | solution.py:53
  121.6 0.0 copy-start.10
  121.6 0.0 copy-done.4
  121.7 0.6 multiply_add_fusion
  122.3 0.0 copy-done.10
  (39 shorter events, 0.7 us)
Async XLA Ops:
  0.6 21.1 %copy-start = (bf16[128,4096]{1,0:T(8,128)(2,1)S(1)}, bf16[128,4096]{1,0:T(8,128)(2,1)}, u32[]{:S(2)}) copy-start(bf16[128,4096]{1,0:T(8,128)(2,1)} %param.10) | copy-start | bytes 3145732
  2.3 25.3 %all-to-all-start = ((bf16[32,64,128]{2,1,0:T(8,128)(2,1)}), bf16[32,64,128]{2,1,0:T(8,128)(2,1)S(1)}, u32[]{:S(2)}, u32[]{:S(2)}) async-start(bf16[32,64,128]{2,1,0:T(8,128)(2,1)} %shard_map.120), calls=%async_computation | async-start | bytes 1048576 | tf_op jit(solution)/shard_map/all_to_all | solution.py:53
  14.8 8.7 %collective-permute-start = (bf16[256,128]{1,0:T(8,128)(2,1)}, bf16[256,128]{1,0:T(8,128)(2,1)}, u32[]{:S(2)}, u32[]{:S(2)}) collective-permute-start(bf16[256,128]{1,0:T(8,128)(2,1)} %param.9), channel_id=1, source_target_pairs={{0,64},{64,0},{1,65},{65,1},{2,66},{66,2},{3,67},{67,3},{4,68},{68... | collective-permute-start | bytes 196616 | tf_op jit(solution)/shard_map/ppermute | solution.py:92
  19.8 7.6 %collective-permute-start.1 = (f32[258,128]{1,0:T(8,128)S(1)}, f32[258,128]{1,0:T(8,128)S(1)}, u32[]{:S(2)}, u32[]{:S(2)}) collective-permute-start(f32[258,128]{1,0:T(8,128)S(1)} %pad_maximum_fusion.2), channel_id=1, source_target_pairs={{0,64},{64,0},{1,65},{65,1},{2,66},{66,2},{3,67},{67,3},{4,68},{68... | collective-permute-start | bytes 396296 | tf_op jit(solution)/shard_map/ppermute | solution.py:94
  22.7 0.7 copy-start.6
  22.7 0.8 copy-start.1
  22.7 0.8 copy-start.8
  22.7 0.9 copy-start.11
  23.6 3.8 %copy-start.7 = (f32[256]{0:T(256)S(1)}, f32[256]{0:T(256)}, u32[]{:S(2)}) copy-start(f32[256]{0:T(256)} %param.12) | copy-start | bytes 3076
  23.6 3.9 %copy-start.3 = (f32[256,128]{1,0:T(8,128)S(1)}, f32[256,128]{1,0:T(8,128)}, u32[]{:S(2)}) copy-start(f32[256,128]{1,0:T(8,128)} %param.13) | copy-start | bytes 393220
  28.5 48.1 %copy-start.9 = (f32[128]{0:T(128)S(1)}, f32[128]{0:T(128)}, u32[]{:S(2)}) copy-start(f32[128]{0:T(128)} %param.17) | copy-start | bytes 1540
  28.5 48.2 %copy-start.5 = (f32[64,128]{1,0:T(8,128)S(1)}, f32[64,128]{1,0:T(8,128)}, u32[]{:S(2)}) copy-start(f32[64,128]{1,0:T(8,128)} %param.14) | copy-start | bytes 98308
  76.7 0.9 copy-start.2
  76.7 44.9 %copy-start.4 = (f32[64,128]{1,0:T(8,128)}, f32[64,128]{1,0:T(8,128)S(1)}, u32[]{:S(2)}) copy-start(f32[64,128]{1,0:T(8,128)S(1)} %multiply_add_fusion.1) | copy-start | bytes 98308
  121.6 0.7 copy-start.10

commit v13 on v9

--- a/solution.py
+++ b/solution.py
@@ -11,7 +11,7 @@
 FEAT = ("zh", "core")
 PLANE = ("x", "y")
 COLUMN = ("zl", "zh", "core")
-LATE_ZL, LATE_ZH = 1, 2
+LATE_ZL, LATE_ZH = 0, 3
 
 PLANE_ORDER = [((x + 2) % 4) * 8 + (y + 4) % 8 for x in range(4) for y in range(8)]
 COLUMN_ORDER = [((i // 8 + LATE_ZL) % 2) * 8 + ((i // 2 + LATE_ZH) % 4) * 2 + i % 2 for i in range(16)]

time: 124 us -> 124 us (level)
  no operation moved by 1% of the time
where the time goes in v13:
time: 124 us; the launch traced here: 123 us
  blocking collectives  91.7 us (74%)
  starting transfers between devices  18.4 us (15%)
  matrix products  5.63 us (5%)
  other arithmetic  2.32 us (2%)
  local copies, waits for them, and re-layouts  1.86 us (2%)
  Pallas kernels  1.7 us (1%)
    all_to_all x6, blocking collectives, exchange(): lax.all_to_all(blocks, axes, 0, 0, axis_index_groups=[ORDERS[axes]], tile...  91.7 us
    all_to_all x1, starting transfers between devices, exchange(): lax.all_to_all(blocks, axes, 0, 0, axis_index_groups=[ORDERS[axes]], tile...  12.5 us
    dot_general x1, matrix products, body(): jnp.dot(rows_x, freq_cols, preferred_element_type=jnp.float32)  4.16 us
    ppermute x1, starting transfers between devices, body(): rows_x = both(descriptors, lax.ppermute(descriptors, 'zl', swap))  4 us
  transfers between devices with their start and end apart: 3, of which 0 were waited for; matrix products, arithmetic and copies ran while one was open for 5% of the time, Pallas kernels for 0%

profile of v13, /device:TPU:1, one launch (start us, length us, event | category | flops | bytes accessed | tf_op | source)
XLA Modules:
  0.0 122.7 jit_solution(4435508269104209830)
XLA Ops:
  0.6 0.0 copy-start
  0.6 1.7 %shard_map.120 = bf16[32,64,128]{2,1,0:T(8,128)(2,1)} custom-call(f32[64,128]{1,0:T(8,128)} %direction_ref.1), custom_call_target="tpu_custom_call" | custom-call | bytes 557056 | tf_op jit(solution)/shard_map/pallas_call | solution.py:83
  2.3 12.5 %all-to-all-start = ((bf16[32,64,128]{2,1,0:T(8,128)(2,1)}), bf16[32,64,128]{2,1,0:T(8,128)(2,1)S(1)}, u32[]{:S(2)}, u32[]{:S(2)}) async-start(bf16[32,64,128]{2,1,0:T(8,128)(2,1)} %shard_map.120), calls=%async_computation | async-start | bytes 1048576 | tf_op jit(solution)/shard_map/all_to_all | solution.py:54
  14.8 4.0 %collective-permute-start = (bf16[256,128]{1,0:T(8,128)(2,1)}, bf16[256,128]{1,0:T(8,128)(2,1)}, u32[]{:S(2)}, u32[]{:S(2)}) collective-permute-start(bf16[256,128]{1,0:T(8,128)(2,1)} %param.9), channel_id=1, source_target_pairs={{0,64},{64,0},{1,65},{65,1},{2,66},{66,2},{3,67},{67,3},{4,68},{68... | collective-permute-start | bytes 196616 | tf_op jit(solution)/shard_map/ppermute | solution.py:93
  18.9 0.9 pad_maximum_fusion.2
  19.8 1.9 %collective-permute-start.1 = (f32[258,128]{1,0:T(8,128)S(1)}, f32[258,128]{1,0:T(8,128)S(1)}, u32[]{:S(2)}, u32[]{:S(2)}) collective-permute-start(f32[258,128]{1,0:T(8,128)S(1)} %pad_maximum_fusion.2), channel_id=1, source_target_pairs={{0,64},{64,0},{1,65},{65,1},{2,66},{66,2},{3,67},{67,3},{4,68},{68... | collective-permute-start | bytes 396296 | tf_op jit(solution)/shard_map/ppermute | solution.py:95
  21.7 0.0 copy-done
  21.7 0.7 copy.19
  22.5 0.2 copy.20
  22.7 0.0 copy-start.6
  22.7 0.0 copy-start.1
  22.7 0.0 copy-start.8
  22.7 0.0 copy-start.11
  22.9 0.3 copy.21
  23.1 0.3 copy-done.6
  23.4 0.0 copy-done.1
  23.5 0.0 copy-done.8
  23.5 0.0 collective-permute-done
  23.5 0.0 copy-done.11
  23.6 0.0 copy-start.7
  23.6 0.0 copy-start.3
  23.6 4.2 %add_convert_fusion = bf16[512,2048]{1,0:T(8,128)(2,1)S(1)} fusion(bf16[128,2048]{0,1:T(8,128)(2,1)S(1)} %bitcast.39, f32[2048]{0:T(1024)S(1)} %bitcast.45, bf16[256,128]{1,0:T(8,128)(2,1)} %collective-permute-done, bf16[256,128]{1,0:T(8,128)(2,1)S(1)} %copy-done.11, pred[]{:T(512)S(6)} %eq.18), kind=kOutput, calls=%fused_computation | convolution fusion | flops 291045376 | bytes 2760705 | tf_op jit(solution)/shard_map/dot_general | solution.py:104
  27.7 0.0 collective-permute-done.1
  27.8 0.0 copy-done.7
  27.8 0.0 copy-done.3
  27.8 0.2 abs_reduce_fusion.1
  28.0 0.0 all-to-all-done
  28.0 0.1 broadcast_in_dim.41
  28.1 0.7 fusion.18
  28.9 0.0 copy-start.9
  28.9 0.0 copy-start.5
  28.9 22.5 %all_to_all.35 = f32[16,40,128]{2,1,0:T(8,128)S(1)} all-to-all(f32[16,40,128]{2,1,0:T(8,128)S(1)} %pad_maximum_fusion.1), channel_id=1, replica_groups={{6,7,0,1,2,3,4,5,70,71,64,65,66,67,68,69},{14,15,8,9,10,11,12,13,78,79,..., dimensions={0} | all-to-all | bytes 655360 | tf_op jit(solution)/shard_map/all_to_all | solution.py:54
  51.5 14.2 %all_to_all.36 = f32[16,32,128]{2,1,0:T(8,128)S(1)} all-to-all(f32[16,32,128]{2,1,0:T(8,128)S(1)} %broadcast_in_dim.43), channel_id=1, replica_groups={{6,7,0,1,2,3,4,5,70,71,64,65,66,67,68,69},{14,15,8,9,10,11,12,13,78,79,..., dimensions={0} | all-to-all | bytes 524288 | tf_op jit(solution)/shard_map/all_to_all | solution.py:54
  65.7 0.1 abs_reduce_fusion
  65.8 11.4 %all_to_all.37 = f32[32,4,128]{2,1,0:T(4,128)S(1)} all-to-all(f32[32,4,128]{2,1,0:T(4,128)S(1)} %broadcast_in_dim.48), channel_id=1, replica_groups={{288,296,304,312,256,264,272,280,416,424,432,440,384,392,400,408,32,40,..., dimensions={0} | all-to-all | bytes 131072 | tf_op jit(solution)/shard_map/all_to_all | solution.py:54
  77.4 0.0 copy-done.9
  77.5 0.0 copy-start.2
  77.5 0.0 copy-done.5
  77.5 0.0 copy-start.4
  77.6 0.8 fusion
  78.3 0.0 copy-done.2
  78.4 21.4 %all_to_all.38 = f16[32,64,128]{2,1,0:T(8,128)(2,1)S(1)} all-to-all(f16[32,64,128]{2,1,0:T(8,128)(2,1)S(1)} %bitcast.34), channel_id=1, replica_groups={{288,296,304,312,256,264,272,280,416,424,432,440,384,392,400,408,32,40,..., dimensions={0} | all-to-all | bytes 1048576 | tf_op jit(solution)/shard_map/all_to_all | solution.py:54
  99.8 0.1 convert_reduce_fusion
  99.9 10.4 %all_to_all.39 = f32[16,1,128]{2,1,0:T(1,128)S(1)} all-to-all(f32[16,1,128]{2,1,0:T(1,128)S(1)} %broadcast_in_dim.49), channel_id=1, replica_groups={{6,7,0,1,2,3,4,5,70,71,64,65,66,67,68,69},{14,15,8,9,10,11,12,13,78,79,..., dimensions={0} | all-to-all | bytes 16384 | tf_op jit(solution)/shard_map/all_to_all | solution.py:54
  110.4 11.7 %all_to_all.40 = f32[32,1,128]{2,1,0:T(1,128)S(1)} all-to-all(f32[32,1,128]{2,1,0:T(1,128)S(1)} %broadcast_in_dim.50), channel_id=1, replica_groups={{288,296,304,312,256,264,272,280,416,424,432,440,384,392,400,408,32,40,..., dimensions={0} | all-to-all | bytes 32768 | tf_op jit(solution)/shard_map/all_to_all | solution.py:54
  122.1 0.0 copy-start.10
  122.1 0.0 copy-done.4
  122.1 0.6 multiply_add_fusion
  122.7 0.0 copy-done.10
  (39 shorter events, 0.7 us)
Async XLA Ops:
  0.6 21.1 %copy-start = (bf16[128,4096]{1,0:T(8,128)(2,1)S(1)}, bf16[128,4096]{1,0:T(8,128)(2,1)}, u32[]{:S(2)}) copy-start(bf16[128,4096]{1,0:T(8,128)(2,1)} %param.10) | copy-start | bytes 3145732
  2.3 25.6 %all-to-all-start = ((bf16[32,64,128]{2,1,0:T(8,128)(2,1)}), bf16[32,64,128]{2,1,0:T(8,128)(2,1)S(1)}, u32[]{:S(2)}, u32[]{:S(2)}) async-start(bf16[32,64,128]{2,1,0:T(8,128)(2,1)} %shard_map.120), calls=%async_computation | async-start | bytes 1048576 | tf_op jit(solution)/shard_map/all_to_all | solution.py:54
  14.8 8.7 %collective-permute-start = (bf16[256,128]{1,0:T(8,128)(2,1)}, bf16[256,128]{1,0:T(8,128)(2,1)}, u32[]{:S(2)}, u32[]{:S(2)}) collective-permute-start(bf16[256,128]{1,0:T(8,128)(2,1)} %param.9), channel_id=1, source_target_pairs={{0,64},{64,0},{1,65},{65,1},{2,66},{66,2},{3,67},{67,3},{4,68},{68... | collective-permute-start | bytes 196616 | tf_op jit(solution)/shard_map/ppermute | solution.py:93
  19.8 8.0 %collective-permute-start.1 = (f32[258,128]{1,0:T(8,128)S(1)}, f32[258,128]{1,0:T(8,128)S(1)}, u32[]{:S(2)}, u32[]{:S(2)}) collective-permute-start(f32[258,128]{1,0:T(8,128)S(1)} %pad_maximum_fusion.2), channel_id=1, source_target_pairs={{0,64},{64,0},{1,65},{65,1},{2,66},{66,2},{3,67},{67,3},{4,68},{68... | collective-permute-start | bytes 396296 | tf_op jit(solution)/shard_map/ppermute | solution.py:95
  22.7 0.7 copy-start.6
  22.7 0.8 copy-start.1
  22.7 0.8 copy-start.8
  22.7 0.9 copy-start.11
  23.6 4.2 %copy-start.7 = (f32[256]{0:T(256)S(1)}, f32[256]{0:T(256)}, u32[]{:S(2)}) copy-start(f32[256]{0:T(256)} %param.12) | copy-start | bytes 3076
  23.6 4.2 %copy-start.3 = (f32[256,128]{1,0:T(8,128)S(1)}, f32[256,128]{1,0:T(8,128)}, u32[]{:S(2)}) copy-start(f32[256,128]{1,0:T(8,128)} %param.13) | copy-start | bytes 393220
  28.9 48.5 %copy-start.9 = (f32[128]{0:T(128)S(1)}, f32[128]{0:T(128)}, u32[]{:S(2)}) copy-start(f32[128]{0:T(128)} %param.17) | copy-start | bytes 1540
  28.9 48.6 %copy-start.5 = (f32[64,128]{1,0:T(8,128)S(1)}, f32[64,128]{1,0:T(8,128)}, u32[]{:S(2)}) copy-start(f32[64,128]{1,0:T(8,128)} %param.14) | copy-start | bytes 98308
  77.5 0.9 copy-start.2
  77.5 44.6 %copy-start.4 = (f32[64,128]{1,0:T(8,128)}, f32[64,128]{1,0:T(8,128)S(1)}, u32[]{:S(2)}) copy-start(f32[64,128]{1,0:T(8,128)S(1)} %multiply_add_fusion.1) | copy-start | bytes 98308
  122.1 0.7 copy-start.10

commit v14 on v9

--- a/solution.py
+++ b/solution.py
@@ -13,7 +13,7 @@
 COLUMN = ("zl", "zh", "core")
 LATE_ZL, LATE_ZH = 1, 2
 
-PLANE_ORDER = [((x + 2) % 4) * 8 + (y + 4) % 8 for x in range(4) for y in range(8)]
+PLANE_ORDER = [((x + 1) % 4) * 8 + (y + 4) % 8 for x in range(4) for y in range(8)]
 COLUMN_ORDER = [((i // 8 + LATE_ZL) % 2) * 8 + ((i // 2 + LATE_ZH) % 4) * 2 + i % 2 for i in range(16)]
 ORDERS = {PLANE: PLANE_ORDER, COLUMN: COLUMN_ORDER}
 
@@ -65,7 +65,7 @@
 
 
 def listed(cols, own):
-    cols = jnp.roll(cols, -2, axis=1)
+    cols = jnp.roll(cols, -1, axis=1)
     return jnp.roll(cols, -4 * own, axis=2).reshape(cols.shape[0], -1)
 
 

time: 124 us -> 124 us (level)
  blocking collectives: 91.4 us -> 93.1 us
  starting transfers between devices: 18.4 us -> 17 us
    all_to_all x6, blocking collectives: 91.4 us -> 93.1 us  [exchange(): lax.all_to_all(blocks, axes, 0, 0, axis_index_groups=[ORDERS[axes]], tile...]
    all_to_all x1, starting transfers between devices: 12.5 us -> 11 us  [exchange(): lax.all_to_all(blocks, axes, 0, 0, axis_index_groups=[ORDERS[axes]], tile...]
where the time goes in v14:
time: 124 us; the launch traced here: 123 us
  blocking collectives  93.1 us (75%)
  starting transfers between devices  17 us (14%)
  matrix products  5.68 us (5%)
  other arithmetic  2.33 us (2%)
  local copies, waits for them, and re-layouts  1.91 us (2%)
  Pallas kernels  1.7 us (1%)
    all_to_all x6, blocking collectives, exchange(): lax.all_to_all(blocks, axes, 0, 0, axis_index_groups=[ORDERS[axes]], tile...  93.1 us
    all_to_all x1, starting transfers between devices, exchange(): lax.all_to_all(blocks, axes, 0, 0, axis_index_groups=[ORDERS[axes]], tile...  11 us
    dot_general x1, matrix products, body(): jnp.dot(rows_x, freq_cols, preferred_element_type=jnp.float32)  4.21 us
    ppermute x1, starting transfers between devices, body(): rows_x = both(descriptors, lax.ppermute(descriptors, 'zl', swap))  4 us
  transfers between devices with their start and end apart: 3, of which 0 were waited for; matrix products, arithmetic and copies ran while one was open for 5% of the time, Pallas kernels for 0%

profile of v14, /device:TPU:1, one launch (start us, length us, event | category | flops | bytes accessed | tf_op | source)
XLA Modules:
  0.0 122.8 jit_solution(7892085476883593761)
XLA Ops:
  0.6 0.0 copy-start
  0.6 1.7 %shard_map.120 = bf16[32,64,128]{2,1,0:T(8,128)(2,1)} custom-call(f32[64,128]{1,0:T(8,128)} %direction_ref.1), custom_call_target="tpu_custom_call" | custom-call | bytes 557056 | tf_op jit(solution)/shard_map/pallas_call | solution.py:83
  2.3 11.0 %all-to-all-start = ((bf16[32,64,128]{2,1,0:T(8,128)(2,1)}), bf16[32,64,128]{2,1,0:T(8,128)(2,1)S(1)}, u32[]{:S(2)}, u32[]{:S(2)}) async-start(bf16[32,64,128]{2,1,0:T(8,128)(2,1)} %shard_map.120), calls=%async_computation | async-start | bytes 1048576 | tf_op jit(solution)/shard_map/all_to_all | solution.py:54
  13.4 4.0 %collective-permute-start = (bf16[256,128]{1,0:T(8,128)(2,1)}, bf16[256,128]{1,0:T(8,128)(2,1)}, u32[]{:S(2)}, u32[]{:S(2)}) collective-permute-start(bf16[256,128]{1,0:T(8,128)(2,1)} %param.9), channel_id=1, source_target_pairs={{0,64},{64,0},{1,65},{65,1},{2,66},{66,2},{3,67},{67,3},{4,68},{68... | collective-permute-start | bytes 196616 | tf_op jit(solution)/shard_map/ppermute | solution.py:93
  17.4 0.9 pad_maximum_fusion.2
  18.3 1.9 %collective-permute-start.1 = (f32[258,128]{1,0:T(8,128)S(1)}, f32[258,128]{1,0:T(8,128)S(1)}, u32[]{:S(2)}, u32[]{:S(2)}) collective-permute-start(f32[258,128]{1,0:T(8,128)S(1)} %pad_maximum_fusion.2), channel_id=1, source_target_pairs={{0,64},{64,0},{1,65},{65,1},{2,66},{66,2},{3,67},{67,3},{4,68},{68... | collective-permute-start | bytes 396296 | tf_op jit(solution)/shard_map/ppermute | solution.py:95
  20.3 0.0 copy-done
  20.3 0.7 copy.19
  20.9 0.0 copy-start.6
  21.0 0.2 copy.20
  21.2 0.0 copy-start.1
  21.2 0.0 copy-start.8
  21.3 0.4 copy-done.6
  21.8 0.3 copy.21
  22.1 0.0 copy-done.1
  22.1 0.0 copy-done.8
  22.2 0.0 collective-permute-done
  22.2 0.0 copy-start.7
  22.2 0.0 copy-start.3
  22.2 4.2 %add_convert_fusion = bf16[512,2048]{1,0:T(8,128)(2,1)S(1)} fusion(bf16[128,2048]{0,1:T(8,128)(2,1)S(1)} %bitcast.40, f32[2048]{0:T(1024)S(1)} %bitcast.46, bf16[256,128]{1,0:T(8,128)(2,1)} %collective-permute-done, bf16[256,128]{1,0:T(8,128)(2,1)} %param.9, pred[]{:T(512)S(6)} %eq.18), kind=kOutput, calls=%fused_computation | convolution fusion | flops 291045376 | bytes 2760705 | tf_op jit(solution)/shard_map/dot_general | solution.py:104
  26.4 0.0 collective-permute-done.1
  26.5 0.0 copy-done.7
  26.5 0.0 copy-done.3
  26.5 0.2 abs_reduce_fusion.1
  26.6 0.0 all-to-all-done
  26.6 0.1 broadcast_in_dim.41
  26.8 0.7 fusion.16
  27.5 0.0 copy-start.9
  27.6 0.0 copy-start.5
  27.6 22.5 %all_to_all.35 = f32[16,40,128]{2,1,0:T(8,128)S(1)} all-to-all(f32[16,40,128]{2,1,0:T(8,128)S(1)} %pad_maximum_fusion.1), channel_id=1, replica_groups={{68,69,70,71,64,65,66,67,4,5,6,7,0,1,2,3},{76,77,78,79,72,73,74,75,12,1..., dimensions={0} | all-to-all | bytes 655360 | tf_op jit(solution)/shard_map/all_to_all | solution.py:54
  50.1 13.9 %all_to_all.36 = f32[16,32,128]{2,1,0:T(8,128)S(1)} all-to-all(f32[16,32,128]{2,1,0:T(8,128)S(1)} %broadcast_in_dim.43), channel_id=1, replica_groups={{68,69,70,71,64,65,66,67,4,5,6,7,0,1,2,3},{76,77,78,79,72,73,74,75,12,1..., dimensions={0} | all-to-all | bytes 524288 | tf_op jit(solution)/shard_map/all_to_all | solution.py:54
  64.1 0.1 abs_reduce_fusion
  64.2 13.3 %all_to_all.37 = f32[32,4,128]{2,1,0:T(4,128)S(1)} all-to-all(f32[32,4,128]{2,1,0:T(4,128)S(1)} %broadcast_in_dim.48), channel_id=1, replica_groups={{160,168,176,184,128,136,144,152,288,296,304,312,256,264,272,280,416,42..., dimensions={0} | all-to-all | bytes 131072 | tf_op jit(solution)/shard_map/all_to_all | solution.py:54
  77.6 0.0 copy-done.9
  77.7 0.0 copy-start.2
  77.7 0.0 copy-done.5
  77.8 0.0 copy-start.4
  77.8 0.8 fusion
  78.6 0.0 copy-done.2
  78.6 19.2 %all_to_all.38 = f16[32,64,128]{2,1,0:T(8,128)(2,1)S(1)} all-to-all(f16[32,64,128]{2,1,0:T(8,128)(2,1)S(1)} %bitcast.34), channel_id=1, replica_groups={{160,168,176,184,128,136,144,152,288,296,304,312,256,264,272,280,416,42..., dimensions={0} | all-to-all | bytes 1048576 | tf_op jit(solution)/shard_map/all_to_all | solution.py:54
  97.8 0.1 convert_reduce_fusion
  98.0 12.5 %all_to_all.39 = f32[16,1,128]{2,1,0:T(1,128)S(1)} all-to-all(f32[16,1,128]{2,1,0:T(1,128)S(1)} %broadcast_in_dim.49), channel_id=1, replica_groups={{68,69,70,71,64,65,66,67,4,5,6,7,0,1,2,3},{76,77,78,79,72,73,74,75,12,1..., dimensions={0} | all-to-all | bytes 16384 | tf_op jit(solution)/shard_map/all_to_all | solution.py:54
  110.5 11.6 %all_to_all.40 = f32[32,1,128]{2,1,0:T(1,128)S(1)} all-to-all(f32[32,1,128]{2,1,0:T(1,128)S(1)} %broadcast_in_dim.50), channel_id=1, replica_groups={{160,168,176,184,128,136,144,152,288,296,304,312,256,264,272,280,416,42..., dimensions={0} | all-to-all | bytes 32768 | tf_op jit(solution)/shard_map/all_to_all | solution.py:54
  122.2 0.0 copy-start.10
  122.2 0.0 copy-done.4
  122.2 0.6 multiply_add_fusion
  122.8 0.0 copy-done.10
  (41 shorter events, 0.7 us)
Async XLA Ops:
  0.6 19.6 %copy-start = (bf16[128,4096]{1,0:T(8,128)(2,1)S(1)}, bf16[128,4096]{1,0:T(8,128)(2,1)}, u32[]{:S(2)}) copy-start(bf16[128,4096]{1,0:T(8,128)(2,1)} %param.10) | copy-start | bytes 3145732
  2.3 24.3 %all-to-all-start = ((bf16[32,64,128]{2,1,0:T(8,128)(2,1)}), bf16[32,64,128]{2,1,0:T(8,128)(2,1)S(1)}, u32[]{:S(2)}, u32[]{:S(2)}) async-start(bf16[32,64,128]{2,1,0:T(8,128)(2,1)} %shard_map.120), calls=%async_computation | async-start | bytes 1048576 | tf_op jit(solution)/shard_map/all_to_all | solution.py:54
  13.4 8.8 %collective-permute-start = (bf16[256,128]{1,0:T(8,128)(2,1)}, bf16[256,128]{1,0:T(8,128)(2,1)}, u32[]{:S(2)}, u32[]{:S(2)}) collective-permute-start(bf16[256,128]{1,0:T(8,128)(2,1)} %param.9), channel_id=1, source_target_pairs={{0,64},{64,0},{1,65},{65,1},{2,66},{66,2},{3,67},{67,3},{4,68},{68... | collective-permute-start | bytes 196616 | tf_op jit(solution)/shard_map/ppermute | solution.py:93
  18.3 8.1 %collective-permute-start.1 = (f32[258,128]{1,0:T(8,128)S(1)}, f32[258,128]{1,0:T(8,128)S(1)}, u32[]{:S(2)}, u32[]{:S(2)}) collective-permute-start(f32[258,128]{1,0:T(8,128)S(1)} %pad_maximum_fusion.2), channel_id=1, source_target_pairs={{0,64},{64,0},{1,65},{65,1},{2,66},{66,2},{3,67},{67,3},{4,68},{68... | collective-permute-start | bytes 396296 | tf_op jit(solution)/shard_map/ppermute | solution.py:95
  20.9 0.7 copy-start.6
  21.2 0.9 copy-start.1
  21.2 0.9 copy-start.8
  22.2 4.3 %copy-start.7 = (f32[256]{0:T(256)S(1)}, f32[256]{0:T(256)}, u32[]{:S(2)}) copy-start(f32[256]{0:T(256)} %param.12) | copy-start | bytes 3076
  22.2 4.3 %copy-start.3 = (f32[256,128]{1,0:T(8,128)S(1)}, f32[256,128]{1,0:T(8,128)}, u32[]{:S(2)}) copy-start(f32[256,128]{1,0:T(8,128)} %param.13) | copy-start | bytes 393220
  27.5 50.1 %copy-start.9 = (f32[128]{0:T(128)S(1)}, f32[128]{0:T(128)}, u32[]{:S(2)}) copy-start(f32[128]{0:T(128)} %param.17) | copy-start | bytes 1540
  27.6 50.2 %copy-start.5 = (f32[64,128]{1,0:T(8,128)S(1)}, f32[64,128]{1,0:T(8,128)}, u32[]{:S(2)}) copy-start(f32[64,128]{1,0:T(8,128)} %param.14) | copy-start | bytes 98308
  77.7 0.9 copy-start.2
  77.8 44.4 %copy-start.4 = (f32[64,128]{1,0:T(8,128)}, f32[64,128]{1,0:T(8,128)S(1)}, u32[]{:S(2)}) copy-start(f32[64,128]{1,0:T(8,128)S(1)} %multiply_add_fusion.1) | copy-start | bytes 98308
  122.2 0.7 copy-start.10
